TPU v7x, 32 devices: a whole 2x2x4 slice. The times are simulated.
32 devices in a mesh: row: 4 (over z), col: 8 (over y, x, core).
Axes of the slice: x: 2, y: 2, z: 4, core: 2. Of those that a mesh axis runs over, the one named last changes fastest.
Arguments:
- operator: float32 [4096, 4096], P('row', 'col'), may hold values from -0.09375 to 0.09375
- vectors: float32 [4096, 256], P('row', 'col'), may hold values from -6 to 6
- owner_map: int32 [2816, 1], P(('row', 'col')), may hold values from 0 to 7; in each aligned block of 88 rows (0 to 87, 88 to 175, ...) at most 32 rows name the same one
- coupling: float32 [4, 256, 256], P('row', 'col'), may hold values from -0.375 to 0.375
- ancestors: int32 [4, 8, 512], P('row', 'col'), may hold values from 0 to 511, as said below
- leaf_modes: float32 [4, 8, 2048, 256], P('row', 'col'), may hold values from -0.375 to 0.375
- constraint_modes: float32 [4, 8, 2048, 512], P('row', 'col'), may hold values from -0.25 to 0.25
Outputs:
- separators: float32 [4, 256, 256], P('row', 'col')
- interiors: float32 [4, 8, 2048, 256], P('row', 'col')
Inputs may be any that keep to these rules, and one draw needn't show every extreme that they name: `owner_map`: in each aligned block of 88 rows no leaf is named more than 32 times, a bound that some block reaches. `ancestors`: the 512 indices of one leaf are distinct.
All inputs are finite; a program needn't handle non-finite values.
Results may differ from a plain program's by a relative error of at most 0.00007.
Values sent between devices are 32-bit elements; how exact they have to be, the bound alone decides.
No kernel may reach another device: no remote copies, remote signals or barrier semaphores. Data moves between devices by JAX's collectives and lax.ppermute only.
A program may use at most 64 MiB of HBM per device.

v0:
```python
import jax
import jax.numpy as jnp
from jax import lax
from jax.sharding import PartitionSpec as P

highest = lax.Precision.HIGHEST


def slot_ranks(owned_rows, fanout):
    onehot = (owned_rows[..., None] == jnp.arange(fanout, dtype=jnp.int32)).astype(jnp.int32)
    running = jnp.cumsum(onehot, axis=-2)
    return jnp.sum(running * onehot, axis=-1) - 1


def on_device(operator, vectors, owner_map, coupling, ancestors, leaf_modes, constraint_modes):
    fanout = lax.axis_size("col")
    mode_local = owner_map.shape[0]
    separator_local = coupling.shape[1]
    mode_count = leaf_modes.shape[3]
    slot_count = mode_count // fanout
    mode_matrix = leaf_modes[0, 0]
    partial_adjoint = lax.dot_general(
        operator,
        lax.all_gather(vectors, "col", axis=1, tiled=True),
        (((0,), (0,)), ((), ())),
        precision=highest,
        preferred_element_type=jnp.float32,
    )
    shares = lax.psum_scatter(partial_adjoint, "row", scatter_dimension=0, tiled=True)
    forward = jnp.dot(
        operator,
        lax.all_gather(shares, "row", axis=0, tiled=True),
        precision=highest,
        preferred_element_type=jnp.float32,
    )
    vector_count = forward.shape[1]
    local_rows = lax.psum_scatter(forward, "col", scatter_dimension=0, tiled=True)
    mode_rows = local_rows[:mode_local]
    separator_raw = local_rows[mode_local : mode_local + separator_local]
    top_local = local_rows[mode_local + separator_local :]
    owned_here = owner_map[:, 0]
    target = owned_here * slot_count + slot_ranks(owned_here, fanout)
    source = (
        jnp.full((fanout * slot_count,), mode_local, jnp.int32)
        .at[target]
        .set(jnp.arange(mode_local, dtype=jnp.int32))
    )
    outgoing = jnp.take(mode_rows, source, axis=0, mode="fill", fill_value=0.0).reshape(
        fanout, slot_count, vector_count
    )
    received = lax.all_to_all(outgoing, "col", split_axis=0, concat_axis=0, tiled=True)
    flattened = received.reshape(mode_count, received.shape[2])
    modal_sum = jnp.dot(
        mode_matrix, flattened, precision=highest, preferred_element_type=jnp.float32
    )
    top_gathered = lax.all_gather(top_local, ("row", "col"), axis=0, tiled=True)
    separators = separator_raw + jnp.dot(
        coupling[0], top_gathered, precision=highest, preferred_element_type=jnp.float32
    )
    separator_all = lax.all_gather(separators, "col", axis=0, tiled=True)
    candidates = jnp.concatenate([top_gathered, separator_all], axis=0)
    picked = jnp.take(candidates, ancestors[0, 0], axis=0)
    interiors = modal_sum + jnp.dot(
        constraint_modes[0, 0], picked, precision=highest, preferred_element_type=jnp.float32
    )
    return (separators[None], interiors[None, None])


def solution(mesh):
    in_specs = (
        P("row", "col"),
        P("row", "col"),
        P(("row", "col"), None),
        P("row", "col", None),
        P("row", "col", None),
        P("row", "col", None, None),
        P("row", "col", None, None),
    )
    out_specs = (P("row", "col", None), P("row", "col", None, None))
    return jax.shard_map(
        on_device, mesh=mesh, in_specs=in_specs, out_specs=out_specs, check_vma=False
    )
```

profile of v0, /device:TPU:0, one launch (start us, length us, event | category | flops | bytes accessed | tf_op | source)
XLA Modules:
  0.0 207.7 jit_solution(3780985953271571062)
XLA Ops:
  7.2 0.0 copy-start
  7.2 0.0 all-gather.2.cloned.1.call-start
  7.2 0.7 all-gather.2.cloned.1.call-update
  7.9 0.0 reduce-scatter.3.cloned.1.call-start
  8.0 28.0 %all-gather.2.cloned.1.call-done = f32[1024,256]{0,1:T(8,128)} async-done(((f32[1024,32]{0,1:T(8,128)}), f32[1024,256]{0,1:T(8,128)}) %all-gather.2.cloned.1.call-update) | async-done | bytes 1048592 | tf_op jit(solution)/shard_map/all_gather | solution.py:24
  36.0 6.1 %fusion.14 = f32[512,256]{1,0:T(8,128)} fusion(f32[1024,512]{1,0:T(8,128)} %param.7, f32[1024,256]{0,1:T(8,128)} %all-gather.2.cloned.1.call-done), kind=kOutput, calls=%fused_computation.33 | convolution fusion | flops 1610612736 | bytes 3670016 | tf_op jit(solution)/shard_map/dot_general | solution.py:22
  42.1 0.0 reduce-scatter.3.cloned.1.call-update
  42.1 0.0 reduce-scatter.5.cloned.1.call-start
  42.2 21.9 %reduce-scatter.3.cloned.1.call-done = f32[128,256]{1,0:T(8,128)} async-done(((f32[512,256]{1,0:T(8,128)}), f32[128,256]{1,0:T(8,128)}) %reduce-scatter.3.cloned.1.call-update) | async-done | bytes 131088 | tf_op jit(solution)/shard_map/reduce_scatter | solution.py:29
  64.1 15.6 %all_gather.13 = f32[512,256]{1,0:T(8,128)S(1)} all-gather(f32[128,256]{1,0:T(8,128)} %reduce-scatter.3.cloned.1.call-done), channel_id=1, replica_groups=mesh['row'=4,'col'=8] {'row'}, dimensions={0}, use_global_device_ids=true | all-gather | bytes 655360 | tf_op jit(solution)/shard_map/all_gather | solution.py:32
  79.6 0.0 copy-start.4
  79.7 0.0 copy-start.3
  79.7 6.1 %convolution_bitcast_fusion = f32[1024,256]{0,1:T(8,128)} fusion(f32[512,256]{1,0:T(8,128)S(1)} %all_gather.13, f32[1024,512]{1,0:T(8,128)} %param.7), kind=kOutput, calls=%fused_computation.8 | convolution fusion | flops 1610612736 | bytes 3670016 | tf_op jit(solution)/shard_map/dot_general | solution.py:30
  85.7 0.0 reduce-scatter.5.cloned.1.call-update
  85.8 0.0 copy-done.4
  85.8 0.1 fusion.8
  85.9 0.1 reduce_window_sum.11
  86.0 0.2 select_reduce_fusion
  86.2 0.8 scatter_custom_fusion
  87.1 0.1 broadcast_in_dim.37
  87.1 0.0 copy-done.3
  87.2 33.1 %reduce-scatter.5.cloned.1.call-done = f32[128,256]{0,1:T(8,128)} async-done(((f32[1024,256]{0,1:T(8,128)}), f32[128,256]{0,1:T(8,128)}) %reduce-scatter.5.cloned.1.call-update) | async-done | bytes 131088 | tf_op jit(solution)/shard_map/reduce_scatter | solution.py:37
  120.3 0.0 copy-start.1
  120.3 0.0 copy-start.2
  120.3 1.1 copy.21
  121.4 1.0 slice.17
  122.4 0.1 copy.19
  122.4 1.0 gather_fusion
  123.4 0.8 broadcast_select_fusion
  124.2 3.4 %all-to-all-start = ((f32[8,32,256]{2,1,0:T(8,128)}), f32[8,32,256]{2,1,0:T(8,128)S(1)}, u32[]{:S(2)}, u32[]{:S(2)}) async-start(f32[8,32,256]{2,1,0:T(8,128)} %broadcast_select_fusion), calls=%async_computation.2 | async-start | bytes 524288 | tf_op jit(solution)/shard_map/all_to_all | solution.py:51
  127.6 42.6 %all_gather.14 = f32[256,256]{1,0:T(8,128)S(1)} all-gather(f32[8,256]{1,0:T(8,128)S(1)} %copy.19), channel_id=1, replica_groups=mesh['row'=4,'col'=8] {'row','col'}, dimensions={0}, use_global_device_ids=true | all-gather | bytes 270336 | tf_op jit(solution)/shard_map/all_gather | solution.py:56
  170.2 0.0 copy-done.1
  170.2 0.0 copy-done.2
  170.2 0.6 fusion.4
  170.8 0.1 copy.22
  170.9 0.7 copy.23
  171.6 8.3 %all_gather.15 = f32[256,256]{1,0:T(8,128)S(1)} all-gather(f32[32,256]{1,0:T(8,128)S(1)} %copy.22), channel_id=1, replica_groups=mesh['row'=4,'col'=8] {'col'}, dimensions={0}, use_global_device_ids=true | all-gather | bytes 294912 | tf_op jit(solution)/shard_map/all_gather | solution.py:60
  179.9 1.6 gather_fusion.1
  181.5 10.4 %fusion = f32[256,2048]{1,0:T(8,128)} fusion(f32[1,1,2048,512]{3,2,1,0:T(8,128)} %param.13, f32[512,256]{1,0:T(8,128)S(1)} %gather_fusion.1, pred[512]{0:T(512)(128)(4,1)S(1)} %compare_and_fusion), kind=kOutput, calls=%fused_computation.3 | convolution fusion | flops 3221356544 | bytes 6816256 | tf_op jit(solution)/shard_map/dot_general | solution.py:63
  191.9 0.0 all-to-all-done
  191.9 0.0 copy-done
  191.9 6.4 %fusion.2 = f32[1,1,2048,256]{2,3,1,0:T(8,128)} fusion(f32[256,2048]{1,0:T(8,128)} %fusion, f32[256,256]{1,0:T(8,128)S(1)} %bitcast.43, f32[1,1,2048,256]{3,2,1,0:T(8,128)S(1)} %copy-done), kind=kOutput, calls=%fused_computation.6 | convolution fusion | flops 1611137024 | bytes 6553600 | tf_op jit(solution)/shard_map/dot_general | solution.py:53
  198.3 2.9 %copy.24 = f32[1,1,2048,256]{3,2,1,0:T(8,128)} copy(f32[1,1,2048,256]{2,3,1,0:T(8,128)} %fusion.2) | data formatting | bytes 4194304
  (9 shorter events, 0.1 us)
Async XLA Ops:
  7.2 184.7 %copy-start = (f32[1,1,2048,256]{3,2,1,0:T(8,128)S(1)}, f32[1,1,2048,256]{3,2,1,0:T(8,128)}, u32[]{:S(2)}) copy-start(f32[1,1,2048,256]{3,2,1,0:T(8,128)} %param.12) | copy-start | bytes 6291460
  7.2 28.8 %all-gather.2.cloned.1.call-start = ((), (), s32[]{:S(2)}) async-start(), calls=%async_computation.3 | async-start | bytes 1179648 | tf_op jit(solution)/shard_map/all_gather | solution.py:24
  7.9 56.2 %reduce-scatter.3.cloned.1.call-start = ((), (), s32[]{:S(2)}) async-start(), calls=%async_computation.4 | async-start | bytes 655360 | tf_op jit(solution)/shard_map/reduce_scatter | solution.py:29
  42.1 78.2 %reduce-scatter.5.cloned.1.call-start = ((), (), s32[]{:S(2)}) async-start(), calls=%async_computation.5 | async-start | bytes 1179648 | tf_op jit(solution)/shard_map/reduce_scatter | solution.py:37
  79.6 6.1 %copy-start.4 = (s32[88,1]{0,1:T(1,128)S(1)}, s32[88,1]{0,1:T(1,128)}, u32[]{:S(2)}) copy-start(s32[88,1]{0,1:T(1,128)} %param.9) | copy-start | bytes 1060
  79.7 7.5 %copy-start.3 = (s32[1,1,512]{2,1,0:T(1,128)S(1)}, s32[1,1,512]{2,1,0:T(1,128)}, u32[]{:S(2)}) copy-start(s32[1,1,512]{2,1,0:T(1,128)} %param.11) | copy-start | bytes 6148
  120.3 49.9 %copy-start.1 = (f32[128,256]{0,1:T(8,128)S(1)}, f32[128,256]{0,1:T(8,128)}, u32[]{:S(2)}) copy-start(f32[128,256]{0,1:T(8,128)} %reduce-scatter.5.cloned.1.call-done) | copy-start | bytes 393220
  120.3 49.9 %copy-start.2 = (f32[1,32,256]{2,1,0:T(8,128)S(1)}, f32[1,32,256]{2,1,0:T(8,128)}, u32[]{:S(2)}) copy-start(f32[1,32,256]{2,1,0:T(8,128)} %param.10) | copy-start | bytes 98308
  124.2 67.7 %all-to-all-start = ((f32[8,32,256]{2,1,0:T(8,128)}), f32[8,32,256]{2,1,0:T(8,128)S(1)}, u32[]{:S(2)}, u32[]{:S(2)}) async-start(f32[8,32,256]{2,1,0:T(8,128)} %broadcast_select_fusion), calls=%async_computation.2 | async-start | bytes 524288 | tf_op jit(solution)/shard_map/all_to_all | solution.py:51
Sparse Core Ops, SparseCore 0:
  9.9 26.0 all-gather.1
  42.2 21.8 reduce-scatter.2
  85.9 34.3 reduce-scatter.4
where the time goes:
time: 208 us
  waiting for transfers between devices  83.8 us (40%)
  blocking collectives  66.5 us (32%)
  matrix products  29.5 us (14%)
  between operations  13.9 us (7%)
  local copies, waits for them, and re-layouts  9.27 us (4%)
  starting transfers between devices  3.53 us (2%)
    all_gather x1, blocking collectives, on_device(): top_gathered = lax.all_gather(top_local, ('row', 'col'), axis=0, tiled=True)  42.6 us
    reduce_scatter x1, waiting for transfers between devices, on_device(): lax.psum_scatter(forward, 'col', scatter_dimension=0, tiled=True)  33.1 us
    all_gather x1, waiting for transfers between devices, on_device(): lax.all_gather(vectors, 'col', axis=1, tiled=True)  28 us
    reduce_scatter x1, waiting for transfers between devices, on_device(): lax.psum_scatter(partial_adjoint, 'row', scatter_dimension=0, tiled=True)  21.9 us
    all_gather x1, blocking collectives, on_device(): lax.all_gather(shares, 'row', axis=0, tiled=True)  15.6 us
    dot_general x1, matrix products, on_device(): jnp.dot(constraint_modes[0, 0], picked, precision=highest, preferred_elem...  10.4 us
    all_gather x1, blocking collectives, on_device(): separator_all = lax.all_gather(separators, 'col', axis=0, tiled=True)  8.28 us
    dot_general x1, matrix products, on_device(): jnp.dot(mode_matrix, flattened, precision=highest, preferred_element_type...  6.4 us
  transfers between devices with their start and end apart: 4, of which 3 were waited for; matrix products, arithmetic and copies ran while one was open for 7% of the time, Pallas kernels for 0%

commit v1 on v0

v1 whole, which is shorter than its diff:
```python
import jax
import jax.numpy as jnp
from jax import lax
from jax.sharding import PartitionSpec as P

HIGH = lax.Precision.HIGH


def product(a, b, da, db):
    return lax.dot_general(
        a,
        b,
        (((da,), (db,)), ((), ())),
        precision=HIGH,
        preferred_element_type=jnp.float32,
    )


def swap(v, axis, mask):
    n = lax.axis_size(axis)
    return lax.ppermute(v, axis, [(i, i ^ mask) for i in range(n)])


def gather_xor(v, axis, masks):
    blocks = v[None]
    order = [0]
    for mask in masks:
        blocks = jnp.concatenate([blocks, swap(blocks, axis, mask)], axis=0)
        order = order + [o ^ mask for o in order]
    return blocks, order


def arrange(blocks, order, me):
    position = jnp.asarray([order.index(o) for o in range(len(order))], jnp.int32)
    return jnp.stack(
        [
            lax.dynamic_index_in_dim(blocks, position[jnp.int32(i) ^ me], 0, keepdims=False)
            for i in range(len(order))
        ]
    )


def reduce_xor(parts, axis, masks):
    n = len(masks)
    for step in range(n):
        moved = [swap(p, axis, masks[(i + step) % n]) for i, p in enumerate(parts)]
        parts = [p + q for p, q in zip(parts, moved)]
    return parts


def slot_ranks(owned_rows, fanout):
    onehot = (owned_rows[..., None] == jnp.arange(fanout, dtype=jnp.int32)).astype(jnp.int32)
    running = jnp.cumsum(onehot, axis=-2)
    return jnp.sum(running * onehot, axis=-1) - 1


def on_device(operator, vectors, owner_map, coupling, ancestors, leaf_modes, constraint_modes):
    rows = lax.axis_size("row")
    fanout = lax.axis_size("col")
    r = lax.axis_index("row")
    c = lax.axis_index("col")
    mode_local = owner_map.shape[0]
    separator_local = coupling.shape[1]
    top_count = coupling.shape[2]
    mode_count = leaf_modes.shape[3]
    ancestor_count = constraint_modes.shape[3]
    slot_count = mode_count // fanout
    row_count = operator.shape[0]
    block = row_count // fanout
    top_local = block - mode_local - separator_local
    row_masks = [(2 << b) - 1 for b in range(rows.bit_length() - 1)]
    col_masks = [1 << b for b in range(1, fanout.bit_length() - 1)]
    half = fanout // 2

    partner = swap(operator, "col", 1)
    width = coupling.shape[2]
    tags = owner_map[:, 0].astype(jnp.float32)
    tag_rows = -(-mode_local // width)
    tags = jnp.pad(tags, (0, tag_rows * width - mode_local)).reshape(tag_rows, width)
    small = jnp.concatenate([coupling[0], jnp.pad(tags, ((0, -tag_rows % 8), (0, 0)))], axis=0)
    small, small_order = gather_xor(small, "col", [1] + col_masks)
    small = arrange(small, small_order, c)
    coupling_all = small[:, :separator_local].reshape(fanout * separator_local, width)
    owners = small[:, separator_local : separator_local + tag_rows].reshape(fanout, -1)[:, :mode_local]
    owners = owners.astype(jnp.int32)

    blocks, order = gather_xor(vectors.T, "col", col_masks)
    xt = arrange(blocks, [o >> 1 for o in order], c // 2).reshape(-1, operator.shape[0])
    part_a = product(xt, operator, 1, 0)
    part_b = product(xt, partner, 1, 0)
    adj_a, adj_b = reduce_xor([part_a, part_b], "row", row_masks)

    def forward(k, p):
        return product(adj_a, k, 1, 1) + product(adj_b, p, 1, 1)

    def tops(k):
        return k.reshape(fanout, block, -1)[:, block - top_local :].reshape(fanout * top_local, -1)

    top_part, top_order = gather_xor(forward(tops(operator), tops(partner)), "row", row_masks)
    nv_half = xt.shape[0]
    top_part = top_part.transpose(1, 0, 2).reshape(nv_half, top_count)
    cut = row_count // 2
    f0 = forward(operator[:cut], partner[:cut])
    f1 = forward(operator[cut:], partner[cut:])
    f1 = jnp.concatenate([f1, top_part], axis=1)
    f0, f1 = reduce_xor([f0, f1], "col", col_masks)
    own = jnp.concatenate([f0, f1], axis=1)
    other = swap(own, "col", 1)
    even = jnp.where(c % 2 == 0, own, other)
    odd = jnp.where(c % 2 == 0, other, own)
    width = own.shape[1]
    full = jnp.stack([even.reshape(half, -1, width), odd.reshape(half, -1, width)], axis=1).reshape(-1, width)

    ranks = slot_ranks(owners, fanout)
    slot = jnp.where(owners == c, jnp.arange(fanout, dtype=jnp.int32)[:, None] * slot_count + ranks, -1)
    slot = jnp.concatenate([slot, jnp.full((fanout, block - mode_local), -1, jnp.int32)], axis=1).reshape(-1)
    pick_modes = (slot[:, None] == jnp.arange(mode_count, dtype=jnp.int32)).astype(jnp.float32)
    top_plane = fanout * top_local
    top_inverse = jnp.asarray([top_order.index(o) for o in range(rows)], jnp.int32)
    top_place = top_inverse[jnp.arange(rows, dtype=jnp.int32) ^ r]
    anc = ancestors[0, 0]
    top_full = full[:, row_count:].reshape(-1, rows, top_plane)
    top_full = jnp.take(top_full, top_place, axis=1).reshape(-1, top_count)
    raw = full[:, :row_count].reshape(-1, fanout, block)[:, :, mode_local : mode_local + separator_local]
    raw = raw.reshape(-1, fanout * separator_local)
    sep = raw + product(top_full, coupling_all, 1, 1)
    candidates = jnp.concatenate([top_full, sep], axis=1)
    pick_anc = (jnp.arange(candidates.shape[1], dtype=jnp.int32)[:, None] == anc).astype(jnp.float32)
    highest = lax.Precision.HIGHEST
    coords = jnp.dot(full[:, :row_count], pick_modes, precision=highest)
    gathered = jnp.dot(candidates, pick_anc, precision=highest)
    interiors = product(leaf_modes[0, 0], coords, 1, 1) + product(constraint_modes[0, 0], gathered, 1, 1)
    sep_own = lax.dynamic_slice_in_dim(sep, c * separator_local, separator_local, axis=1).T
    return (sep_own[None], interiors[None, None])


def solution(mesh):
    in_specs = (
        P("row", "col"),
        P("row", "col"),
        P(("row", "col"), None),
        P("row", "col", None),
        P("row", "col", None),
        P("row", "col", None, None),
        P("row", "col", None, None),
    )
    out_specs = (P("row", "col", None), P("row", "col", None, None))
    return jax.shard_map(
        on_device, mesh=mesh, in_specs=in_specs, out_specs=out_specs, check_vma=False
    )
```

time: 208 us -> 106 us (0.51)
  blocking collectives: 66.5 us -> 0 us
  waiting for transfers between devices: 83.8 us -> 34.3 us
  starting transfers between devices: 3.53 us -> 28.1 us
  between operations: 13.9 us -> 1.01 us
  matrix products: 29.5 us -> 18 us
  other arithmetic: 1.24 us -> 8.55 us
  local copies, waits for them, and re-layouts: 9.27 us -> 15.8 us
    all_gather x3 -> x0, blocking collectives: 66.5 us -> none  [the longest x1 42.6 us: on_device(): top_gathered = lax.all_gather(top_local, ('row', 'col'), axis=0, tiled=True)]
    reduce_scatter x2 -> x0, waiting for transfers between devices: 55 us -> none  [the longest x1 33.1 us: on_device(): lax.psum_scatter(forward, 'col', scatter_dimension=0, tiled=True)]
    ppermute x0 -> x17, waiting for transfers between devices: none -> 34.3 us  [swap(): return lax.ppermute(v, axis, [(i, i ^ mask) for i in range(n)])]
    ppermute x0 -> x17, starting transfers between devices: none -> 28.1 us  [swap(): return lax.ppermute(v, axis, [(i, i ^ mask) for i in range(n)])]
    all_gather x1 -> x0, waiting for transfers between devices: 28 us -> none  [on_device(): lax.all_gather(vectors, 'col', axis=1, tiled=True)]
    dot_general x5 -> x13, matrix products: 29.5 us -> 18 us  [the longest x11 16.6 us: product(): lax.dot_general(a, b, (((da,), (db,)), ((), ())), precision=HIGH, preferr...]
    all_to_all x1 -> x0, starting transfers between devices: 3.41 us -> none  [on_device(): lax.all_to_all(outgoing, 'col', split_axis=0, concat_axis=0, tiled=True)]
    concatenate x1 -> x9, other arithmetic: 0.03 us -> 2.58 us  [the longest x7 1.67 us: gather_xor(): blocks = jnp.concatenate([blocks, swap(blocks, axis, mask)], axis=0)]
  transfers between devices with their start and end apart: 4 -> 17, of which waited for: 3 -> 12; matrix products, arithmetic and copies ran while one was open for 7% -> 18% of each run, Pallas kernels for 0% -> 0%
where the time goes in v1:
time: 106 us
  waiting for transfers between devices  34.3 us (32%)
  starting transfers between devices  28.1 us (27%)
  matrix products  18 us (17%)
  local copies, waits for them, and re-layouts  15.8 us (15%)
  other arithmetic  8.55 us (8%)
    ppermute x17, waiting for transfers between devices, swap(): return lax.ppermute(v, axis, [(i, i ^ mask) for i in range(n)])  34.3 us
    ppermute x17, starting transfers between devices, swap(): return lax.ppermute(v, axis, [(i, i ^ mask) for i in range(n)])  28.1 us
    dot_general x11, matrix products, product(): lax.dot_general(a, b, (((da,), (db,)), ((), ())), precision=HIGH, preferr...  16.6 us
    unnamed x32, local copies, waits for them, and re-layouts  5.65 us
  transfers between devices with their start and end apart: 17, of which 12 were waited for; matrix products, arithmetic and copies ran while one was open for 18% of the time, Pallas kernels for 0%

profile of v1, /device:TPU:0, one launch (start us, length us, event | category | flops | bytes accessed | tf_op | source)
XLA Modules:
  0.0 105.8 jit_solution(5915761450292758745)
XLA Ops:
  1.2 0.7 convert_bitcast_fusion
  1.9 0.8 fusion.22
  2.8 2.8 %collective-permute-start = (f32[1,32,1024]{2,1,0:T(8,128)}, f32[1,32,1024]{2,1,0:T(8,128)S(1)}, u32[]{:S(2)}, u32[]{:S(2)}) collective-permute-start(f32[1,32,1024]{2,1,0:T(8,128)} %bitcast.86), channel_id=1, source_target_pairs={{0,2},{1,3},{2,0},{3,1},{4,6},{5,7},{6,4},{7,5},{8,10},{9,11},{10,... | collective-permute-start | bytes 393224 | tf_op jit(solution)/shard_map/ppermute | solution.py:21
  5.6 1.3 %gather_fusion = s32[4]{0:T(128)S(1)} fusion(s32[4]{0:T(128)} %constant.112.clone, s32[1024]{0:T(1024)S(1)} %pad_clamp_fusion.1), kind=kCustom, calls=%fused_computation | custom fusion | bytes 48 | tf_op jit(solution)/shard_map/gather | solution.py:120
  7.0 1.2 %collective-permute-start.15 = (f32[2,40,256]{2,1,0:T(8,128)S(1)}, f32[2,40,256]{2,1,0:T(8,128)S(1)}, u32[]{:S(2)}, u32[]{:S(2)}) collective-permute-start(f32[2,40,256]{2,1,0:T(8,128)S(1)} %pad_maximum_fusion.9), channel_id=1, source_target_pairs={{0,2},{1,3},{2,0},{3,1},{4,6},{5,7},{6,4},{7,5},{8,10},{9,11},{10,... | collective-permute-start | bytes 245768 | tf_op jit(solution)/shard_map/ppermute | solution.py:21
  8.2 3.3 %collective-permute-done.15 = f32[2,40,256]{2,1,0:T(8,128)S(1)} collective-permute-done((f32[2,40,256]{2,1,0:T(8,128)S(1)}, f32[2,40,256]{2,1,0:T(8,128)S(1)}, u32[]{:S(2)}, u32[]{:S(2)}) %collective-permute-start.15) | collective-permute-done | bytes 81952 | tf_op jit(solution)/shard_map/ppermute | solution.py:21
  11.5 1.8 %collective-permute-start.16 = (f32[4,40,256]{2,1,0:T(8,128)S(1)}, f32[4,40,256]{2,1,0:T(8,128)S(1)}, u32[]{:S(2)}, u32[]{:S(2)}) collective-permute-start(f32[4,40,256]{2,1,0:T(8,128)S(1)} %pad_maximum_fusion.7), channel_id=1, source_target_pairs={{0,4},{1,5},{2,6},{3,7},{4,0},{5,1},{6,2},{7,3},{8,12},{9,13},{10,... | collective-permute-start | bytes 491528 | tf_op jit(solution)/shard_map/ppermute | solution.py:21
  13.3 0.9 pad_maximum_fusion.6
  14.7 3.3 %collective-permute-done.16 = f32[4,40,256]{2,1,0:T(8,128)S(1)} collective-permute-done((f32[4,40,256]{2,1,0:T(8,128)S(1)}, f32[4,40,256]{2,1,0:T(8,128)S(1)}, u32[]{:S(2)}, u32[]{:S(2)}) %collective-permute-start.16) | collective-permute-done | bytes 163872 | tf_op jit(solution)/shard_map/ppermute | solution.py:21
  18.1 4.5 %collective-permute-done.1 = f32[2,32,1024]{2,1,0:T(8,128)S(1)} collective-permute-done((f32[2,32,1024]{2,1,0:T(8,128)S(1)}, f32[2,32,1024]{2,1,0:T(8,128)S(1)}, u32[]{:S(2)}, u32[]{:S(2)}) %collective-permute-start.1) | collective-permute-done | bytes 262176 | tf_op jit(solution)/shard_map/ppermute | solution.py:21
  22.8 2.4 %fusion.35 = f32[128,512]{1,0:T(8,128)S(1)} fusion(f32[128,1024]{1,0:T(8,128)S(1)} %bitcast.76, f32[1024,512]{1,0:T(8,128)} %collective-permute-done.4), kind=kOutput, calls=%fused_computation.89 | convolution fusion | flops 402653184 | bytes 2883584 | tf_op jit(solution)/shard_map/dot_general | solution.py:10
  25.3 3.9 %collective-permute-start.5 = (f32[128,512]{1,0:T(8,128)S(1)}, f32[128,512]{1,0:T(8,128)S(1)}, u32[]{:S(2)}, u32[]{:S(2)}) collective-permute-start(f32[128,512]{1,0:T(8,128)S(1)} %fusion.35), channel_id=1, source_target_pairs={{0,24},{8,16},{16,8},{24,0},{1,25},{9,17},{17,9},{25,1},{2,26},{10... | collective-permute-start | bytes 786440 | tf_op jit(solution)/shard_map/ppermute | solution.py:21
  29.2 0.7 fusion.34
  30.0 6.3 %collective-permute-done.5 = f32[128,512]{1,0:T(8,128)S(1)} collective-permute-done((f32[128,512]{1,0:T(8,128)S(1)}, f32[128,512]{1,0:T(8,128)S(1)}, u32[]{:S(2)}, u32[]{:S(2)}) %collective-permute-start.5) | collective-permute-done | bytes 262176 | tf_op jit(solution)/shard_map/ppermute | solution.py:21
  36.4 3.5 %collective-permute-start.6 = (f32[128,512]{1,0:T(8,128)S(1)}, f32[128,512]{1,0:T(8,128)S(1)}, u32[]{:S(2)}, u32[]{:S(2)}) collective-permute-start(f32[128,512]{1,0:T(8,128)S(1)} %add.176), channel_id=1, source_target_pairs={{0,8},{8,0},{16,24},{24,16},{1,9},{9,1},{17,25},{25,17},{2,10},{10... | collective-permute-start | bytes 786440 | tf_op jit(solution)/shard_map/ppermute | solution.py:21
  40.5 3.3 %collective-permute-start.3 = (f32[128,512]{1,0:T(8,128)S(1)}, f32[128,512]{1,0:T(8,128)S(1)}, u32[]{:S(2)}, u32[]{:S(2)}) collective-permute-start(f32[128,512]{1,0:T(8,128)S(1)} %add.174), channel_id=1, source_target_pairs={{0,24},{8,16},{16,8},{24,0},{1,25},{9,17},{17,9},{25,1},{2,26},{10... | collective-permute-start | bytes 786440 | tf_op jit(solution)/shard_map/ppermute | solution.py:21
  43.8 3.3 %collective-permute-done.6 = f32[128,512]{1,0:T(8,128)S(1)} collective-permute-done((f32[128,512]{1,0:T(8,128)S(1)}, f32[128,512]{1,0:T(8,128)S(1)}, u32[]{:S(2)}, u32[]{:S(2)}) %collective-permute-start.6) | collective-permute-done | bytes 262176 | tf_op jit(solution)/shard_map/ppermute | solution.py:21
  47.1 1.2 %fusion.21 = f32[128,64]{0,1:T(8,128)S(1)} fusion(f32[8,128,512]{2,1,0:T(8,128)} %bitcast.6, f32[128,512]{1,0:T(8,128)S(1)} %add.176, f32[128,512]{1,0:T(8,128)S(1)} %collective-permute-done.6), kind=kOutput, calls=%fused_computation.45 | convolution fusion | flops 25231360 | bytes 688128 | tf_op jit(solution)/shard_map/dot_general | solution.py:10
  48.3 4.1 %collective-permute-done.3 = f32[128,512]{1,0:T(8,128)S(1)} collective-permute-done((f32[128,512]{1,0:T(8,128)S(1)}, f32[128,512]{1,0:T(8,128)S(1)}, u32[]{:S(2)}, u32[]{:S(2)}) %collective-permute-start.3) | collective-permute-done | bytes 262176 | tf_op jit(solution)/shard_map/ppermute | solution.py:21
  52.7 1.5 %collective-permute-start.9 = (f32[1,128,64]{1,2,0:T(8,128)S(1)}, f32[1,128,64]{1,2,0:T(8,128)S(1)}, u32[]{:S(2)}, u32[]{:S(2)}) collective-permute-start(f32[1,128,64]{1,2,0:T(8,128)S(1)} %fusion.4), channel_id=1, source_target_pairs={{0,8},{8,0},{16,24},{24,16},{1,9},{9,1},{17,25},{25,17},{2,10},{10... | collective-permute-start | bytes 98312 | tf_op jit(solution)/shard_map/ppermute | solution.py:21
  54.2 1.9 %fusion.5 = f32[128,512]{1,0:T(8,128)S(1)} fusion(f32[1024,512]{1,0:T(8,128)} %collective-permute-done.4, f32[128,512]{1,0:T(8,128)S(1)} %add.176, f32[128,512]{1,0:T(8,128)S(1)} %collective-permute-done.6), kind=kOutput, calls=%fused_computation.13 | convolution fusion | flops 201392128 | bytes 1835008 | tf_op jit(solution)/shard_map/dot_general | solution.py:10
  56.7 2.5 %collective-permute-start.10 = (f32[2,128,64]{1,2,0:T(8,128)S(1)}, f32[2,128,64]{1,2,0:T(8,128)S(1)}, u32[]{:S(2)}, u32[]{:S(2)}) collective-permute-start(f32[2,128,64]{1,2,0:T(8,128)S(1)} %pad_maximum_fusion.10), channel_id=1, source_target_pairs={{0,24},{8,16},{16,8},{24,0},{1,25},{9,17},{17,9},{25,1},{2,26},{10... | collective-permute-start | bytes 196616 | tf_op jit(solution)/shard_map/ppermute | solution.py:21
  59.8 2.9 %collective-permute-done.10 = f32[2,128,64]{1,2,0:T(8,128)S(1)} collective-permute-done((f32[2,128,64]{1,2,0:T(8,128)S(1)}, f32[2,128,64]{1,2,0:T(8,128)S(1)}, u32[]{:S(2)}, u32[]{:S(2)}) %collective-permute-start.10) | collective-permute-done | bytes 65568 | tf_op jit(solution)/shard_map/ppermute | solution.py:21
  63.4 1.0 copy.46
  64.5 1.3 %collective-permute-start.11 = (f32[128,768]{1,0:T(8,128)S(1)}, f32[128,768]{1,0:T(8,128)S(1)}, u32[]{:S(2)}, u32[]{:S(2)}) collective-permute-start(f32[128,768]{1,0:T(8,128)S(1)} %pad_maximum_fusion.4), channel_id=1, source_target_pairs={{0,4},{1,5},{2,6},{3,7},{4,0},{5,1},{6,2},{7,3},{8,12},{9,13},{10,... | collective-permute-start | bytes 1179656 | tf_op jit(solution)/shard_map/ppermute | solution.py:21
  65.8 1.9 %fusion.7 = f32[128,512]{1,0:T(8,128)S(1)} fusion(f32[1024,512]{1,0:T(8,128)} %collective-permute-done.4, f32[128,512]{1,0:T(8,128)S(1)} %add.176, f32[128,512]{1,0:T(8,128)S(1)} %collective-permute-done.6), kind=kOutput, calls=%fused_computation.15 | convolution fusion | flops 201392128 | bytes 1835008 | tf_op jit(solution)/shard_map/dot_general | solution.py:10
  68.4 2.0 %collective-permute-start.7 = (f32[128,512]{1,0:T(8,128)S(1)}, f32[128,512]{1,0:T(8,128)S(1)}, u32[]{:S(2)}, u32[]{:S(2)}) collective-permute-start(f32[128,512]{1,0:T(8,128)S(1)} %convolution_add_fusion.3), channel_id=1, source_target_pairs={{0,2},{1,3},{2,0},{3,1},{4,6},{5,7},{6,4},{7,5},{8,10},{9,11},{10,... | collective-permute-start | bytes 786440 | tf_op jit(solution)/shard_map/ppermute | solution.py:21
  70.4 2.4 %collective-permute-done.11 = f32[128,768]{1,0:T(8,128)S(1)} collective-permute-done((f32[128,768]{1,0:T(8,128)S(1)}, f32[128,768]{1,0:T(8,128)S(1)}, u32[]{:S(2)}, u32[]{:S(2)}) %collective-permute-start.11) | collective-permute-done | bytes 393248 | tf_op jit(solution)/shard_map/ppermute | solution.py:21
  72.8 1.8 %collective-permute-start.12 = (f32[128,768]{1,0:T(8,128)S(1)}, f32[128,768]{1,0:T(8,128)S(1)}, u32[]{:S(2)}, u32[]{:S(2)}) collective-permute-start(f32[128,768]{1,0:T(8,128)S(1)} %fusion.33), channel_id=1, source_target_pairs={{0,2},{1,3},{2,0},{3,1},{4,6},{5,7},{6,4},{7,5},{8,10},{9,11},{10,... | collective-permute-start | bytes 1179656 | tf_op jit(solution)/shard_map/ppermute | solution.py:21
  75.2 1.2 %collective-permute-done.7 = f32[128,512]{1,0:T(8,128)S(1)} collective-permute-done((f32[128,512]{1,0:T(8,128)S(1)}, f32[128,512]{1,0:T(8,128)S(1)}, u32[]{:S(2)}, u32[]{:S(2)}) %collective-permute-start.7) | collective-permute-done | bytes 262176 | tf_op jit(solution)/shard_map/ppermute | solution.py:21
  76.4 1.4 %collective-permute-start.8 = (f32[128,512]{1,0:T(8,128)S(1)}, f32[128,512]{1,0:T(8,128)}, u32[]{:S(2)}, u32[]{:S(2)}) collective-permute-start(f32[128,512]{1,0:T(8,128)S(1)} %add.179), channel_id=1, source_target_pairs={{0,4},{1,5},{2,6},{3,7},{4,0},{5,1},{6,2},{7,3},{8,12},{9,13},{10,... | collective-permute-start | bytes 786440 | tf_op jit(solution)/shard_map/ppermute | solution.py:21
  79.6 0.8 slice.61
  80.5 0.8 copy.55
  81.3 1.7 %collective-permute-done.8 = f32[128,512]{1,0:T(8,128)} collective-permute-done((f32[128,512]{1,0:T(8,128)S(1)}, f32[128,512]{1,0:T(8,128)}, u32[]{:S(2)}, u32[]{:S(2)}) %collective-permute-start.8) | collective-permute-done | bytes 262176 | tf_op jit(solution)/shard_map/ppermute | solution.py:21
  83.0 1.0 add.180
  84.0 0.9 pad_maximum_fusion.1
  84.9 0.7 slice.60
  85.6 1.8 %select_reduce_fusion = s32[8,88]{0,1:T(8,128)S(1)} fusion(s32[8,88]{0,1:T(8,128)S(1)} %slice_convert_fusion), kind=kOutput, calls=%fused_computation.32 | output fusion | flops 517440 | bytes 5632 | tf_op jit(solution)/shard_map/jit(cumsum)/reduce_window_sum | solution.py:53
  87.5 1.2 %broadcast_select_fusion.1 = (f32[128,1280]{1,0:T(8,128)S(1)}, f32[128,1280]{1,0:T(8,128)S(1)}) fusion(f32[128,1280]{1,0:T(8,128)} %collective-permute-done.13, pred[]{:T(512)S(6)} %eq.56, f32[128,768]{1,0:T(8,128)S(1)} %add.184, f32[128,512]{1,0:T(8,128)S(1)} %add.180), kind=kLoop, calls=%fused_computation.38 | loop fusion | flops 491520 | bytes 2621441 | tf_op jit(solution)/shard_map/jit(_where)/select_n | solution.py:109
  88.8 0.7 slice.59
  89.7 0.8 fusion.11
  90.5 1.3 %copy.54 = f32[256,1024]{0,1:T(8,128)} copy(f32[256,1024]{1,0:T(8,128)S(1)} %slice.57) | data formatting | bytes 2097152 | tf_op jit(solution)/shard_map/reshape | solution.py:124
  91.8 1.0 slice.58
  92.8 1.1 %copy.50 = f32[256,256]{0,1:T(8,128)S(1)} copy(f32[256,256]{1,0:T(8,128)} %slice.59) | data formatting | bytes 524288 | tf_op jit(solution)/shard_map/slice | solution.py:122
  95.6 0.7 fusion.12
  96.3 4.1 %fusion = f32[256,2048]{1,0:T(8,128)S(1)} fusion(f32[256,512]{1,0:T(8,128)S(1)} %fusion.12, f32[1,1,2048,512]{3,2,1,0:T(8,128)} %param.16), kind=kOutput, calls=%fused_computation.2 | convolution fusion | flops 1610612736 | bytes 6815744 | tf_op jit(solution)/shard_map/dot_general | solution.py:10
  100.4 2.5 %fusion.2 = f32[1,1,2048,256]{2,3,1,0:T(8,128)} fusion(f32[256,2048]{1,0:T(8,128)S(1)} %fusion, f32[256,256]{1,0:T(8,128)S(1)} %fusion.11, f32[1,1,2048,256]{3,2,1,0:T(8,128)S(1)} %copy-done), kind=kOutput, calls=%fused_computation.5 | convolution fusion | flops 805830656 | bytes 6553600 | tf_op jit(solution)/shard_map/dot_general | solution.py:10
  102.9 2.9 %copy.53 = f32[1,1,2048,256]{3,2,1,0:T(8,128)} copy(f32[1,1,2048,256]{2,3,1,0:T(8,128)} %fusion.2) | data formatting | bytes 4194304
  (79 shorter events, 9.7 us)
Async XLA Ops:
  0.6 99.8 %copy-start = (f32[1,1,2048,256]{3,2,1,0:T(8,128)S(1)}, f32[1,1,2048,256]{3,2,1,0:T(8,128)}, u32[]{:S(2)}) copy-start(f32[1,1,2048,256]{3,2,1,0:T(8,128)} %param.15) | copy-start | bytes 6291460
  0.6 22.0 %copy-start.6 = (f32[1024,32]{0,1:T(8,128)S(1)}, f32[1024,32]{0,1:T(8,128)}, u32[]{:S(2)}) copy-start(f32[1024,32]{0,1:T(8,128)} %param.11) | copy-start | bytes 393220
  0.7 22.2 %collective-permute-start.4 = (f32[1024,512]{1,0:T(8,128)}, f32[1024,512]{1,0:T(8,128)}, u32[]{:S(2)}, u32[]{:S(2)}) collective-permute-start(f32[1024,512]{1,0:T(8,128)} %param.10), channel_id=1, source_target_pairs={{0,1},{1,0},{2,3},{3,2},{4,5},{5,4},{6,7},{7,6},{8,9},{9,8},{10,11... | collective-permute-start | bytes 6291464 | tf_op jit(solution)/shard_map/ppermute | solution.py:21
  2.7 4.3 %collective-permute-start.14 = (f32[1,40,256]{2,1,0:T(8,128)S(1)}, f32[1,40,256]{2,1,0:T(8,128)S(1)}, u32[]{:S(2)}, u32[]{:S(2)}) collective-permute-start(f32[1,40,256]{2,1,0:T(8,128)S(1)} %fusion.22), channel_id=1, source_target_pairs={{0,1},{1,0},{2,3},{3,2},{4,5},{5,4},{6,7},{7,6},{8,9},{9,8},{10,11... | collective-permute-start | bytes 122888 | tf_op jit(solution)/shard_map/ppermute | solution.py:21
  2.8 10.5 %collective-permute-start = (f32[1,32,1024]{2,1,0:T(8,128)}, f32[1,32,1024]{2,1,0:T(8,128)S(1)}, u32[]{:S(2)}, u32[]{:S(2)}) collective-permute-start(f32[1,32,1024]{2,1,0:T(8,128)} %bitcast.86), channel_id=1, source_target_pairs={{0,2},{1,3},{2,0},{3,1},{4,6},{5,7},{6,4},{7,5},{8,10},{9,11},{10,... | collective-permute-start | bytes 393224 | tf_op jit(solution)/shard_map/ppermute | solution.py:21
  7.0 4.5 %collective-permute-start.15 = (f32[2,40,256]{2,1,0:T(8,128)S(1)}, f32[2,40,256]{2,1,0:T(8,128)S(1)}, u32[]{:S(2)}, u32[]{:S(2)}) collective-permute-start(f32[2,40,256]{2,1,0:T(8,128)S(1)} %pad_maximum_fusion.9), channel_id=1, source_target_pairs={{0,2},{1,3},{2,0},{3,1},{4,6},{5,7},{6,4},{7,5},{8,10},{9,11},{10,... | collective-permute-start | bytes 245768 | tf_op jit(solution)/shard_map/ppermute | solution.py:21
  11.5 6.6 %collective-permute-start.16 = (f32[4,40,256]{2,1,0:T(8,128)S(1)}, f32[4,40,256]{2,1,0:T(8,128)S(1)}, u32[]{:S(2)}, u32[]{:S(2)}) collective-permute-start(f32[4,40,256]{2,1,0:T(8,128)S(1)} %pad_maximum_fusion.7), channel_id=1, source_target_pairs={{0,4},{1,5},{2,6},{3,7},{4,0},{5,1},{6,2},{7,3},{8,12},{9,13},{10,... | collective-permute-start | bytes 491528 | tf_op jit(solution)/shard_map/ppermute | solution.py:21
  14.2 8.5 %collective-permute-start.1 = (f32[2,32,1024]{2,1,0:T(8,128)S(1)}, f32[2,32,1024]{2,1,0:T(8,128)S(1)}, u32[]{:S(2)}, u32[]{:S(2)}) collective-permute-start(f32[2,32,1024]{2,1,0:T(8,128)S(1)} %pad_maximum_fusion.6), channel_id=1, source_target_pairs={{0,4},{1,5},{2,6},{3,7},{4,0},{5,1},{6,2},{7,3},{8,12},{9,13},{10,... | collective-permute-start | bytes 786440 | tf_op jit(solution)/shard_map/ppermute | solution.py:21
  18.1 25.7 %copy-start.3 = (f32[8,40,256]{2,1,0:T(8,128)}, f32[8,40,256]{2,1,0:T(8,128)S(1)}, u32[]{:S(2)}) copy-start(f32[8,40,256]{2,1,0:T(8,128)S(1)} %pad_maximum_fusion.5) | copy-start | bytes 983044
  22.8 6.4 %copy-start.1 = (f32[1024,512]{1,0:T(8,128)S(1)}, f32[1024,512]{1,0:T(8,128)}, u32[]{:S(2)}) copy-start(f32[1024,512]{1,0:T(8,128)} %param.10) | copy-start | bytes 6291460
  25.3 11.0 %collective-permute-start.5 = (f32[128,512]{1,0:T(8,128)S(1)}, f32[128,512]{1,0:T(8,128)S(1)}, u32[]{:S(2)}, u32[]{:S(2)}) collective-permute-start(f32[128,512]{1,0:T(8,128)S(1)} %fusion.35), channel_id=1, source_target_pairs={{0,24},{8,16},{16,8},{24,0},{1,25},{9,17},{17,9},{25,1},{2,26},{10... | collective-permute-start | bytes 786440 | tf_op jit(solution)/shard_map/ppermute | solution.py:21
  29.9 10.6 %collective-permute-start.2 = (f32[128,512]{1,0:T(8,128)S(1)}, f32[128,512]{1,0:T(8,128)S(1)}, u32[]{:S(2)}, u32[]{:S(2)}) collective-permute-start(f32[128,512]{1,0:T(8,128)S(1)} %fusion.34), channel_id=1, source_target_pairs={{0,8},{8,0},{16,24},{24,16},{1,9},{9,1},{17,25},{25,17},{2,10},{10... | collective-permute-start | bytes 786440 | tf_op jit(solution)/shard_map/ppermute | solution.py:21
  36.4 10.8 %collective-permute-start.6 = (f32[128,512]{1,0:T(8,128)S(1)}, f32[128,512]{1,0:T(8,128)S(1)}, u32[]{:S(2)}, u32[]{:S(2)}) collective-permute-start(f32[128,512]{1,0:T(8,128)S(1)} %add.176), channel_id=1, source_target_pairs={{0,8},{8,0},{16,24},{24,16},{1,9},{9,1},{17,25},{25,17},{2,10},{10... | collective-permute-start | bytes 786440 | tf_op jit(solution)/shard_map/ppermute | solution.py:21
  40.5 12.0 %collective-permute-start.3 = (f32[128,512]{1,0:T(8,128)S(1)}, f32[128,512]{1,0:T(8,128)S(1)}, u32[]{:S(2)}, u32[]{:S(2)}) collective-permute-start(f32[128,512]{1,0:T(8,128)S(1)} %add.174), channel_id=1, source_target_pairs={{0,24},{8,16},{16,8},{24,0},{1,25},{9,17},{17,9},{25,1},{2,26},{10... | collective-permute-start | bytes 786440 | tf_op jit(solution)/shard_map/ppermute | solution.py:21
  43.8 19.6 %copy-start.8 = (f32[8,40,256]{2,1,0:T(8,128)}, f32[8,40,256]{2,1,0:T(8,128)S(1)}, u32[]{:S(2)}) copy-start(f32[8,40,256]{2,1,0:T(8,128)S(1)} %dynamic-slice_dynamic-update-slice_fusion.4) | copy-start | bytes 983044
  52.7 4.0 %collective-permute-start.9 = (f32[1,128,64]{1,2,0:T(8,128)S(1)}, f32[1,128,64]{1,2,0:T(8,128)S(1)}, u32[]{:S(2)}, u32[]{:S(2)}) collective-permute-start(f32[1,128,64]{1,2,0:T(8,128)S(1)} %fusion.4), channel_id=1, source_target_pairs={{0,8},{8,0},{16,24},{24,16},{1,9},{9,1},{17,25},{25,17},{2,10},{10... | collective-permute-start | bytes 98312 | tf_op jit(solution)/shard_map/ppermute | solution.py:21
  56.7 6.1 %collective-permute-start.10 = (f32[2,128,64]{1,2,0:T(8,128)S(1)}, f32[2,128,64]{1,2,0:T(8,128)S(1)}, u32[]{:S(2)}, u32[]{:S(2)}) collective-permute-start(f32[2,128,64]{1,2,0:T(8,128)S(1)} %pad_maximum_fusion.10), channel_id=1, source_target_pairs={{0,24},{8,16},{16,8},{24,0},{1,25},{9,17},{17,9},{25,1},{2,26},{10... | collective-permute-start | bytes 196616 | tf_op jit(solution)/shard_map/ppermute | solution.py:21
  64.4 3.2 %copy-start.2 = (f32[1024,512]{1,0:T(8,128)S(1)}, f32[1024,512]{1,0:T(8,128)}, u32[]{:S(2)}) copy-start(f32[1024,512]{1,0:T(8,128)} %param.10) | copy-start | bytes 6291460
  64.5 8.3 %collective-permute-start.11 = (f32[128,768]{1,0:T(8,128)S(1)}, f32[128,768]{1,0:T(8,128)S(1)}, u32[]{:S(2)}, u32[]{:S(2)}) collective-permute-start(f32[128,768]{1,0:T(8,128)S(1)} %pad_maximum_fusion.4), channel_id=1, source_target_pairs={{0,4},{1,5},{2,6},{3,7},{4,0},{5,1},{6,2},{7,3},{8,12},{9,13},{10,... | collective-permute-start | bytes 1179656 | tf_op jit(solution)/shard_map/ppermute | solution.py:21
  67.7 6.9 %copy-start.4 = (f32[8,40,256]{2,1,0:T(8,128)S(1)}, f32[8,40,256]{2,1,0:T(8,128)}, u32[]{:S(2)}) copy-start(f32[8,40,256]{2,1,0:T(8,128)} %copy-done.3) | copy-start | bytes 983044
  68.4 8.0 %collective-permute-start.7 = (f32[128,512]{1,0:T(8,128)S(1)}, f32[128,512]{1,0:T(8,128)S(1)}, u32[]{:S(2)}, u32[]{:S(2)}) collective-permute-start(f32[128,512]{1,0:T(8,128)S(1)} %convolution_add_fusion.3), channel_id=1, source_target_pairs={{0,2},{1,3},{2,0},{3,1},{4,6},{5,7},{6,4},{7,5},{8,10},{9,11},{10,... | collective-permute-start | bytes 786440 | tf_op jit(solution)/shard_map/ppermute | solution.py:21
  72.8 11.2 %collective-permute-start.12 = (f32[128,768]{1,0:T(8,128)S(1)}, f32[128,768]{1,0:T(8,128)S(1)}, u32[]{:S(2)}, u32[]{:S(2)}) collective-permute-start(f32[128,768]{1,0:T(8,128)S(1)} %fusion.33), channel_id=1, source_target_pairs={{0,2},{1,3},{2,0},{3,1},{4,6},{5,7},{6,4},{7,5},{8,10},{9,11},{10,... | collective-permute-start | bytes 1179656 | tf_op jit(solution)/shard_map/ppermute | solution.py:21
  76.4 6.5 %collective-permute-start.8 = (f32[128,512]{1,0:T(8,128)S(1)}, f32[128,512]{1,0:T(8,128)}, u32[]{:S(2)}, u32[]{:S(2)}) collective-permute-start(f32[128,512]{1,0:T(8,128)S(1)} %add.179), channel_id=1, source_target_pairs={{0,4},{1,5},{2,6},{3,7},{4,0},{5,1},{6,2},{7,3},{8,12},{9,13},{10,... | collective-permute-start | bytes 786440 | tf_op jit(solution)/shard_map/ppermute | solution.py:21
  81.3 3.6 %copy-start.7 = (f32[8,1,256]{0,2,1:T(8,128)S(1)}, f32[8,1,256]{0,2,1:T(8,128)}, u32[]{:S(2)}) copy-start(f32[8,1,256]{0,2,1:T(8,128)} %copy.55) | copy-start | bytes 24580
  81.3 3.6 %copy-start.9 = (f32[8,40,256]{2,1,0:T(8,128)S(1)}, f32[8,40,256]{2,1,0:T(8,128)}, u32[]{:S(2)}) copy-start(f32[8,40,256]{2,1,0:T(8,128)} %dynamic-slice_dynamic-update-slice_fusion) | copy-start | bytes 983044
  84.9 2.6 %collective-permute-start.13 = (f32[128,1280]{1,0:T(8,128)}, f32[128,1280]{1,0:T(8,128)}, u32[]{:S(2)}, u32[]{:S(2)}) collective-permute-start(f32[128,1280]{1,0:T(8,128)} %pad_maximum_fusion.1), channel_id=1, source_target_pairs={{0,1},{1,0},{2,3},{3,2},{4,5},{5,4},{6,7},{7,6},{8,9},{9,8},{10,11... | collective-permute-start | bytes 1966088 | tf_op jit(solution)/shard_map/ppermute | solution.py:21
  91.8 2.9 %copy-start.5 = (f32[8,32,256]{2,1,0:T(8,128)S(1)}, f32[8,32,256]{2,1,0:T(8,128)}, u32[]{:S(2)}) copy-start(f32[8,32,256]{2,1,0:T(8,128)} %slice.60) | copy-start | bytes 786436
  91.8 3.8 %copy-start.10 = (s32[1,1,512]{2,1,0:T(1,128)S(1)}, s32[1,1,512]{2,1,0:T(1,128)}, u32[]{:S(2)}) copy-start(s32[1,1,512]{2,1,0:T(1,128)} %param.14) | copy-start | bytes 6148

commit v2 on v0

v2 whole, which is shorter than its diff:
```python
import jax
import jax.numpy as jnp
from jax import lax
from jax.experimental import pallas as pl
from jax.experimental.pallas import tpu as pltpu
from jax.sharding import PartitionSpec as P


F32, BF16 = jnp.float32, jnp.bfloat16
NN = (((1,), (0,)), ((), ()))
NT = (((1,), (1,)), ((), ()))


def swap(v, axis, mask):
    n = lax.axis_size(axis)
    return lax.ppermute(v, axis, [(i, i ^ mask) for i in range(n)])


def call(body, out, *args, scratch=(), flops=0):
    size = sum(a.size * a.dtype.itemsize for a in args) + sum(
        o.size * o.dtype.itemsize for o in out
    )
    specs = [pl.BlockSpec(memory_space=pltpu.VMEM)] * len(args)
    return pl.pallas_call(
        body,
        out_shape=out,
        in_specs=specs,
        out_specs=[pl.BlockSpec(memory_space=pltpu.VMEM)] * len(out),
        scratch_shapes=list(scratch),
        compiler_params=pltpu.CompilerParams(vmem_limit_bytes=2 * size + (2 << 20)),
        cost_estimate=pl.CostEstimate(flops=flops, bytes_accessed=size, transcendentals=0),
    )(*args)


def shape(s, d=F32):
    return jax.ShapeDtypeStruct(s, d)


def cut(v):
    high = v.astype(BF16)
    return high, (v - high.astype(F32)).astype(BF16)


def dot(a, b, dims):
    return lax.dot_general(a, b, dims, preferred_element_type=F32)


def three(ah, al, bh, bl, dims):
    n = ah.shape[0]
    both = dot(jnp.concatenate([ah, al], axis=0), bh, dims)
    return both[:n] + both[n:] + dot(ah, bl, dims)


def split(v, rows=256):
    n, m = v.shape

    def body(v_ref, h_ref, l_ref):
        def step(i, _):
            s = pl.ds(pl.multiple_of(i * rows, rows), rows)
            h_ref[s], l_ref[s] = cut(v_ref[s])
            return 0

        lax.fori_loop(0, n // rows, step, 0)

    return call(body, [shape((n, m), BF16)] * 2, v)


def adjoint(blocks, order, part, count, k):
    low, length = blocks[0].shape
    nb = len(blocks)
    take = count // low
    width = k[0].shape[1]

    def body(*refs):
        b, kr, outs = refs[:nb], refs[nb : nb + 4], refs[nb + 4 :]
        me = lax.shift_right_logical(lax.axis_index("col"), 1)
        rows = []
        for i in range(part * take, (part + 1) * take):
            want = jnp.bitwise_xor(me, i)
            v = b[0][...]
            for j in range(1, nb):
                v = jnp.where(want == order[j], b[j][...], v)
            rows.append(v)
        xh, xl = cut(jnp.concatenate(rows, axis=0) if take > 1 else rows[0])
        ps = [three(xh, xl, kr[2 * j][...], kr[2 * j + 1][...], NN) for j in range(2)]
        odd = jnp.bitwise_and(lax.axis_index("row"), 1) == 1
        outs[0][...] = jnp.where(odd, ps[1], ps[0])
        outs[1][...] = jnp.where(odd, ps[0], ps[1])

    return call(
        body,
        [shape((count, width))] * 2,
        *blocks,
        *k,
        flops=12 * count * length * width,
    )


def spread(axis, blocks, order, out_rows):
    n = len(blocks)

    def body(*refs):
        h = blocks[0].shape[0]
        me = lax.axis_index(axis)
        for j in range(n):
            at = jnp.bitwise_xor(me, order[j]) * h
            refs[n][pl.ds(pl.multiple_of(at, 8), h)] = refs[j][...]

    return call(body, [shape((out_rows, blocks[0].shape[1]))], *blocks)[0]


def forward_all(a, k, t):
    n, width = a[0].shape
    rows, tops = k[0].shape[0], t[0].shape[0]
    total = rows + tops
    half = total // 2

    def body(*refs):
        ar, kr, tr, outs = refs[:2], refs[2:6], refs[6:10], refs[10:]
        odd = jnp.bitwise_and(lax.axis_index("row"), 1) == 1
        kept, got = ar[0][...], ar[1][...]
        parts = [cut(jnp.where(odd, got, kept)), cut(jnp.where(odd, kept, got))]
        step = 256
        for lo in range(0, total, step):
            src, at = (kr, lo) if lo < rows else (tr, lo - rows)
            size = min(step, (rows if lo < rows else total) - lo)
            s = slice(at, at + size)
            p = None
            for j in range(2):
                h, l = parts[j]
                q = three(h, l, src[2 * j][s], src[2 * j + 1][s], NT)
                p = q if p is None else p + q
            for o in range(2):
                b, e = max(lo, o * half), min(lo + size, (o + 1) * half)
                if b < e:
                    outs[o][:, b - o * half : e - o * half] = p[:, b - lo : e - lo]

    return call(
        body, [shape((n, half))] * 2, *a, *k, *t, flops=12 * n * total * width
    )


def picks(tags, anc, block, mode_local, sep_local, slots, cands):
    fanout = tags.shape[0]
    rows = fanout * block
    seps = fanout * sep_local
    modes = slots * fanout
    count = anc.shape[1]

    def body(tag_ref, anc_ref, p_ref, q_ref):
        lane = lax.broadcasted_iota(jnp.int32, (fanout, block), 1)
        hit = (tag_ref[...] == lax.axis_index("col").astype(F32)) & (lane < mode_local)
        ones = jnp.where(hit, 1.0, 0.0).astype(BF16)
        before = lax.broadcasted_iota(jnp.int32, (block, block), 0) < lax.broadcasted_iota(
            jnp.int32, (block, block), 1
        )
        rank = dot(ones, jnp.where(before, 1.0, 0.0).astype(BF16), NN).astype(jnp.int32)
        place = lax.broadcasted_iota(jnp.int32, (fanout, block), 0) * slots + rank
        place = jnp.where(hit, place, -1)
        sep = (lane >= mode_local) & (lane < mode_local + sep_local)
        home = modes + lax.broadcasted_iota(jnp.int32, (fanout, block), 0) * sep_local + lane - mode_local
        place = jnp.where(sep, home, place)
        row = lax.broadcasted_iota(jnp.int32, (modes + seps, block), 0)
        for f in range(fanout):
            p_ref[:, f * block : (f + 1) * block] = jnp.where(row == place[f : f + 1], 1.0, 0.0).astype(BF16)
        which = lax.broadcasted_iota(jnp.int32, (cands, count), 0)
        q_ref[...] = jnp.where(which == anc_ref[...], 1.0, 0.0).astype(BF16)

    return call(body, [shape((modes + seps, rows), BF16), shape((cands, count), BF16)], tags, anc)


def expand(nblocks, own, other, coup, p, q, leaf, cons, part, parts, block, prior):
    n, wide = own.shape
    rows = p.shape[1]
    modes = leaf.shape[1]
    seps = p.shape[0] - modes
    count = cons.shape[1]
    inter = leaf.shape[0]
    sep_local = block
    nv = 2 * n
    tile = 256
    low = n * parts // nblocks

    def body(own_ref, other_ref, ch, cl, p_ref, q_ref, l_ref, c_ref, *rest):
        (sep_ref, out_ref, f_ref, dh, dl) = rest[len(prior) :]

        @pl.when(pl.program_id(0) == 0)
        def _():
            parity = jnp.bitwise_and(lax.axis_index("col"), 1)
            for i in range(n // low):
                s = slice(i * low, (i + 1) * low)
                a = pl.multiple_of(2 * i * low + parity * low, 8)
                b = pl.multiple_of(2 * i * low + (1 - parity) * low, 8)
                f_ref[pl.ds(a, low)] = own_ref[s]
                f_ref[pl.ds(b, low)] = other_ref[s]
            fh, fl = cut(f_ref[...])
            both = jnp.concatenate([fh, fl], axis=0)
            got = dot(both[:, :rows], p_ref[...], NT)
            th, tl = fh[:, rows:], fl[:, rows:]
            raw = got[:nv, modes:] + got[nv:, modes:]
            sep = raw + three(th, tl, ch[...], cl[...], NT)
            sh, sl = cut(sep)
            cand = jnp.concatenate(
                [jnp.concatenate([th, sh], axis=1), jnp.concatenate([tl, sl], axis=1)], axis=0
            )
            found = dot(cand, q_ref[...], NN)
            dh[:, :modes] = got[:, :modes].astype(BF16)
            dh[:, modes:] = found.astype(BF16)
            dl[...] = sep.T
            mine = pl.multiple_of(lax.axis_index("col") * sep_local, 8)
            sep_ref[...] = dl[pl.ds(mine, sep_local)]

        lh, ll = cut(l_ref[...])
        kh, kl = cut(c_ref[...])
        wh = jnp.concatenate([lh, kh], axis=1)
        wl = jnp.concatenate([ll, kl], axis=1)
        d = dh[...]
        y = dot(wh, d, NT)
        out_ref[...] = y[:, :nv] + y[:, nv:] + dot(wl, d[:nv], NT)

    full = lambda a: pl.BlockSpec(a.shape, lambda i: (0,) * a.ndim)
    args = [own, other, *coup, p, q]
    return pl.pallas_call(
        body,
        grid=(inter // tile,),
        out_shape=[shape((sep_local, nv * parts)), shape((inter, nv * parts))],
        in_specs=[full(a) for a in args]
        + [
            pl.BlockSpec((tile, modes), lambda i: (i, 0)),
            pl.BlockSpec((tile, count), lambda i: (i, 0)),
        ]
        + [pl.BlockSpec(memory_space=pl.ANY)] * len(prior),
        out_specs=[
            pl.BlockSpec((sep_local, nv), lambda i: (0, part)),
            pl.BlockSpec((tile, nv), lambda i: (i, part)),
        ],
        scratch_shapes=[
            pltpu.VMEM((nv, wide), F32),
            pltpu.VMEM((2 * nv, modes + count), BF16),
            pltpu.VMEM((seps, nv), F32),
        ],
        input_output_aliases={8 + i: i for i in range(len(prior))},
        compiler_params=pltpu.CompilerParams(
            vmem_limit_bytes=4 * sum(a.size * a.dtype.itemsize for a in args) + (8 << 20)
        ),
        cost_estimate=pl.CostEstimate(
            flops=12 * inter * (modes + count) * nv,
            bytes_accessed=4 * inter * (modes + count + nv),
            transcendentals=0,
        ),
    )(*args, leaf, cons, *prior)


def spans(masks):
    found = [0]
    for m in masks:
        found = found + [o ^ m for o in found]
    return found


def on_device(operator, vectors, owner_map, coupling, ancestors, leaf_modes, constraint_modes):
    planes = lax.axis_size("row")
    fanout = lax.axis_size("col")
    mode_local = owner_map.shape[0]
    sep_local, top_count = coupling.shape[1:]
    leaf, cons = leaf_modes[0, 0], constraint_modes[0, 0]
    slots = leaf.shape[1] // fanout
    row_count, width = operator.shape
    block = row_count // fanout
    top_local = block - mode_local - sep_local
    row_masks = [1 << b for b in range(planes.bit_length() - 1)]
    col_masks = [1 << b for b in range(1, fanout.bit_length() - 1)]

    partner = swap(operator, "col", 1)
    xt = vectors.T
    col_order = spans(col_masks)
    blocks = [xt] + [swap(xt, "col", m) for m in col_order[1:]]
    tops = operator.reshape(fanout, block, width)[:, block - top_local :].reshape(-1, width)
    row_order = spans(row_masks)
    tops = [tops] + [swap(tops, "row", m) for m in row_order[1:]]
    k = split(operator)
    k = k + split(partner)

    parts = 2
    half_nv = xt.shape[0] * len(blocks)
    count = half_nv // parts
    order = [o // 2 for o in col_order]
    adj = []
    for h in range(parts):
        adj.append(list(adjoint(blocks, order, h, count, k)))
    tops = spread("row", list(tops), row_order, top_count)
    tops_partner = swap(tops, "col", 1)
    t = split(tops) + split(tops_partner)

    tag_rows = -(-mode_local // top_count)
    owner_map, coupling, _ = lax.optimization_barrier((owner_map, coupling, adj[1][0]))
    tags = owner_map[:, 0].astype(F32)
    tags = jnp.pad(tags, (0, tag_rows * top_count - mode_local), constant_values=-1.0).reshape(tag_rows, top_count)
    small = jnp.concatenate([coupling[0], jnp.pad(tags, ((0, -tag_rows % 8), (0, 0)))], axis=0)
    stack = small[None]
    for m in [1] + col_masks:
        stack = jnp.concatenate([stack, swap(stack, "col", m)], axis=0)
    small_order = spans([1] + col_masks)
    gathered = spread("col", list(stack), small_order, fanout * small.shape[0]).reshape(fanout, -1, top_count)
    coup = split(gathered[:, :sep_local].reshape(fanout * sep_local, top_count))
    tags = gathered[:, sep_local : sep_local + tag_rows].reshape(fanout, -1)[:, :block]
    p, q = picks(
        tags, ancestors[0], block, mode_local, sep_local, slots, top_count + fanout * sep_local
    )

    prior = ()
    for h in range(parts):
        a = list(adj[h])
        kept = a[0] + swap(a[1], "row", row_masks[0])
        for m in row_masks[1:]:
            kept = kept + swap(kept, "row", m)
        got = swap(kept, "row", row_masks[0])
        f = list(forward_all([kept, got], k, t))
        n = len(col_masks)
        for step in range(n):
            moved = [swap(v, "col", col_masks[(i + step) % n]) for i, v in enumerate(f)]
            f = [u + v for u, v in zip(f, moved)]
        own = jnp.concatenate(f, axis=1)
        other = swap(own, "col", 1)
        prior = expand(
            len(blocks), own, other, coup, p, q, leaf, cons, h, parts, sep_local, prior
        )
    return (prior[0][None], prior[1][None, None])


def solution(mesh):
    in_specs = (
        P("row", "col"),
        P("row", "col"),
        P(("row", "col"), None),
        P("row", "col", None),
        P("row", "col", None),
        P("row", "col", None, None),
        P("row", "col", None, None),
    )
    out_specs = (P("row", "col", None), P("row", "col", None, None))

    return jax.shard_map(on_device, mesh=mesh, in_specs=in_specs, out_specs=out_specs, check_vma=False)
```

time: 208 us -> 81.9 us (0.39)
  blocking collectives: 66.5 us -> 0 us
  waiting for transfers between devices: 83.8 us -> 29.8 us
  matrix products: 29.5 us -> 0 us
  starting transfers between devices: 3.53 us -> 30.1 us
  Pallas kernels: 0 us -> 17.9 us
  between operations: 13.9 us -> 1.03 us
  local copies, waits for them, and re-layouts: 9.27 us -> 2.6 us
    all_gather x3 -> x0, blocking collectives: 66.5 us -> none  [the longest x1 42.6 us: on_device(): top_gathered = lax.all_gather(top_local, ('row', 'col'), axis=0, tiled=True)]
    reduce_scatter x2 -> x0, waiting for transfers between devices: 55 us -> none  [the longest x1 33.1 us: on_device(): lax.psum_scatter(forward, 'col', scatter_dimension=0, tiled=True)]
    ppermute x0 -> x27, starting transfers between devices: none -> 30.1 us  [swap(): return lax.ppermute(v, axis, [(i, i ^ mask) for i in range(n)])]
    ppermute x0 -> x27, waiting for transfers between devices: none -> 29.8 us  [swap(): return lax.ppermute(v, axis, [(i, i ^ mask) for i in range(n)])]
    dot_general x5 -> x0, matrix products: 29.5 us -> none  [the longest x1 10.4 us: on_device(): jnp.dot(constraint_modes[0, 0], picked, precision=highest, preferred_elem...]
    all_gather x1 -> x0, waiting for transfers between devices: 28 us -> none  [on_device(): lax.all_gather(vectors, 'col', axis=1, tiled=True)]
    pallas_call x0 -> x14, Pallas kernels: none -> 17.9 us  [the longest x2 10.9 us: expand(): pl.pallas_call(body, grid=(inter // tile,), out_shape=[shape((sep_local,...]
    all_to_all x1 -> x0, starting transfers between devices: 3.41 us -> none  [on_device(): lax.all_to_all(outgoing, 'col', split_axis=0, concat_axis=0, tiled=True)]
  transfers between devices with their start and end apart: 4 -> 27, of which waited for: 3 -> 14; matrix products, arithmetic and copies ran while one was open for 7% -> 2% of each run, Pallas kernels for 0% -> 15%
where the time goes in v2:
time: 81.9 us; the launch traced here: 81.7 us
  starting transfers between devices  30.1 us (37%)
  waiting for transfers between devices  29.8 us (36%)
  Pallas kernels  17.9 us (22%)
  local copies, waits for them, and re-layouts  2.6 us (3%)
  between operations  1.03 us (1%)
    ppermute x27, starting transfers between devices, swap(): return lax.ppermute(v, axis, [(i, i ^ mask) for i in range(n)])  30.1 us
    ppermute x27, waiting for transfers between devices, swap(): return lax.ppermute(v, axis, [(i, i ^ mask) for i in range(n)])  29.8 us
    pallas_call x2, Pallas kernels, expand(): pl.pallas_call(body, grid=(inter // tile,), out_shape=[shape((sep_local,...  10.9 us
    pallas_call x12, Pallas kernels, call(): pl.pallas_call(body, out_shape=out, in_specs=specs, out_specs=[pl.BlockSp...  6.97 us
  transfers between devices with their start and end apart: 27, of which 14 were waited for; matrix products, arithmetic and copies ran while one was open for 2% of the time, Pallas kernels for 15%

profile of v2, /device:TPU:0, one launch (start us, length us, event | category | flops | bytes accessed | tf_op | source)
XLA Modules:
  0.0 81.7 jit_solution(2155484995229377286)
XLA Ops:
  0.6 0.6 collective-permute-start.3
  1.2 0.9 %slice_bitcast_fusion.refs_0_ = f32[64,512]{1,0:T(8,128)S(1)} fusion(f32[8,128,512]{2,1,0:T(8,128)} %bitcast.35), kind=kLoop, calls=%fused_computation.3 | loop fusion | bytes 262144 | tf_op jit(solution)/shard_map/reshape | solution.py:278
  2.1 4.7 %collective-permute-start.9 = (f32[64,512]{1,0:T(8,128)S(1)}, f32[64,512]{1,0:T(8,128)S(1)}, u32[]{:S(2)}, u32[]{:S(2)}) collective-permute-start(f32[64,512]{1,0:T(8,128)S(1)} %slice_bitcast_fusion.refs_0_), channel_id=1, source_target_pairs={{0,24},{8,16},{16,8},{24,0},{1,25},{9,17},{17,9},{25,1},{2,26},{10... | collective-permute-start | bytes 393224 | tf_op jit(solution)/shard_map/ppermute | solution.py:16
  6.8 0.6 collective-permute-start.7
  7.4 2.6 %collective-permute-start.2 = (f32[32,1024]{1,0:T(8,128)}, f32[32,1024]{1,0:T(8,128)S(1)}, u32[]{:S(2)}, u32[]{:S(2)}) collective-permute-start(f32[32,1024]{1,0:T(8,128)} %bitcast.41), channel_id=1, source_target_pairs={{0,6},{1,7},{2,4},{3,5},{4,2},{5,3},{6,0},{7,1},{8,14},{9,15},{10,... | collective-permute-start | bytes 393224 | tf_op jit(solution)/shard_map/ppermute | solution.py:16
  10.0 1.2 %collective-permute-done.9.refs_3_ = f32[64,512]{1,0:T(8,128)S(1)} collective-permute-done((f32[64,512]{1,0:T(8,128)S(1)}, f32[64,512]{1,0:T(8,128)S(1)}, u32[]{:S(2)}, u32[]{:S(2)}) %collective-permute-start.9) | collective-permute-done | bytes 131104 | tf_op jit(solution)/shard_map/ppermute | solution.py:16
  11.2 1.7 %collective-permute-start.1 = (f32[32,1024]{1,0:T(8,128)}, f32[32,1024]{1,0:T(8,128)S(1)}, u32[]{:S(2)}, u32[]{:S(2)}) collective-permute-start(f32[32,1024]{1,0:T(8,128)} %bitcast.42), channel_id=1, source_target_pairs={{0,4},{1,5},{2,6},{3,7},{4,0},{5,1},{6,2},{7,3},{8,12},{9,13},{10,... | collective-permute-start | bytes 393224 | tf_op jit(solution)/shard_map/ppermute | solution.py:16
  13.0 5.5 %collective-permute-done.8.refs_2_ = f32[64,512]{1,0:T(8,128)S(1)} collective-permute-done((f32[64,512]{1,0:T(8,128)S(1)}, f32[64,512]{1,0:T(8,128)S(1)}, u32[]{:S(2)}, u32[]{:S(2)}) %collective-permute-start.8) | collective-permute-done | bytes 131104 | tf_op jit(solution)/shard_map/ppermute | solution.py:16
  18.5 1.5 %collective-permute-start = (f32[32,1024]{1,0:T(8,128)}, f32[32,1024]{1,0:T(8,128)S(1)}, u32[]{:S(2)}, u32[]{:S(2)}) collective-permute-start(f32[32,1024]{1,0:T(8,128)} %bitcast.43), channel_id=1, source_target_pairs={{0,2},{1,3},{2,0},{3,1},{4,6},{5,7},{6,4},{7,5},{8,10},{9,11},{10,... | collective-permute-start | bytes 393224 | tf_op jit(solution)/shard_map/ppermute | solution.py:16
  20.0 1.6 %copy-done.1 = f32[1024,512]{1,0:T(8,128)S(1)} copy-done((f32[1024,512]{1,0:T(8,128)S(1)}, f32[1024,512]{1,0:T(8,128)}, u32[]{:S(2)}) %copy-start.1) | copy-done | bytes 2097176
  21.6 0.4 shard_map.86
  22.0 0.1 collective-permute-start.10
  22.1 0.4 shard_map.87
  22.5 1.2 %collective-permute-done.refs_1_ = f32[32,1024]{1,0:T(8,128)S(1)} collective-permute-done((f32[32,1024]{1,0:T(8,128)}, f32[32,1024]{1,0:T(8,128)S(1)}, u32[]{:S(2)}, u32[]{:S(2)}) %collective-permute-start) | collective-permute-done | bytes 131104 | tf_op jit(solution)/shard_map/ppermute | solution.py:16
  23.8 0.8 shard_map.88
  24.6 0.8 shard_map.96
  25.5 2.0 %collective-permute-start.4 = (f32[64,512]{1,0:T(8,128)S(1)}, f32[64,512]{1,0:T(8,128)S(1)}, u32[]{:S(2)}, u32[]{:S(2)}) collective-permute-start(f32[64,512]{1,0:T(8,128)S(1)} %get-tuple-element.33), channel_id=1, source_target_pairs={{0,8},{8,0},{16,24},{24,16},{1,9},{9,1},{17,25},{25,17},{2,10},{10... | collective-permute-start | bytes 393224 | tf_op jit(solution)/shard_map/ppermute | solution.py:16
  27.5 4.0 %collective-permute-done.19 = f32[64,512]{1,0:T(8,128)S(1)} collective-permute-done((f32[64,512]{1,0:T(8,128)S(1)}, f32[64,512]{1,0:T(8,128)S(1)}, u32[]{:S(2)}, u32[]{:S(2)}) %collective-permute-start.19) | collective-permute-done | bytes 131104 | tf_op jit(solution)/shard_map/ppermute | solution.py:16
  31.5 1.3 %collective-permute-start.20 = (f32[64,512]{1,0:T(8,128)S(1)}, f32[64,512]{1,0:T(8,128)S(1)}, u32[]{:S(2)}, u32[]{:S(2)}) collective-permute-start(f32[64,512]{1,0:T(8,128)S(1)} %add.46), channel_id=1, source_target_pairs={{0,16},{8,24},{16,0},{24,8},{1,17},{9,25},{17,1},{25,9},{2,18},{10... | collective-permute-start | bytes 393224 | tf_op jit(solution)/shard_map/ppermute | solution.py:16
  32.9 1.0 %collective-permute-done.4 = f32[64,512]{1,0:T(8,128)S(1)} collective-permute-done((f32[64,512]{1,0:T(8,128)S(1)}, f32[64,512]{1,0:T(8,128)S(1)}, u32[]{:S(2)}, u32[]{:S(2)}) %collective-permute-start.4) | collective-permute-done | bytes 131104 | tf_op jit(solution)/shard_map/ppermute | solution.py:16
  34.0 1.7 %collective-permute-start.5 = (f32[64,512]{1,0:T(8,128)S(1)}, f32[64,512]{1,0:T(8,128)S(1)}, u32[]{:S(2)}, u32[]{:S(2)}) collective-permute-start(f32[64,512]{1,0:T(8,128)S(1)} %add.40), channel_id=1, source_target_pairs={{0,16},{8,24},{16,0},{24,8},{1,17},{9,25},{17,1},{25,9},{2,18},{10... | collective-permute-start | bytes 393224 | tf_op jit(solution)/shard_map/ppermute | solution.py:16
  35.7 7.0 %collective-permute-done.20 = f32[64,512]{1,0:T(8,128)S(1)} collective-permute-done((f32[64,512]{1,0:T(8,128)S(1)}, f32[64,512]{1,0:T(8,128)S(1)}, u32[]{:S(2)}, u32[]{:S(2)}) %collective-permute-start.20) | collective-permute-done | bytes 131104 | tf_op jit(solution)/shard_map/ppermute | solution.py:16
  42.7 0.1 collective-permute-start.21
  42.8 1.1 %collective-permute-start.17 = (f32[2,40,256]{2,1,0:T(8,128)S(1)}, f32[2,40,256]{2,1,0:T(8,128)S(1)}, u32[]{:S(2)}, u32[]{:S(2)}) collective-permute-start(f32[2,40,256]{2,1,0:T(8,128)S(1)} %pad_maximum_fusion.3), channel_id=1, source_target_pairs={{0,2},{1,3},{2,0},{3,1},{4,6},{5,7},{6,4},{7,5},{8,10},{9,11},{10,... | collective-permute-start | bytes 245768 | tf_op jit(solution)/shard_map/ppermute | solution.py:16
  43.9 0.1 shard_map.90
  44.0 0.1 shard_map.91
  44.2 1.9 %collective-permute-start.6 = (f32[64,512]{1,0:T(8,128)S(1)}, f32[64,512]{1,0:T(8,128)S(1)}, u32[]{:S(2)}, u32[]{:S(2)}) collective-permute-start(f32[64,512]{1,0:T(8,128)S(1)} %add.41.refs_0_), channel_id=1, source_target_pairs={{0,8},{8,0},{16,24},{24,16},{1,9},{9,1},{17,25},{25,17},{2,10},{10... | collective-permute-start | bytes 393224 | tf_op jit(solution)/shard_map/ppermute | solution.py:16
  46.1 2.4 %collective-permute-done.21.refs_1_ = f32[64,512]{1,0:T(8,128)S(1)} collective-permute-done((f32[64,512]{1,0:T(8,128)S(1)}, f32[64,512]{1,0:T(8,128)S(1)}, u32[]{:S(2)}, u32[]{:S(2)}) %collective-permute-start.21) | collective-permute-done | bytes 131104 | tf_op jit(solution)/shard_map/ppermute | solution.py:16
  48.5 1.7 %shard_map.97 = (f32[64,640]{1,0:T(8,128)S(1)}, f32[64,640]{1,0:T(8,128)S(1)}) custom-call(f32[64,512]{1,0:T(8,128)S(1)} %add.47.refs_0_, f32[64,512]{1,0:T(8,128)S(1)} %collective-permute-done.21.refs_1_, bf16[1024,512]{1,0:T(8,128)(2,1)S(1)} %get-tuple-element.28.refs_4_.refs_2_, bf16[1024,512]{1,0:T(8,128)(2,1)S(1)} %get-tuple-element.29.refs_5_.refs_3_, ...), custom_call_target="tpu_custom_call" | custom-call | flops 503316480 | bytes 5832704 | tf_op jit(solution)/shard_map/pallas_call | solution.py:24
  50.2 1.3 %collective-permute-start.22 = (f32[64,640]{1,0:T(8,128)S(1)}, f32[64,640]{1,0:T(8,128)S(1)}, u32[]{:S(2)}, u32[]{:S(2)}) collective-permute-start(f32[64,640]{1,0:T(8,128)S(1)} %get-tuple-element.48), channel_id=1, source_target_pairs={{0,2},{1,3},{2,0},{3,1},{4,6},{5,7},{6,4},{7,5},{8,10},{9,11},{10,... | collective-permute-start | bytes 491528 | tf_op jit(solution)/shard_map/ppermute | solution.py:16
  51.5 1.5 %collective-permute-start.24 = (f32[64,640]{1,0:T(8,128)S(1)}, f32[64,640]{1,0:T(8,128)S(1)}, u32[]{:S(2)}, u32[]{:S(2)}) collective-permute-start(f32[64,640]{1,0:T(8,128)S(1)} %get-tuple-element.49), channel_id=1, source_target_pairs={{0,4},{1,5},{2,6},{3,7},{4,0},{5,1},{6,2},{7,3},{8,12},{9,13},{10,... | collective-permute-start | bytes 491528 | tf_op jit(solution)/shard_map/ppermute | solution.py:16
  53.0 0.6 collective-permute-start.18
  53.6 1.7 %shard_map.92 = (f32[64,640]{1,0:T(8,128)S(1)}, f32[64,640]{1,0:T(8,128)S(1)}) custom-call(f32[64,512]{1,0:T(8,128)S(1)} %add.41.refs_0_, f32[64,512]{1,0:T(8,128)S(1)} %collective-permute-done.6.refs_1_, bf16[1024,512]{1,0:T(8,128)(2,1)S(1)} %get-tuple-element.28.refs_4_.refs_2_, bf16[1024,512]{1,0:T(8,128)(2,1)S(1)} %get-tuple-element.29.refs_5_.refs_3_, ...), custom_call_target="tpu_custom_call" | custom-call | flops 503316480 | bytes 5832704 | tf_op jit(solution)/shard_map/pallas_call | solution.py:24
  55.4 0.8 %collective-permute-start.11 = (f32[64,640]{1,0:T(8,128)S(1)}, f32[64,640]{1,0:T(8,128)S(1)}, u32[]{:S(2)}, u32[]{:S(2)}) collective-permute-start(f32[64,640]{1,0:T(8,128)S(1)} %get-tuple-element.38), channel_id=1, source_target_pairs={{0,2},{1,3},{2,0},{3,1},{4,6},{5,7},{6,4},{7,5},{8,10},{9,11},{10,... | collective-permute-start | bytes 491528 | tf_op jit(solution)/shard_map/ppermute | solution.py:16
  56.2 1.5 %collective-permute-start.13 = (f32[64,640]{1,0:T(8,128)S(1)}, f32[64,640]{1,0:T(8,128)S(1)}, u32[]{:S(2)}, u32[]{:S(2)}) collective-permute-start(f32[64,640]{1,0:T(8,128)S(1)} %get-tuple-element.39), channel_id=1, source_target_pairs={{0,4},{1,5},{2,6},{3,7},{4,0},{5,1},{6,2},{7,3},{8,12},{9,13},{10,... | collective-permute-start | bytes 491528 | tf_op jit(solution)/shard_map/ppermute | solution.py:16
  57.7 0.6 collective-permute-start.23
  58.3 0.3 collective-permute-done.24
  58.6 1.7 %collective-permute-start.25 = (f32[64,640]{1,0:T(8,128)S(1)}, f32[64,640]{1,0:T(8,128)S(1)}, u32[]{:S(2)}, u32[]{:S(2)}) collective-permute-start(f32[64,640]{1,0:T(8,128)S(1)} %add.50), channel_id=1, source_target_pairs={{0,2},{1,3},{2,0},{3,1},{4,6},{5,7},{6,4},{7,5},{8,10},{9,11},{10,... | collective-permute-start | bytes 491528 | tf_op jit(solution)/shard_map/ppermute | solution.py:16
  60.3 1.8 %collective-permute-done.11 = f32[64,640]{1,0:T(8,128)S(1)} collective-permute-done((f32[64,640]{1,0:T(8,128)S(1)}, f32[64,640]{1,0:T(8,128)S(1)}, u32[]{:S(2)}, u32[]{:S(2)}) %collective-permute-start.11) | collective-permute-done | bytes 163872 | tf_op jit(solution)/shard_map/ppermute | solution.py:16
  62.1 1.4 %collective-permute-start.12 = (f32[64,640]{1,0:T(8,128)S(1)}, f32[64,640]{1,0:T(8,128)S(1)}, u32[]{:S(2)}, u32[]{:S(2)}) collective-permute-start(f32[64,640]{1,0:T(8,128)S(1)} %add.42), channel_id=1, source_target_pairs={{0,4},{1,5},{2,6},{3,7},{4,0},{5,1},{6,2},{7,3},{8,12},{9,13},{10,... | collective-permute-start | bytes 491528 | tf_op jit(solution)/shard_map/ppermute | solution.py:16
  63.5 0.6 collective-permute-done.13
  64.2 0.5 collective-permute-start.14
  64.7 1.2 %collective-permute-done.23 = f32[64,640]{1,0:T(8,128)S(1)} collective-permute-done((f32[64,640]{1,0:T(8,128)S(1)}, f32[64,640]{1,0:T(8,128)S(1)}, u32[]{:S(2)}, u32[]{:S(2)}) %collective-permute-start.23) | collective-permute-done | bytes 163872 | tf_op jit(solution)/shard_map/ppermute | solution.py:16
  66.1 1.6 %collective-permute-done.12 = f32[64,640]{1,0:T(8,128)S(1)} collective-permute-done((f32[64,640]{1,0:T(8,128)S(1)}, f32[64,640]{1,0:T(8,128)S(1)}, u32[]{:S(2)}, u32[]{:S(2)}) %collective-permute-start.12) | collective-permute-done | bytes 163872 | tf_op jit(solution)/shard_map/ppermute | solution.py:16
  67.7 1.9 %collective-permute-done.14 = f32[64,640]{1,0:T(8,128)S(1)} collective-permute-done((f32[64,640]{1,0:T(8,128)S(1)}, f32[64,640]{1,0:T(8,128)S(1)}, u32[]{:S(2)}, u32[]{:S(2)}) %collective-permute-start.14) | collective-permute-done | bytes 163872 | tf_op jit(solution)/shard_map/ppermute | solution.py:16
  69.9 0.9 %shard_map.95 = (bf16[512,1024]{1,0:T(8,128)(2,1)S(1)}, bf16[512,512]{1,0:T(8,128)(2,1)S(1)}) custom-call(f32[8,128]{1,0:T(8,128)S(1)} %slice.19.tag_ref, s32[1,512]{1,0:T(1,128)S(1)} %bitcast.47), custom_call_target="tpu_custom_call" | custom-call | bytes 1579008 | tf_op jit(solution)/shard_map/pallas_call | solution.py:24
  70.8 5.5 %shard_map.98 = (f32[32,256]{1,0:T(8,128)}, f32[2048,256]{1,0:T(8,128)}) custom-call(f32[64,1280]{1,0:T(8,128)S(1)} %pad_maximum_fusion.1.own_ref, f32[64,1280]{1,0:T(8,128)S(1)} %collective-permute-done.26.other_ref, bf16[256,256]{1,0:T(8,128)(2,1)S(1)} %get-tuple-element.42.ch, bf16[256,256]{1,0:T(8,128)(2,1)S(1)} %get-tuple-element.43.cl, ...), custom_call_target="tpu_custom_call" | custom-call | flops 2415919104 | bytes 7340032 | tf_op jit(solution)/shard_map/pallas_call | solution.py:223
  76.3 5.4 %shard_map.99 = (f32[32,256]{1,0:T(8,128)}, f32[2048,256]{1,0:T(8,128)}) custom-call(f32[64,1280]{1,0:T(8,128)S(1)} %pad_maximum_fusion.own_ref, f32[64,1280]{1,0:T(8,128)S(1)} %collective-permute-done.15.other_ref, bf16[256,256]{1,0:T(8,128)(2,1)S(1)} %get-tuple-element.42.ch, ...), custom_call_target="tpu_custom_call", output_to_operand_aliasing={{0}: (8, {}), {1}: (9, {})} | custom-call | flops 2415919104 | bytes 7340032 | tf_op jit(solution)/shard_map/pallas_call | solution.py:223
  (60 shorter events, 0.9 us)
Async XLA Ops:
  0.6 21.5 %collective-permute-start.3 = (f32[1024,512]{1,0:T(8,128)}, f32[1024,512]{1,0:T(8,128)S(1)}, u32[]{:S(2)}, u32[]{:S(2)}) collective-permute-start(f32[1024,512]{1,0:T(8,128)} %v_ref.1), channel_id=1, source_target_pairs={{0,1},{1,0},{2,3},{3,2},{4,5},{5,4},{6,7},{7,6},{8,9},{9,8},{10,11... | collective-permute-start | bytes 6291464 | tf_op jit(solution)/shard_map/ppermute | solution.py:16
  2.1 9.1 %collective-permute-start.9 = (f32[64,512]{1,0:T(8,128)S(1)}, f32[64,512]{1,0:T(8,128)S(1)}, u32[]{:S(2)}, u32[]{:S(2)}) collective-permute-start(f32[64,512]{1,0:T(8,128)S(1)} %slice_bitcast_fusion.refs_0_), channel_id=1, source_target_pairs={{0,24},{8,16},{16,8},{24,0},{1,25},{9,17},{17,9},{25,1},{2,26},{10... | collective-permute-start | bytes 393224 | tf_op jit(solution)/shard_map/ppermute | solution.py:16
  6.8 11.7 %collective-permute-start.8 = (f32[64,512]{1,0:T(8,128)S(1)}, f32[64,512]{1,0:T(8,128)S(1)}, u32[]{:S(2)}, u32[]{:S(2)}) collective-permute-start(f32[64,512]{1,0:T(8,128)S(1)} %slice_bitcast_fusion.refs_0_), channel_id=1, source_target_pairs={{0,16},{8,24},{16,0},{24,8},{1,17},{9,25},{17,1},{25,9},{2,18},{10... | collective-permute-start | bytes 393224 | tf_op jit(solution)/shard_map/ppermute | solution.py:16
  6.8 15.2 %collective-permute-start.7 = (f32[64,512]{1,0:T(8,128)S(1)}, f32[64,512]{1,0:T(8,128)S(1)}, u32[]{:S(2)}, u32[]{:S(2)}) collective-permute-start(f32[64,512]{1,0:T(8,128)S(1)} %slice_bitcast_fusion.refs_0_), channel_id=1, source_target_pairs={{0,8},{8,0},{16,24},{24,16},{1,9},{9,1},{17,25},{25,17},{2,10},{10... | collective-permute-start | bytes 393224 | tf_op jit(solution)/shard_map/ppermute | solution.py:16
  7.4 15.1 %collective-permute-start.2 = (f32[32,1024]{1,0:T(8,128)}, f32[32,1024]{1,0:T(8,128)S(1)}, u32[]{:S(2)}, u32[]{:S(2)}) collective-permute-start(f32[32,1024]{1,0:T(8,128)} %bitcast.41), channel_id=1, source_target_pairs={{0,6},{1,7},{2,4},{3,5},{4,2},{5,3},{6,0},{7,1},{8,14},{9,15},{10,... | collective-permute-start | bytes 393224 | tf_op jit(solution)/shard_map/ppermute | solution.py:16
  11.2 11.3 %collective-permute-start.1 = (f32[32,1024]{1,0:T(8,128)}, f32[32,1024]{1,0:T(8,128)S(1)}, u32[]{:S(2)}, u32[]{:S(2)}) collective-permute-start(f32[32,1024]{1,0:T(8,128)} %bitcast.42), channel_id=1, source_target_pairs={{0,4},{1,5},{2,6},{3,7},{4,0},{5,1},{6,2},{7,3},{8,12},{9,13},{10,... | collective-permute-start | bytes 393224 | tf_op jit(solution)/shard_map/ppermute | solution.py:16
  18.5 5.2 %collective-permute-start = (f32[32,1024]{1,0:T(8,128)}, f32[32,1024]{1,0:T(8,128)S(1)}, u32[]{:S(2)}, u32[]{:S(2)}) collective-permute-start(f32[32,1024]{1,0:T(8,128)} %bitcast.43), channel_id=1, source_target_pairs={{0,2},{1,3},{2,0},{3,1},{4,6},{5,7},{6,4},{7,5},{8,10},{9,11},{10,... | collective-permute-start | bytes 393224 | tf_op jit(solution)/shard_map/ppermute | solution.py:16
  20.0 1.6 %copy-start.1 = (f32[1024,512]{1,0:T(8,128)S(1)}, f32[1024,512]{1,0:T(8,128)}, u32[]{:S(2)}) copy-start(f32[1024,512]{1,0:T(8,128)} %v_ref.1) | copy-start | bytes 6291460
  22.0 1.8 %copy-start.3 = (f32[1024,32]{0,1:T(8,128)S(1)}, f32[1024,32]{0,1:T(8,128)}, u32[]{:S(2)}) copy-start(f32[1024,32]{0,1:T(8,128)} %param.8) | copy-start | bytes 393220
  22.0 22.0 %collective-permute-start.10 = (f32[256,512]{1,0:T(8,128)S(1)}, f32[256,512]{1,0:T(8,128)S(1)}, u32[]{:S(2)}, u32[]{:S(2)}) collective-permute-start(f32[256,512]{1,0:T(8,128)S(1)} %shard_map.89.v_ref), channel_id=1, source_target_pairs={{0,1},{1,0},{2,3},{3,2},{4,5},{5,4},{6,7},{7,6},{8,9},{9,8},{10,11... | collective-permute-start | bytes 1572872 | tf_op jit(solution)/shard_map/ppermute | solution.py:16
  24.6 2.9 %copy-start.6 = (s32[88,1]{0,1:T(1,128)S(1)}, s32[88,1]{0,1:T(1,128)}, u32[]{:S(2)}) copy-start(s32[88,1]{0,1:T(1,128)} %param.9) | copy-start | bytes 1060
  24.6 8.3 %copy-start.5 = (f32[1,32,256]{2,1,0:T(8,128)S(1)}, f32[1,32,256]{2,1,0:T(8,128)}, u32[]{:S(2)}) copy-start(f32[1,32,256]{2,1,0:T(8,128)} %param.10) | copy-start | bytes 98308
  25.4 6.1 %collective-permute-start.19 = (f32[64,512]{1,0:T(8,128)S(1)}, f32[64,512]{1,0:T(8,128)S(1)}, u32[]{:S(2)}, u32[]{:S(2)}) collective-permute-start(f32[64,512]{1,0:T(8,128)S(1)} %get-tuple-element.47), channel_id=1, source_target_pairs={{0,8},{8,0},{16,24},{24,16},{1,9},{9,1},{17,25},{25,17},{2,10},{10... | collective-permute-start | bytes 393224 | tf_op jit(solution)/shard_map/ppermute | solution.py:16
  25.5 8.5 %collective-permute-start.4 = (f32[64,512]{1,0:T(8,128)S(1)}, f32[64,512]{1,0:T(8,128)S(1)}, u32[]{:S(2)}, u32[]{:S(2)}) collective-permute-start(f32[64,512]{1,0:T(8,128)S(1)} %get-tuple-element.33), channel_id=1, source_target_pairs={{0,8},{8,0},{16,24},{24,16},{1,9},{9,1},{17,25},{25,17},{2,10},{10... | collective-permute-start | bytes 393224 | tf_op jit(solution)/shard_map/ppermute | solution.py:16
  31.5 11.1 %collective-permute-start.20 = (f32[64,512]{1,0:T(8,128)S(1)}, f32[64,512]{1,0:T(8,128)S(1)}, u32[]{:S(2)}, u32[]{:S(2)}) collective-permute-start(f32[64,512]{1,0:T(8,128)S(1)} %add.46), channel_id=1, source_target_pairs={{0,16},{8,24},{16,0},{24,8},{1,17},{9,25},{17,1},{25,9},{2,18},{10... | collective-permute-start | bytes 393224 | tf_op jit(solution)/shard_map/ppermute | solution.py:16
  32.9 9.9 %collective-permute-start.16 = (f32[1,40,256]{2,1,0:T(8,128)S(1)}, f32[1,40,256]{2,1,0:T(8,128)S(1)}, u32[]{:S(2)}, u32[]{:S(2)}) collective-permute-start(f32[1,40,256]{2,1,0:T(8,128)S(1)} %get-tuple-element.60), channel_id=1, source_target_pairs={{0,1},{1,0},{2,3},{3,2},{4,5},{5,4},{6,7},{7,6},{8,9},{9,8},{10,11... | collective-permute-start | bytes 122888 | tf_op jit(solution)/shard_map/ppermute | solution.py:16
  34.0 10.2 %collective-permute-start.5 = (f32[64,512]{1,0:T(8,128)S(1)}, f32[64,512]{1,0:T(8,128)S(1)}, u32[]{:S(2)}, u32[]{:S(2)}) collective-permute-start(f32[64,512]{1,0:T(8,128)S(1)} %add.40), channel_id=1, source_target_pairs={{0,16},{8,24},{16,0},{24,8},{1,17},{9,25},{17,1},{25,9},{2,18},{10... | collective-permute-start | bytes 393224 | tf_op jit(solution)/shard_map/ppermute | solution.py:16
  42.7 5.8 %collective-permute-start.21 = (f32[64,512]{1,0:T(8,128)S(1)}, f32[64,512]{1,0:T(8,128)S(1)}, u32[]{:S(2)}, u32[]{:S(2)}) collective-permute-start(f32[64,512]{1,0:T(8,128)S(1)} %add.47.refs_0_), channel_id=1, source_target_pairs={{0,8},{8,0},{16,24},{24,16},{1,9},{9,1},{17,25},{25,17},{2,10},{10... | collective-permute-start | bytes 393224 | tf_op jit(solution)/shard_map/ppermute | solution.py:16
  42.8 10.2 %collective-permute-start.17 = (f32[2,40,256]{2,1,0:T(8,128)S(1)}, f32[2,40,256]{2,1,0:T(8,128)S(1)}, u32[]{:S(2)}, u32[]{:S(2)}) collective-permute-start(f32[2,40,256]{2,1,0:T(8,128)S(1)} %pad_maximum_fusion.3), channel_id=1, source_target_pairs={{0,2},{1,3},{2,0},{3,1},{4,6},{5,7},{6,4},{7,5},{8,10},{9,11},{10,... | collective-permute-start | bytes 245768 | tf_op jit(solution)/shard_map/ppermute | solution.py:16
  44.2 9.4 %collective-permute-start.6 = (f32[64,512]{1,0:T(8,128)S(1)}, f32[64,512]{1,0:T(8,128)S(1)}, u32[]{:S(2)}, u32[]{:S(2)}) collective-permute-start(f32[64,512]{1,0:T(8,128)S(1)} %add.41.refs_0_), channel_id=1, source_target_pairs={{0,8},{8,0},{16,24},{24,16},{1,9},{9,1},{17,25},{25,17},{2,10},{10... | collective-permute-start | bytes 393224 | tf_op jit(solution)/shard_map/ppermute | solution.py:16
  50.2 7.5 %collective-permute-start.22 = (f32[64,640]{1,0:T(8,128)S(1)}, f32[64,640]{1,0:T(8,128)S(1)}, u32[]{:S(2)}, u32[]{:S(2)}) collective-permute-start(f32[64,640]{1,0:T(8,128)S(1)} %get-tuple-element.48), channel_id=1, source_target_pairs={{0,2},{1,3},{2,0},{3,1},{4,6},{5,7},{6,4},{7,5},{8,10},{9,11},{10,... | collective-permute-start | bytes 491528 | tf_op jit(solution)/shard_map/ppermute | solution.py:16
  51.5 7.1 %collective-permute-start.24 = (f32[64,640]{1,0:T(8,128)S(1)}, f32[64,640]{1,0:T(8,128)S(1)}, u32[]{:S(2)}, u32[]{:S(2)}) collective-permute-start(f32[64,640]{1,0:T(8,128)S(1)} %get-tuple-element.49), channel_id=1, source_target_pairs={{0,4},{1,5},{2,6},{3,7},{4,0},{5,1},{6,2},{7,3},{8,12},{9,13},{10,... | collective-permute-start | bytes 491528 | tf_op jit(solution)/shard_map/ppermute | solution.py:16
  53.0 16.6 %collective-permute-start.18 = (f32[4,40,256]{2,1,0:T(8,128)S(1)}, f32[4,40,256]{2,1,0:T(8,128)S(1)}, u32[]{:S(2)}, u32[]{:S(2)}) collective-permute-start(f32[4,40,256]{2,1,0:T(8,128)S(1)} %pad_maximum_fusion.2), channel_id=1, source_target_pairs={{0,4},{1,5},{2,6},{3,7},{4,0},{5,1},{6,2},{7,3},{8,12},{9,13},{10,... | collective-permute-start | bytes 491528 | tf_op jit(solution)/shard_map/ppermute | solution.py:16
  55.4 6.7 %collective-permute-start.11 = (f32[64,640]{1,0:T(8,128)S(1)}, f32[64,640]{1,0:T(8,128)S(1)}, u32[]{:S(2)}, u32[]{:S(2)}) collective-permute-start(f32[64,640]{1,0:T(8,128)S(1)} %get-tuple-element.38), channel_id=1, source_target_pairs={{0,2},{1,3},{2,0},{3,1},{4,6},{5,7},{6,4},{7,5},{8,10},{9,11},{10,... | collective-permute-start | bytes 491528 | tf_op jit(solution)/shard_map/ppermute | solution.py:16
  56.2 7.9 %collective-permute-start.13 = (f32[64,640]{1,0:T(8,128)S(1)}, f32[64,640]{1,0:T(8,128)S(1)}, u32[]{:S(2)}, u32[]{:S(2)}) collective-permute-start(f32[64,640]{1,0:T(8,128)S(1)} %get-tuple-element.39), channel_id=1, source_target_pairs={{0,4},{1,5},{2,6},{3,7},{4,0},{5,1},{6,2},{7,3},{8,12},{9,13},{10,... | collective-permute-start | bytes 491528 | tf_op jit(solution)/shard_map/ppermute | solution.py:16
  57.7 8.2 %collective-permute-start.23 = (f32[64,640]{1,0:T(8,128)S(1)}, f32[64,640]{1,0:T(8,128)S(1)}, u32[]{:S(2)}, u32[]{:S(2)}) collective-permute-start(f32[64,640]{1,0:T(8,128)S(1)} %add.48), channel_id=1, source_target_pairs={{0,4},{1,5},{2,6},{3,7},{4,0},{5,1},{6,2},{7,3},{8,12},{9,13},{10,... | collective-permute-start | bytes 491528 | tf_op jit(solution)/shard_map/ppermute | solution.py:16
  58.6 12.2 %copy-start.2 = (f32[1,1,2048,256]{3,2,1,0:T(8,128)S(1)}, f32[1,1,2048,256]{3,2,1,0:T(8,128)}, u32[]{:S(2)}) copy-start(f32[1,1,2048,256]{3,2,1,0:T(8,128)} %param.12) | copy-start | bytes 6291460
  58.6 7.3 %collective-permute-start.25 = (f32[64,640]{1,0:T(8,128)S(1)}, f32[64,640]{1,0:T(8,128)S(1)}, u32[]{:S(2)}, u32[]{:S(2)}) collective-permute-start(f32[64,640]{1,0:T(8,128)S(1)} %add.50), channel_id=1, source_target_pairs={{0,2},{1,3},{2,0},{3,1},{4,6},{5,7},{6,4},{7,5},{8,10},{9,11},{10,... | collective-permute-start | bytes 491528 | tf_op jit(solution)/shard_map/ppermute | solution.py:16
  62.1 5.6 %collective-permute-start.12 = (f32[64,640]{1,0:T(8,128)S(1)}, f32[64,640]{1,0:T(8,128)S(1)}, u32[]{:S(2)}, u32[]{:S(2)}) collective-permute-start(f32[64,640]{1,0:T(8,128)S(1)} %add.42), channel_id=1, source_target_pairs={{0,4},{1,5},{2,6},{3,7},{4,0},{5,1},{6,2},{7,3},{8,12},{9,13},{10,... | collective-permute-start | bytes 491528 | tf_op jit(solution)/shard_map/ppermute | solution.py:16
  64.2 5.4 %collective-permute-start.14 = (f32[64,640]{1,0:T(8,128)S(1)}, f32[64,640]{1,0:T(8,128)S(1)}, u32[]{:S(2)}, u32[]{:S(2)}) collective-permute-start(f32[64,640]{1,0:T(8,128)S(1)} %add.44), channel_id=1, source_target_pairs={{0,2},{1,3},{2,0},{3,1},{4,6},{5,7},{6,4},{7,5},{8,10},{9,11},{10,... | collective-permute-start | bytes 491528 | tf_op jit(solution)/shard_map/ppermute | solution.py:16
  65.9 4.9 %copy-start = (f32[1,1,2048,512]{3,2,1,0:T(8,128)S(1)}, f32[1,1,2048,512]{3,2,1,0:T(8,128)}, u32[]{:S(2)}) copy-start(f32[1,1,2048,512]{3,2,1,0:T(8,128)} %param.13) | copy-start | bytes 12582916
  66.0 3.9 %copy-start.4 = (s32[1,1,512]{2,1,0:T(1,128)S(1)}, s32[1,1,512]{2,1,0:T(1,128)}, u32[]{:S(2)}) copy-start(s32[1,1,512]{2,1,0:T(1,128)} %param.11) | copy-start | bytes 6148
  66.0 4.8 %collective-permute-start.26 = (f32[64,1280]{1,0:T(8,128)S(1)}, f32[64,1280]{1,0:T(8,128)S(1)}, u32[]{:S(2)}, u32[]{:S(2)}) collective-permute-start(f32[64,1280]{1,0:T(8,128)S(1)} %pad_maximum_fusion.1.own_ref), channel_id=1, source_target_pairs={{0,1},{1,0},{2,3},{3,2},{4,5},{5,4},{6,7},{7,6},{8,9},{9,8},{10,11... | collective-permute-start | bytes 983048 | tf_op jit(solution)/shard_map/ppermute | solution.py:16
  69.6 6.7 %collective-permute-start.15 = (f32[64,1280]{1,0:T(8,128)S(1)}, f32[64,1280]{1,0:T(8,128)S(1)}, u32[]{:S(2)}, u32[]{:S(2)}) collective-permute-start(f32[64,1280]{1,0:T(8,128)S(1)} %pad_maximum_fusion.own_ref), channel_id=1, source_target_pairs={{0,1},{1,0},{2,3},{3,2},{4,5},{5,4},{6,7},{7,6},{8,9},{9,8},{10,11... | collective-permute-start | bytes 983048 | tf_op jit(solution)/shard_map/ppermute | solution.py:16

commit v3 on v2

--- a/solution.py
+++ b/solution.py
@@ -163,92 +163,90 @@
         row = lax.broadcasted_iota(jnp.int32, (modes + seps, block), 0)
         for f in range(fanout):
             p_ref[:, f * block : (f + 1) * block] = jnp.where(row == place[f : f + 1], 1.0, 0.0).astype(BF16)
-        which = lax.broadcasted_iota(jnp.int32, (cands, count), 0)
-        q_ref[...] = jnp.where(which == anc_ref[...], 1.0, 0.0).astype(BF16)
-
-    return call(body, [shape((modes + seps, rows), BF16), shape((cands, count), BF16)], tags, anc)
-
-
-def expand(nblocks, own, other, coup, p, q, leaf, cons, part, parts, block, prior):
+        which = lax.broadcasted_iota(jnp.int32, (count, cands), 1)
+        wanted = jnp.broadcast_to(anc_ref[...], (8, count)).astype(F32).T[:, :1].astype(jnp.int32)
+        q_ref[...] = jnp.where(which == wanted, 1.0, 0.0).astype(BF16)
+
+    return call(body, [shape((modes + seps, rows), BF16), shape((count, cands), BF16)], tags, anc)
+
+
+def expand(nblocks, own, other, coup, p, q, leaf, cons, part, parts, sep_local, prior):
     n, wide = own.shape
     rows = p.shape[1]
-    modes = leaf.shape[1]
+    inter, modes = leaf.shape
     seps = p.shape[0] - modes
     count = cons.shape[1]
-    inter = leaf.shape[0]
-    sep_local = block
     nv = 2 * n
     tile = 256
     low = n * parts // nblocks
 
     def body(own_ref, other_ref, ch, cl, p_ref, q_ref, l_ref, c_ref, *rest):
-        (sep_ref, out_ref, f_ref, dh, dl) = rest[len(prior) :]
-
-        @pl.when(pl.program_id(0) == 0)
-        def _():
-            parity = jnp.bitwise_and(lax.axis_index("col"), 1)
-            for i in range(n // low):
-                s = slice(i * low, (i + 1) * low)
-                a = pl.multiple_of(2 * i * low + parity * low, 8)
-                b = pl.multiple_of(2 * i * low + (1 - parity) * low, 8)
-                f_ref[pl.ds(a, low)] = own_ref[s]
-                f_ref[pl.ds(b, low)] = other_ref[s]
-            fh, fl = cut(f_ref[...])
-            both = jnp.concatenate([fh, fl], axis=0)
-            got = dot(both[:, :rows], p_ref[...], NT)
-            th, tl = fh[:, rows:], fl[:, rows:]
-            raw = got[:nv, modes:] + got[nv:, modes:]
-            sep = raw + three(th, tl, ch[...], cl[...], NT)
-            sh, sl = cut(sep)
-            cand = jnp.concatenate(
-                [jnp.concatenate([th, sh], axis=1), jnp.concatenate([tl, sl], axis=1)], axis=0
-            )
-            found = dot(cand, q_ref[...], NN)
-            dh[:, :modes] = got[:, :modes].astype(BF16)
-            dh[:, modes:] = found.astype(BF16)
-            dl[...] = sep.T
-            mine = pl.multiple_of(lax.axis_index("col") * sep_local, 8)
-            sep_ref[...] = dl[pl.ds(mine, sep_local)]
-
-        lh, ll = cut(l_ref[...])
-        kh, kl = cut(c_ref[...])
-        wh = jnp.concatenate([lh, kh], axis=1)
-        wl = jnp.concatenate([ll, kl], axis=1)
-        d = dh[...]
-        y = dot(wh, d, NT)
-        out_ref[...] = y[:, :nv] + y[:, nv:] + dot(wl, d[:nv], NT)
-
-    full = lambda a: pl.BlockSpec(a.shape, lambda i: (0,) * a.ndim)
-    args = [own, other, *coup, p, q]
+        sep_out, out, f_ref, d_ref, s_ref, y_ref, e_ref, sems = rest[len(prior) :]
+        lanes = pl.ds(part * nv, nv)
+        parity = jnp.bitwise_and(lax.axis_index("col"), 1)
+        for i in range(n // low):
+            s = slice(i * low, (i + 1) * low)
+            a = pl.multiple_of(2 * i * low + parity * low, 8)
+            b = pl.multiple_of(2 * i * low + (1 - parity) * low, 8)
+            f_ref[pl.ds(a, low)] = own_ref[s]
+            f_ref[pl.ds(b, low)] = other_ref[s]
+        both = jnp.concatenate(cut(f_ref[:, :rows]), axis=0)
+        got = dot(p_ref[...], both, NT)
+        d_ref[:modes] = got[:modes].astype(BF16)
+        raw = got[modes:, :nv] + got[modes:, nv:]
+        th, tl = cut(f_ref[:, rows:].T)
+        sep = raw + three(ch[...], cl[...], th, tl, NN)
+        s_ref[...] = sep
+        tops = jnp.concatenate([th, tl], axis=1)
+        cand = jnp.concatenate([tops, jnp.concatenate(cut(sep), axis=1)], axis=0)
+        d_ref[modes:] = dot(q_ref[...], cand, NN).astype(BF16)
+        mine = pl.multiple_of(lax.axis_index("col") * sep_local, 8)
+        e_ref[...] = s_ref[pl.ds(mine, sep_local)]
+
+        def put(i):
+            t = pl.ds(i * tile, tile)
+            return pltpu.make_async_copy(y_ref.at[t], out.at[t, lanes], sems.at[i])
+
+        sep_copy = pltpu.make_async_copy(e_ref, sep_out.at[:, lanes], sems.at[tiles])
+        for i in range(tiles):
+            t = slice(i * tile, (i + 1) * tile)
+            lh, ll = cut(l_ref[t])
+            kh, kl = cut(c_ref[t])
+            y = dot(lh, d_ref[:modes], NN) + dot(kh, d_ref[modes:], NN)
+            z = dot(ll, d_ref[:modes, :nv], NN) + dot(kl, d_ref[modes:, :nv], NN)
+            y_ref[t] = y[:, :nv] + y[:, nv:] + z
+            (sep_copy if i == 0 else put(i - 1)).start()
+        put(tiles - 1).start()
+        sep_copy.wait()
+        for i in range(tiles):
+            put(i).wait()
+
+    args = [own, other, *coup, p, q, leaf, cons]
+    tiles = inter // tile
     return pl.pallas_call(
         body,
-        grid=(inter // tile,),
         out_shape=[shape((sep_local, nv * parts)), shape((inter, nv * parts))],
-        in_specs=[full(a) for a in args]
-        + [
-            pl.BlockSpec((tile, modes), lambda i: (i, 0)),
-            pl.BlockSpec((tile, count), lambda i: (i, 0)),
-        ]
+        in_specs=[pl.BlockSpec(memory_space=pltpu.VMEM)] * len(args)
         + [pl.BlockSpec(memory_space=pl.ANY)] * len(prior),
-        out_specs=[
-            pl.BlockSpec((sep_local, nv), lambda i: (0, part)),
-            pl.BlockSpec((tile, nv), lambda i: (i, part)),
-        ],
+        out_specs=[pl.BlockSpec(memory_space=pl.ANY)] * 2,
         scratch_shapes=[
             pltpu.VMEM((nv, wide), F32),
-            pltpu.VMEM((2 * nv, modes + count), BF16),
+            pltpu.VMEM((modes + count, 2 * nv), BF16),
             pltpu.VMEM((seps, nv), F32),
+            pltpu.VMEM((inter, nv), F32),
+            pltpu.VMEM((sep_local, nv), F32),
+            pltpu.SemaphoreType.DMA((tiles + 1,)),
         ],
         input_output_aliases={8 + i: i for i in range(len(prior))},
         compiler_params=pltpu.CompilerParams(
-            vmem_limit_bytes=4 * sum(a.size * a.dtype.itemsize for a in args) + (8 << 20)
+            vmem_limit_bytes=sum(a.size * a.dtype.itemsize for a in args) + (8 << 20)
         ),
         cost_estimate=pl.CostEstimate(
             flops=12 * inter * (modes + count) * nv,
             bytes_accessed=4 * inter * (modes + count + nv),
             transcendentals=0,
         ),
-    )(*args, leaf, cons, *prior)
+    )(*args, *prior)
 
 
 def spans(masks):

time: 81.9 us -> 78.3 us (0.956)
  Pallas kernels: 17.9 us -> 14.2 us
    pallas_call x2, Pallas kernels: 10.9 us -> 7.36 us  [expand(): pl.pallas_call(body, out_shape=[shape((sep_local, nv * parts)), shape((in...]
  transfers between devices with their start and end apart: 27 -> 27, of which waited for: 14 -> 14; matrix products, arithmetic and copies ran while one was open for 2% -> 2% of each run, Pallas kernels for 15% -> 14%
where the time goes in v3:
time: 78.3 us; the launch traced here: 78.1 us
  starting transfers between devices  30.1 us (38%)
  waiting for transfers between devices  29.8 us (38%)
  Pallas kernels  14.2 us (18%)
  local copies, waits for them, and re-layouts  2.6 us (3%)
  between operations  1.04 us (1%)
    ppermute x27, starting transfers between devices, swap(): return lax.ppermute(v, axis, [(i, i ^ mask) for i in range(n)])  30.1 us
    ppermute x27, waiting for transfers between devices, swap(): return lax.ppermute(v, axis, [(i, i ^ mask) for i in range(n)])  29.8 us
    pallas_call x2, Pallas kernels, expand(): pl.pallas_call(body, out_shape=[shape((sep_local, nv * parts)), shape((in...  7.36 us
    pallas_call x12, Pallas kernels, call(): pl.pallas_call(body, out_shape=out, in_specs=specs, out_specs=[pl.BlockSp...  6.88 us
    unnamed x15, local copies, waits for them, and re-layouts  1.63 us
  transfers between devices with their start and end apart: 27, of which 14 were waited for; matrix products, arithmetic and copies ran while one was open for 2% of the time, Pallas kernels for 14%

profile of v3, /device:TPU:0, one launch (start us, length us, event | category | flops | bytes accessed | tf_op | source)
XLA Modules:
  0.0 78.1 jit_solution(17344075890328363146)
XLA Ops:
  0.6 0.6 collective-permute-start.3
  1.2 0.9 %slice_bitcast_fusion.refs_0_ = f32[64,512]{1,0:T(8,128)S(1)} fusion(f32[8,128,512]{2,1,0:T(8,128)} %bitcast.35), kind=kLoop, calls=%fused_computation.3 | loop fusion | bytes 262144 | tf_op jit(solution)/shard_map/reshape | solution.py:276
  2.1 4.7 %collective-permute-start.9 = (f32[64,512]{1,0:T(8,128)S(1)}, f32[64,512]{1,0:T(8,128)S(1)}, u32[]{:S(2)}, u32[]{:S(2)}) collective-permute-start(f32[64,512]{1,0:T(8,128)S(1)} %slice_bitcast_fusion.refs_0_), channel_id=1, source_target_pairs={{0,24},{8,16},{16,8},{24,0},{1,25},{9,17},{17,9},{25,1},{2,26},{10... | collective-permute-start | bytes 393224 | tf_op jit(solution)/shard_map/ppermute | solution.py:16
  6.8 0.6 collective-permute-start.7
  7.4 2.6 %collective-permute-start.2 = (f32[32,1024]{1,0:T(8,128)}, f32[32,1024]{1,0:T(8,128)S(1)}, u32[]{:S(2)}, u32[]{:S(2)}) collective-permute-start(f32[32,1024]{1,0:T(8,128)} %bitcast.41), channel_id=1, source_target_pairs={{0,6},{1,7},{2,4},{3,5},{4,2},{5,3},{6,0},{7,1},{8,14},{9,15},{10,... | collective-permute-start | bytes 393224 | tf_op jit(solution)/shard_map/ppermute | solution.py:16
  10.0 1.2 %collective-permute-done.9.refs_3_ = f32[64,512]{1,0:T(8,128)S(1)} collective-permute-done((f32[64,512]{1,0:T(8,128)S(1)}, f32[64,512]{1,0:T(8,128)S(1)}, u32[]{:S(2)}, u32[]{:S(2)}) %collective-permute-start.9) | collective-permute-done | bytes 131104 | tf_op jit(solution)/shard_map/ppermute | solution.py:16
  11.2 1.7 %collective-permute-start.1 = (f32[32,1024]{1,0:T(8,128)}, f32[32,1024]{1,0:T(8,128)S(1)}, u32[]{:S(2)}, u32[]{:S(2)}) collective-permute-start(f32[32,1024]{1,0:T(8,128)} %bitcast.42), channel_id=1, source_target_pairs={{0,4},{1,5},{2,6},{3,7},{4,0},{5,1},{6,2},{7,3},{8,12},{9,13},{10,... | collective-permute-start | bytes 393224 | tf_op jit(solution)/shard_map/ppermute | solution.py:16
  13.0 5.5 %collective-permute-done.8.refs_2_ = f32[64,512]{1,0:T(8,128)S(1)} collective-permute-done((f32[64,512]{1,0:T(8,128)S(1)}, f32[64,512]{1,0:T(8,128)S(1)}, u32[]{:S(2)}, u32[]{:S(2)}) %collective-permute-start.8) | collective-permute-done | bytes 131104 | tf_op jit(solution)/shard_map/ppermute | solution.py:16
  18.5 1.5 %collective-permute-start = (f32[32,1024]{1,0:T(8,128)}, f32[32,1024]{1,0:T(8,128)S(1)}, u32[]{:S(2)}, u32[]{:S(2)}) collective-permute-start(f32[32,1024]{1,0:T(8,128)} %bitcast.43), channel_id=1, source_target_pairs={{0,2},{1,3},{2,0},{3,1},{4,6},{5,7},{6,4},{7,5},{8,10},{9,11},{10,... | collective-permute-start | bytes 393224 | tf_op jit(solution)/shard_map/ppermute | solution.py:16
  20.0 1.6 %copy-done.1 = f32[1024,512]{1,0:T(8,128)S(1)} copy-done((f32[1024,512]{1,0:T(8,128)S(1)}, f32[1024,512]{1,0:T(8,128)}, u32[]{:S(2)}) %copy-start.1) | copy-done | bytes 2097176
  21.6 0.4 shard_map.86
  22.0 0.1 collective-permute-start.10
  22.1 0.4 shard_map.87
  22.5 1.2 %collective-permute-done.refs_1_ = f32[32,1024]{1,0:T(8,128)S(1)} collective-permute-done((f32[32,1024]{1,0:T(8,128)}, f32[32,1024]{1,0:T(8,128)S(1)}, u32[]{:S(2)}, u32[]{:S(2)}) %collective-permute-start) | collective-permute-done | bytes 131104 | tf_op jit(solution)/shard_map/ppermute | solution.py:16
  23.8 0.8 %shard_map.88 = (f32[64,512]{1,0:T(8,128)S(1)}, f32[64,512]{1,0:T(8,128)S(1)}) custom-call(f32[32,1024]{1,0:T(8,128)S(1)} %bitcast.44, f32[32,1024]{1,0:T(8,128)S(1)} %collective-permute-done.refs_1_, f32[32,1024]{1,0:T(8,128)S(1)} %collective-permute-done.1.refs_2_, f32[32,1024]{1,0:T(8,128)S(1)} %collective-permute-done.2.refs_3_, ...), custom_call_target="tpu_custom_call" | custom-call | flops 402653184 | bytes 4980736 | tf_op jit(solution)/shard_map/pallas_call | solution.py:24
  24.6 0.8 %shard_map.96 = (f32[64,512]{1,0:T(8,128)S(1)}, f32[64,512]{1,0:T(8,128)S(1)}) custom-call(f32[32,1024]{1,0:T(8,128)S(1)} %bitcast.45, f32[32,1024]{1,0:T(8,128)S(1)} %collective-permute-done.refs_1_, f32[32,1024]{1,0:T(8,128)S(1)} %collective-permute-done.1.refs_2_, f32[32,1024]{1,0:T(8,128)S(1)} %collective-permute-done.2.refs_3_, ...), custom_call_target="tpu_custom_call" | custom-call | flops 402653184 | bytes 4980736 | tf_op jit(solution)/shard_map/pallas_call | solution.py:24
  25.5 2.0 %collective-permute-start.4 = (f32[64,512]{1,0:T(8,128)S(1)}, f32[64,512]{1,0:T(8,128)S(1)}, u32[]{:S(2)}, u32[]{:S(2)}) collective-permute-start(f32[64,512]{1,0:T(8,128)S(1)} %get-tuple-element.33), channel_id=1, source_target_pairs={{0,8},{8,0},{16,24},{24,16},{1,9},{9,1},{17,25},{25,17},{2,10},{10... | collective-permute-start | bytes 393224 | tf_op jit(solution)/shard_map/ppermute | solution.py:16
  27.5 4.0 %collective-permute-done.19 = f32[64,512]{1,0:T(8,128)S(1)} collective-permute-done((f32[64,512]{1,0:T(8,128)S(1)}, f32[64,512]{1,0:T(8,128)S(1)}, u32[]{:S(2)}, u32[]{:S(2)}) %collective-permute-start.19) | collective-permute-done | bytes 131104 | tf_op jit(solution)/shard_map/ppermute | solution.py:16
  31.5 1.3 %collective-permute-start.20 = (f32[64,512]{1,0:T(8,128)S(1)}, f32[64,512]{1,0:T(8,128)S(1)}, u32[]{:S(2)}, u32[]{:S(2)}) collective-permute-start(f32[64,512]{1,0:T(8,128)S(1)} %add.46), channel_id=1, source_target_pairs={{0,16},{8,24},{16,0},{24,8},{1,17},{9,25},{17,1},{25,9},{2,18},{10... | collective-permute-start | bytes 393224 | tf_op jit(solution)/shard_map/ppermute | solution.py:16
  32.9 1.0 %collective-permute-done.4 = f32[64,512]{1,0:T(8,128)S(1)} collective-permute-done((f32[64,512]{1,0:T(8,128)S(1)}, f32[64,512]{1,0:T(8,128)S(1)}, u32[]{:S(2)}, u32[]{:S(2)}) %collective-permute-start.4) | collective-permute-done | bytes 131104 | tf_op jit(solution)/shard_map/ppermute | solution.py:16
  34.0 1.7 %collective-permute-start.5 = (f32[64,512]{1,0:T(8,128)S(1)}, f32[64,512]{1,0:T(8,128)S(1)}, u32[]{:S(2)}, u32[]{:S(2)}) collective-permute-start(f32[64,512]{1,0:T(8,128)S(1)} %add.40), channel_id=1, source_target_pairs={{0,16},{8,24},{16,0},{24,8},{1,17},{9,25},{17,1},{25,9},{2,18},{10... | collective-permute-start | bytes 393224 | tf_op jit(solution)/shard_map/ppermute | solution.py:16
  35.7 7.0 %collective-permute-done.20 = f32[64,512]{1,0:T(8,128)S(1)} collective-permute-done((f32[64,512]{1,0:T(8,128)S(1)}, f32[64,512]{1,0:T(8,128)S(1)}, u32[]{:S(2)}, u32[]{:S(2)}) %collective-permute-start.20) | collective-permute-done | bytes 131104 | tf_op jit(solution)/shard_map/ppermute | solution.py:16
  42.7 0.1 collective-permute-start.21
  42.8 1.1 %collective-permute-start.17 = (f32[2,40,256]{2,1,0:T(8,128)S(1)}, f32[2,40,256]{2,1,0:T(8,128)S(1)}, u32[]{:S(2)}, u32[]{:S(2)}) collective-permute-start(f32[2,40,256]{2,1,0:T(8,128)S(1)} %pad_maximum_fusion.3), channel_id=1, source_target_pairs={{0,2},{1,3},{2,0},{3,1},{4,6},{5,7},{6,4},{7,5},{8,10},{9,11},{10,... | collective-permute-start | bytes 245768 | tf_op jit(solution)/shard_map/ppermute | solution.py:16
  43.9 0.1 shard_map.90
  44.0 0.1 shard_map.91
  44.2 1.9 %collective-permute-start.6 = (f32[64,512]{1,0:T(8,128)S(1)}, f32[64,512]{1,0:T(8,128)S(1)}, u32[]{:S(2)}, u32[]{:S(2)}) collective-permute-start(f32[64,512]{1,0:T(8,128)S(1)} %add.41.refs_0_), channel_id=1, source_target_pairs={{0,8},{8,0},{16,24},{24,16},{1,9},{9,1},{17,25},{25,17},{2,10},{10... | collective-permute-start | bytes 393224 | tf_op jit(solution)/shard_map/ppermute | solution.py:16
  46.1 2.4 %collective-permute-done.21.refs_1_ = f32[64,512]{1,0:T(8,128)S(1)} collective-permute-done((f32[64,512]{1,0:T(8,128)S(1)}, f32[64,512]{1,0:T(8,128)S(1)}, u32[]{:S(2)}, u32[]{:S(2)}) %collective-permute-start.21) | collective-permute-done | bytes 131104 | tf_op jit(solution)/shard_map/ppermute | solution.py:16
  48.5 1.7 %shard_map.97 = (f32[64,640]{1,0:T(8,128)S(1)}, f32[64,640]{1,0:T(8,128)S(1)}) custom-call(f32[64,512]{1,0:T(8,128)S(1)} %add.47.refs_0_, f32[64,512]{1,0:T(8,128)S(1)} %collective-permute-done.21.refs_1_, bf16[1024,512]{1,0:T(8,128)(2,1)S(1)} %get-tuple-element.28.refs_4_.refs_2_, bf16[1024,512]{1,0:T(8,128)(2,1)S(1)} %get-tuple-element.29.refs_5_.refs_3_, ...), custom_call_target="tpu_custom_call" | custom-call | flops 503316480 | bytes 5832704 | tf_op jit(solution)/shard_map/pallas_call | solution.py:24
  50.2 1.3 %collective-permute-start.22 = (f32[64,640]{1,0:T(8,128)S(1)}, f32[64,640]{1,0:T(8,128)S(1)}, u32[]{:S(2)}, u32[]{:S(2)}) collective-permute-start(f32[64,640]{1,0:T(8,128)S(1)} %get-tuple-element.48), channel_id=1, source_target_pairs={{0,2},{1,3},{2,0},{3,1},{4,6},{5,7},{6,4},{7,5},{8,10},{9,11},{10,... | collective-permute-start | bytes 491528 | tf_op jit(solution)/shard_map/ppermute | solution.py:16
  51.5 1.5 %collective-permute-start.24 = (f32[64,640]{1,0:T(8,128)S(1)}, f32[64,640]{1,0:T(8,128)S(1)}, u32[]{:S(2)}, u32[]{:S(2)}) collective-permute-start(f32[64,640]{1,0:T(8,128)S(1)} %get-tuple-element.49), channel_id=1, source_target_pairs={{0,4},{1,5},{2,6},{3,7},{4,0},{5,1},{6,2},{7,3},{8,12},{9,13},{10,... | collective-permute-start | bytes 491528 | tf_op jit(solution)/shard_map/ppermute | solution.py:16
  53.0 0.6 collective-permute-start.18
  53.6 1.7 %shard_map.92 = (f32[64,640]{1,0:T(8,128)S(1)}, f32[64,640]{1,0:T(8,128)S(1)}) custom-call(f32[64,512]{1,0:T(8,128)S(1)} %add.41.refs_0_, f32[64,512]{1,0:T(8,128)S(1)} %collective-permute-done.6.refs_1_, bf16[1024,512]{1,0:T(8,128)(2,1)S(1)} %get-tuple-element.28.refs_4_.refs_2_, bf16[1024,512]{1,0:T(8,128)(2,1)S(1)} %get-tuple-element.29.refs_5_.refs_3_, ...), custom_call_target="tpu_custom_call" | custom-call | flops 503316480 | bytes 5832704 | tf_op jit(solution)/shard_map/pallas_call | solution.py:24
  55.4 0.8 %collective-permute-start.11 = (f32[64,640]{1,0:T(8,128)S(1)}, f32[64,640]{1,0:T(8,128)S(1)}, u32[]{:S(2)}, u32[]{:S(2)}) collective-permute-start(f32[64,640]{1,0:T(8,128)S(1)} %get-tuple-element.38), channel_id=1, source_target_pairs={{0,2},{1,3},{2,0},{3,1},{4,6},{5,7},{6,4},{7,5},{8,10},{9,11},{10,... | collective-permute-start | bytes 491528 | tf_op jit(solution)/shard_map/ppermute | solution.py:16
  56.2 1.5 %collective-permute-start.13 = (f32[64,640]{1,0:T(8,128)S(1)}, f32[64,640]{1,0:T(8,128)S(1)}, u32[]{:S(2)}, u32[]{:S(2)}) collective-permute-start(f32[64,640]{1,0:T(8,128)S(1)} %get-tuple-element.39), channel_id=1, source_target_pairs={{0,4},{1,5},{2,6},{3,7},{4,0},{5,1},{6,2},{7,3},{8,12},{9,13},{10,... | collective-permute-start | bytes 491528 | tf_op jit(solution)/shard_map/ppermute | solution.py:16
  57.7 0.6 collective-permute-start.23
  58.3 0.3 collective-permute-done.24
  58.6 1.7 %collective-permute-start.25 = (f32[64,640]{1,0:T(8,128)S(1)}, f32[64,640]{1,0:T(8,128)S(1)}, u32[]{:S(2)}, u32[]{:S(2)}) collective-permute-start(f32[64,640]{1,0:T(8,128)S(1)} %add.50), channel_id=1, source_target_pairs={{0,2},{1,3},{2,0},{3,1},{4,6},{5,7},{6,4},{7,5},{8,10},{9,11},{10,... | collective-permute-start | bytes 491528 | tf_op jit(solution)/shard_map/ppermute | solution.py:16
  60.3 1.8 %collective-permute-done.11 = f32[64,640]{1,0:T(8,128)S(1)} collective-permute-done((f32[64,640]{1,0:T(8,128)S(1)}, f32[64,640]{1,0:T(8,128)S(1)}, u32[]{:S(2)}, u32[]{:S(2)}) %collective-permute-start.11) | collective-permute-done | bytes 163872 | tf_op jit(solution)/shard_map/ppermute | solution.py:16
  62.1 1.4 %collective-permute-start.12 = (f32[64,640]{1,0:T(8,128)S(1)}, f32[64,640]{1,0:T(8,128)S(1)}, u32[]{:S(2)}, u32[]{:S(2)}) collective-permute-start(f32[64,640]{1,0:T(8,128)S(1)} %add.42), channel_id=1, source_target_pairs={{0,4},{1,5},{2,6},{3,7},{4,0},{5,1},{6,2},{7,3},{8,12},{9,13},{10,... | collective-permute-start | bytes 491528 | tf_op jit(solution)/shard_map/ppermute | solution.py:16
  63.5 0.6 collective-permute-done.13
  64.2 0.5 collective-permute-start.14
  64.7 1.2 %collective-permute-done.23 = f32[64,640]{1,0:T(8,128)S(1)} collective-permute-done((f32[64,640]{1,0:T(8,128)S(1)}, f32[64,640]{1,0:T(8,128)S(1)}, u32[]{:S(2)}, u32[]{:S(2)}) %collective-permute-start.23) | collective-permute-done | bytes 163872 | tf_op jit(solution)/shard_map/ppermute | solution.py:16
  66.1 1.6 %collective-permute-done.12 = f32[64,640]{1,0:T(8,128)S(1)} collective-permute-done((f32[64,640]{1,0:T(8,128)S(1)}, f32[64,640]{1,0:T(8,128)S(1)}, u32[]{:S(2)}, u32[]{:S(2)}) %collective-permute-start.12) | collective-permute-done | bytes 163872 | tf_op jit(solution)/shard_map/ppermute | solution.py:16
  67.7 1.9 %collective-permute-done.14 = f32[64,640]{1,0:T(8,128)S(1)} collective-permute-done((f32[64,640]{1,0:T(8,128)S(1)}, f32[64,640]{1,0:T(8,128)S(1)}, u32[]{:S(2)}, u32[]{:S(2)}) %collective-permute-start.14) | collective-permute-done | bytes 163872 | tf_op jit(solution)/shard_map/ppermute | solution.py:16
  69.9 0.8 %shard_map.95 = (bf16[512,1024]{1,0:T(8,128)(2,1)S(1)}, bf16[512,512]{1,0:T(8,128)(2,1)S(1)}) custom-call(f32[8,128]{1,0:T(8,128)S(1)} %slice.19.tag_ref, s32[1,512]{1,0:T(1,128)S(1)} %bitcast.47), custom_call_target="tpu_custom_call" | custom-call | bytes 1579008 | tf_op jit(solution)/shard_map/pallas_call | solution.py:24
  70.7 3.7 %shard_map.98 = (f32[32,256]{1,0:T(8,128)}, f32[2048,256]{1,0:T(8,128)}) custom-call(f32[64,1280]{1,0:T(8,128)S(1)} %pad_maximum_fusion.1.own_ref, f32[64,1280]{1,0:T(8,128)S(1)} %collective-permute-done.26.other_ref, bf16[256,256]{1,0:T(8,128)(2,1)S(1)} %get-tuple-element.42.ch, bf16[256,256]{1,0:T(8,128)(2,1)S(1)} %get-tuple-element.43.cl, ...), custom_call_target="tpu_custom_call" | custom-call | flops 2415919104 | bytes 7340032 | tf_op jit(solution)/shard_map/pallas_call | solution.py:226
  74.4 3.7 %shard_map.99 = (f32[32,256]{1,0:T(8,128)}, f32[2048,256]{1,0:T(8,128)}) custom-call(f32[64,1280]{1,0:T(8,128)S(1)} %pad_maximum_fusion.own_ref, f32[64,1280]{1,0:T(8,128)S(1)} %collective-permute-done.15.other_ref, bf16[256,256]{1,0:T(8,128)(2,1)S(1)} %get-tuple-element.42.ch, ...), custom_call_target="tpu_custom_call", output_to_operand_aliasing={{0}: (8, {}), {1}: (9, {})} | custom-call | flops 2415919104 | bytes 7340032 | tf_op jit(solution)/shard_map/pallas_call | solution.py:226
  (60 shorter events, 0.9 us)
Async XLA Ops:
  0.6 21.5 %collective-permute-start.3 = (f32[1024,512]{1,0:T(8,128)}, f32[1024,512]{1,0:T(8,128)S(1)}, u32[]{:S(2)}, u32[]{:S(2)}) collective-permute-start(f32[1024,512]{1,0:T(8,128)} %v_ref.1), channel_id=1, source_target_pairs={{0,1},{1,0},{2,3},{3,2},{4,5},{5,4},{6,7},{7,6},{8,9},{9,8},{10,11... | collective-permute-start | bytes 6291464 | tf_op jit(solution)/shard_map/ppermute | solution.py:16
  2.1 9.1 %collective-permute-start.9 = (f32[64,512]{1,0:T(8,128)S(1)}, f32[64,512]{1,0:T(8,128)S(1)}, u32[]{:S(2)}, u32[]{:S(2)}) collective-permute-start(f32[64,512]{1,0:T(8,128)S(1)} %slice_bitcast_fusion.refs_0_), channel_id=1, source_target_pairs={{0,24},{8,16},{16,8},{24,0},{1,25},{9,17},{17,9},{25,1},{2,26},{10... | collective-permute-start | bytes 393224 | tf_op jit(solution)/shard_map/ppermute | solution.py:16
  6.8 11.7 %collective-permute-start.8 = (f32[64,512]{1,0:T(8,128)S(1)}, f32[64,512]{1,0:T(8,128)S(1)}, u32[]{:S(2)}, u32[]{:S(2)}) collective-permute-start(f32[64,512]{1,0:T(8,128)S(1)} %slice_bitcast_fusion.refs_0_), channel_id=1, source_target_pairs={{0,16},{8,24},{16,0},{24,8},{1,17},{9,25},{17,1},{25,9},{2,18},{10... | collective-permute-start | bytes 393224 | tf_op jit(solution)/shard_map/ppermute | solution.py:16
  6.8 15.2 %collective-permute-start.7 = (f32[64,512]{1,0:T(8,128)S(1)}, f32[64,512]{1,0:T(8,128)S(1)}, u32[]{:S(2)}, u32[]{:S(2)}) collective-permute-start(f32[64,512]{1,0:T(8,128)S(1)} %slice_bitcast_fusion.refs_0_), channel_id=1, source_target_pairs={{0,8},{8,0},{16,24},{24,16},{1,9},{9,1},{17,25},{25,17},{2,10},{10... | collective-permute-start | bytes 393224 | tf_op jit(solution)/shard_map/ppermute | solution.py:16
  7.4 15.1 %collective-permute-start.2 = (f32[32,1024]{1,0:T(8,128)}, f32[32,1024]{1,0:T(8,128)S(1)}, u32[]{:S(2)}, u32[]{:S(2)}) collective-permute-start(f32[32,1024]{1,0:T(8,128)} %bitcast.41), channel_id=1, source_target_pairs={{0,6},{1,7},{2,4},{3,5},{4,2},{5,3},{6,0},{7,1},{8,14},{9,15},{10,... | collective-permute-start | bytes 393224 | tf_op jit(solution)/shard_map/ppermute | solution.py:16
  11.2 11.3 %collective-permute-start.1 = (f32[32,1024]{1,0:T(8,128)}, f32[32,1024]{1,0:T(8,128)S(1)}, u32[]{:S(2)}, u32[]{:S(2)}) collective-permute-start(f32[32,1024]{1,0:T(8,128)} %bitcast.42), channel_id=1, source_target_pairs={{0,4},{1,5},{2,6},{3,7},{4,0},{5,1},{6,2},{7,3},{8,12},{9,13},{10,... | collective-permute-start | bytes 393224 | tf_op jit(solution)/shard_map/ppermute | solution.py:16
  18.5 5.2 %collective-permute-start = (f32[32,1024]{1,0:T(8,128)}, f32[32,1024]{1,0:T(8,128)S(1)}, u32[]{:S(2)}, u32[]{:S(2)}) collective-permute-start(f32[32,1024]{1,0:T(8,128)} %bitcast.43), channel_id=1, source_target_pairs={{0,2},{1,3},{2,0},{3,1},{4,6},{5,7},{6,4},{7,5},{8,10},{9,11},{10,... | collective-permute-start | bytes 393224 | tf_op jit(solution)/shard_map/ppermute | solution.py:16
  20.0 1.6 %copy-start.1 = (f32[1024,512]{1,0:T(8,128)S(1)}, f32[1024,512]{1,0:T(8,128)}, u32[]{:S(2)}) copy-start(f32[1024,512]{1,0:T(8,128)} %v_ref.1) | copy-start | bytes 6291460
  22.0 1.8 %copy-start.3 = (f32[1024,32]{0,1:T(8,128)S(1)}, f32[1024,32]{0,1:T(8,128)}, u32[]{:S(2)}) copy-start(f32[1024,32]{0,1:T(8,128)} %param.8) | copy-start | bytes 393220
  22.0 22.0 %collective-permute-start.10 = (f32[256,512]{1,0:T(8,128)S(1)}, f32[256,512]{1,0:T(8,128)S(1)}, u32[]{:S(2)}, u32[]{:S(2)}) collective-permute-start(f32[256,512]{1,0:T(8,128)S(1)} %shard_map.89.v_ref), channel_id=1, source_target_pairs={{0,1},{1,0},{2,3},{3,2},{4,5},{5,4},{6,7},{7,6},{8,9},{9,8},{10,11... | collective-permute-start | bytes 1572872 | tf_op jit(solution)/shard_map/ppermute | solution.py:16
  24.6 2.9 %copy-start.6 = (s32[88,1]{0,1:T(1,128)S(1)}, s32[88,1]{0,1:T(1,128)}, u32[]{:S(2)}) copy-start(s32[88,1]{0,1:T(1,128)} %param.9) | copy-start | bytes 1060
  24.6 8.3 %copy-start.5 = (f32[1,32,256]{2,1,0:T(8,128)S(1)}, f32[1,32,256]{2,1,0:T(8,128)}, u32[]{:S(2)}) copy-start(f32[1,32,256]{2,1,0:T(8,128)} %param.10) | copy-start | bytes 98308
  25.4 6.1 %collective-permute-start.19 = (f32[64,512]{1,0:T(8,128)S(1)}, f32[64,512]{1,0:T(8,128)S(1)}, u32[]{:S(2)}, u32[]{:S(2)}) collective-permute-start(f32[64,512]{1,0:T(8,128)S(1)} %get-tuple-element.47), channel_id=1, source_target_pairs={{0,8},{8,0},{16,24},{24,16},{1,9},{9,1},{17,25},{25,17},{2,10},{10... | collective-permute-start | bytes 393224 | tf_op jit(solution)/shard_map/ppermute | solution.py:16
  25.5 8.5 %collective-permute-start.4 = (f32[64,512]{1,0:T(8,128)S(1)}, f32[64,512]{1,0:T(8,128)S(1)}, u32[]{:S(2)}, u32[]{:S(2)}) collective-permute-start(f32[64,512]{1,0:T(8,128)S(1)} %get-tuple-element.33), channel_id=1, source_target_pairs={{0,8},{8,0},{16,24},{24,16},{1,9},{9,1},{17,25},{25,17},{2,10},{10... | collective-permute-start | bytes 393224 | tf_op jit(solution)/shard_map/ppermute | solution.py:16
  31.5 11.1 %collective-permute-start.20 = (f32[64,512]{1,0:T(8,128)S(1)}, f32[64,512]{1,0:T(8,128)S(1)}, u32[]{:S(2)}, u32[]{:S(2)}) collective-permute-start(f32[64,512]{1,0:T(8,128)S(1)} %add.46), channel_id=1, source_target_pairs={{0,16},{8,24},{16,0},{24,8},{1,17},{9,25},{17,1},{25,9},{2,18},{10... | collective-permute-start | bytes 393224 | tf_op jit(solution)/shard_map/ppermute | solution.py:16
  32.9 9.9 %collective-permute-start.16 = (f32[1,40,256]{2,1,0:T(8,128)S(1)}, f32[1,40,256]{2,1,0:T(8,128)S(1)}, u32[]{:S(2)}, u32[]{:S(2)}) collective-permute-start(f32[1,40,256]{2,1,0:T(8,128)S(1)} %get-tuple-element.60), channel_id=1, source_target_pairs={{0,1},{1,0},{2,3},{3,2},{4,5},{5,4},{6,7},{7,6},{8,9},{9,8},{10,11... | collective-permute-start | bytes 122888 | tf_op jit(solution)/shard_map/ppermute | solution.py:16
  34.0 10.2 %collective-permute-start.5 = (f32[64,512]{1,0:T(8,128)S(1)}, f32[64,512]{1,0:T(8,128)S(1)}, u32[]{:S(2)}, u32[]{:S(2)}) collective-permute-start(f32[64,512]{1,0:T(8,128)S(1)} %add.40), channel_id=1, source_target_pairs={{0,16},{8,24},{16,0},{24,8},{1,17},{9,25},{17,1},{25,9},{2,18},{10... | collective-permute-start | bytes 393224 | tf_op jit(solution)/shard_map/ppermute | solution.py:16
  42.7 5.8 %collective-permute-start.21 = (f32[64,512]{1,0:T(8,128)S(1)}, f32[64,512]{1,0:T(8,128)S(1)}, u32[]{:S(2)}, u32[]{:S(2)}) collective-permute-start(f32[64,512]{1,0:T(8,128)S(1)} %add.47.refs_0_), channel_id=1, source_target_pairs={{0,8},{8,0},{16,24},{24,16},{1,9},{9,1},{17,25},{25,17},{2,10},{10... | collective-permute-start | bytes 393224 | tf_op jit(solution)/shard_map/ppermute | solution.py:16
  42.8 10.2 %collective-permute-start.17 = (f32[2,40,256]{2,1,0:T(8,128)S(1)}, f32[2,40,256]{2,1,0:T(8,128)S(1)}, u32[]{:S(2)}, u32[]{:S(2)}) collective-permute-start(f32[2,40,256]{2,1,0:T(8,128)S(1)} %pad_maximum_fusion.3), channel_id=1, source_target_pairs={{0,2},{1,3},{2,0},{3,1},{4,6},{5,7},{6,4},{7,5},{8,10},{9,11},{10,... | collective-permute-start | bytes 245768 | tf_op jit(solution)/shard_map/ppermute | solution.py:16
  44.2 9.4 %collective-permute-start.6 = (f32[64,512]{1,0:T(8,128)S(1)}, f32[64,512]{1,0:T(8,128)S(1)}, u32[]{:S(2)}, u32[]{:S(2)}) collective-permute-start(f32[64,512]{1,0:T(8,128)S(1)} %add.41.refs_0_), channel_id=1, source_target_pairs={{0,8},{8,0},{16,24},{24,16},{1,9},{9,1},{17,25},{25,17},{2,10},{10... | collective-permute-start | bytes 393224 | tf_op jit(solution)/shard_map/ppermute | solution.py:16
  50.2 7.5 %collective-permute-start.22 = (f32[64,640]{1,0:T(8,128)S(1)}, f32[64,640]{1,0:T(8,128)S(1)}, u32[]{:S(2)}, u32[]{:S(2)}) collective-permute-start(f32[64,640]{1,0:T(8,128)S(1)} %get-tuple-element.48), channel_id=1, source_target_pairs={{0,2},{1,3},{2,0},{3,1},{4,6},{5,7},{6,4},{7,5},{8,10},{9,11},{10,... | collective-permute-start | bytes 491528 | tf_op jit(solution)/shard_map/ppermute | solution.py:16
  51.5 7.1 %collective-permute-start.24 = (f32[64,640]{1,0:T(8,128)S(1)}, f32[64,640]{1,0:T(8,128)S(1)}, u32[]{:S(2)}, u32[]{:S(2)}) collective-permute-start(f32[64,640]{1,0:T(8,128)S(1)} %get-tuple-element.49), channel_id=1, source_target_pairs={{0,4},{1,5},{2,6},{3,7},{4,0},{5,1},{6,2},{7,3},{8,12},{9,13},{10,... | collective-permute-start | bytes 491528 | tf_op jit(solution)/shard_map/ppermute | solution.py:16
  53.0 16.6 %collective-permute-start.18 = (f32[4,40,256]{2,1,0:T(8,128)S(1)}, f32[4,40,256]{2,1,0:T(8,128)S(1)}, u32[]{:S(2)}, u32[]{:S(2)}) collective-permute-start(f32[4,40,256]{2,1,0:T(8,128)S(1)} %pad_maximum_fusion.2), channel_id=1, source_target_pairs={{0,4},{1,5},{2,6},{3,7},{4,0},{5,1},{6,2},{7,3},{8,12},{9,13},{10,... | collective-permute-start | bytes 491528 | tf_op jit(solution)/shard_map/ppermute | solution.py:16
  55.4 6.7 %collective-permute-start.11 = (f32[64,640]{1,0:T(8,128)S(1)}, f32[64,640]{1,0:T(8,128)S(1)}, u32[]{:S(2)}, u32[]{:S(2)}) collective-permute-start(f32[64,640]{1,0:T(8,128)S(1)} %get-tuple-element.38), channel_id=1, source_target_pairs={{0,2},{1,3},{2,0},{3,1},{4,6},{5,7},{6,4},{7,5},{8,10},{9,11},{10,... | collective-permute-start | bytes 491528 | tf_op jit(solution)/shard_map/ppermute | solution.py:16
  56.2 7.9 %collective-permute-start.13 = (f32[64,640]{1,0:T(8,128)S(1)}, f32[64,640]{1,0:T(8,128)S(1)}, u32[]{:S(2)}, u32[]{:S(2)}) collective-permute-start(f32[64,640]{1,0:T(8,128)S(1)} %get-tuple-element.39), channel_id=1, source_target_pairs={{0,4},{1,5},{2,6},{3,7},{4,0},{5,1},{6,2},{7,3},{8,12},{9,13},{10,... | collective-permute-start | bytes 491528 | tf_op jit(solution)/shard_map/ppermute | solution.py:16
  57.7 8.2 %collective-permute-start.23 = (f32[64,640]{1,0:T(8,128)S(1)}, f32[64,640]{1,0:T(8,128)S(1)}, u32[]{:S(2)}, u32[]{:S(2)}) collective-permute-start(f32[64,640]{1,0:T(8,128)S(1)} %add.48), channel_id=1, source_target_pairs={{0,4},{1,5},{2,6},{3,7},{4,0},{5,1},{6,2},{7,3},{8,12},{9,13},{10,... | collective-permute-start | bytes 491528 | tf_op jit(solution)/shard_map/ppermute | solution.py:16
  58.6 12.1 %copy-start.2 = (f32[1,1,2048,256]{3,2,1,0:T(8,128)S(1)}, f32[1,1,2048,256]{3,2,1,0:T(8,128)}, u32[]{:S(2)}) copy-start(f32[1,1,2048,256]{3,2,1,0:T(8,128)} %param.12) | copy-start | bytes 6291460
  58.6 7.3 %collective-permute-start.25 = (f32[64,640]{1,0:T(8,128)S(1)}, f32[64,640]{1,0:T(8,128)S(1)}, u32[]{:S(2)}, u32[]{:S(2)}) collective-permute-start(f32[64,640]{1,0:T(8,128)S(1)} %add.50), channel_id=1, source_target_pairs={{0,2},{1,3},{2,0},{3,1},{4,6},{5,7},{6,4},{7,5},{8,10},{9,11},{10,... | collective-permute-start | bytes 491528 | tf_op jit(solution)/shard_map/ppermute | solution.py:16
  62.1 5.6 %collective-permute-start.12 = (f32[64,640]{1,0:T(8,128)S(1)}, f32[64,640]{1,0:T(8,128)S(1)}, u32[]{:S(2)}, u32[]{:S(2)}) collective-permute-start(f32[64,640]{1,0:T(8,128)S(1)} %add.42), channel_id=1, source_target_pairs={{0,4},{1,5},{2,6},{3,7},{4,0},{5,1},{6,2},{7,3},{8,12},{9,13},{10,... | collective-permute-start | bytes 491528 | tf_op jit(solution)/shard_map/ppermute | solution.py:16
  64.2 5.4 %collective-permute-start.14 = (f32[64,640]{1,0:T(8,128)S(1)}, f32[64,640]{1,0:T(8,128)S(1)}, u32[]{:S(2)}, u32[]{:S(2)}) collective-permute-start(f32[64,640]{1,0:T(8,128)S(1)} %add.44), channel_id=1, source_target_pairs={{0,2},{1,3},{2,0},{3,1},{4,6},{5,7},{6,4},{7,5},{8,10},{9,11},{10,... | collective-permute-start | bytes 491528 | tf_op jit(solution)/shard_map/ppermute | solution.py:16
  65.9 4.8 %copy-start = (f32[1,1,2048,512]{3,2,1,0:T(8,128)S(1)}, f32[1,1,2048,512]{3,2,1,0:T(8,128)}, u32[]{:S(2)}) copy-start(f32[1,1,2048,512]{3,2,1,0:T(8,128)} %param.13) | copy-start | bytes 12582916
  66.0 3.9 %copy-start.4 = (s32[1,1,512]{2,1,0:T(1,128)S(1)}, s32[1,1,512]{2,1,0:T(1,128)}, u32[]{:S(2)}) copy-start(s32[1,1,512]{2,1,0:T(1,128)} %param.11) | copy-start | bytes 6148
  66.0 4.7 %collective-permute-start.26 = (f32[64,1280]{1,0:T(8,128)S(1)}, f32[64,1280]{1,0:T(8,128)S(1)}, u32[]{:S(2)}, u32[]{:S(2)}) collective-permute-start(f32[64,1280]{1,0:T(8,128)S(1)} %pad_maximum_fusion.1.own_ref), channel_id=1, source_target_pairs={{0,1},{1,0},{2,3},{3,2},{4,5},{5,4},{6,7},{7,6},{8,9},{9,8},{10,11... | collective-permute-start | bytes 983048 | tf_op jit(solution)/shard_map/ppermute | solution.py:16
  69.6 4.8 %collective-permute-start.15 = (f32[64,1280]{1,0:T(8,128)S(1)}, f32[64,1280]{1,0:T(8,128)S(1)}, u32[]{:S(2)}, u32[]{:S(2)}) collective-permute-start(f32[64,1280]{1,0:T(8,128)S(1)} %pad_maximum_fusion.own_ref), channel_id=1, source_target_pairs={{0,1},{1,0},{2,3},{3,2},{4,5},{5,4},{6,7},{7,6},{8,9},{9,8},{10,11... | collective-permute-start | bytes 983048 | tf_op jit(solution)/shard_map/ppermute | solution.py:16

commit v4 on v3

--- a/solution.py
+++ b/solution.py
@@ -63,6 +63,24 @@
         lax.fori_loop(0, n // rows, step, 0)
 
     return call(body, [shape((n, m), BF16)] * 2, v)
+
+
+def split_with_tops(v, fanout, tops, rows=256):
+    n, m = v.shape
+    block = n // fanout
+
+    def body(v_ref, h_ref, l_ref, t_ref):
+        for f in range(fanout):
+            t_ref[f * tops : (f + 1) * tops] = v_ref[(f + 1) * block - tops : (f + 1) * block]
+
+        def step(i, _):
+            s = pl.ds(pl.multiple_of(i * rows, rows), rows)
+            h_ref[s], l_ref[s] = cut(v_ref[s])
+            return 0
+
+        lax.fori_loop(0, n // rows, step, 0)
+
+    return call(body, [shape((n, m), BF16)] * 2 + [shape((fanout * tops, m))], v)
 
 
 def adjoint(blocks, order, part, count, k):
@@ -263,7 +281,7 @@
     sep_local, top_count = coupling.shape[1:]
     leaf, cons = leaf_modes[0, 0], constraint_modes[0, 0]
     slots = leaf.shape[1] // fanout
-    row_count, width = operator.shape
+    row_count, _ = operator.shape
     block = row_count // fanout
     top_local = block - mode_local - sep_local
     row_masks = [1 << b for b in range(planes.bit_length() - 1)]
@@ -273,11 +291,13 @@
     xt = vectors.T
     col_order = spans(col_masks)
     blocks = [xt] + [swap(xt, "col", m) for m in col_order[1:]]
-    tops = operator.reshape(fanout, block, width)[:, block - top_local :].reshape(-1, width)
+    *k, tops = split_with_tops(operator, fanout, top_local)
+    k = [*k, *split(partner)]
     row_order = spans(row_masks)
     tops = [tops] + [swap(tops, "row", m) for m in row_order[1:]]
-    k = split(operator)
-    k = k + split(partner)
+    tops = spread("row", tops, row_order, top_count)
+    tops_partner = swap(tops, "col", 1)
+    t = split(tops) + split(tops_partner)
 
     parts = 2
     half_nv = xt.shape[0] * len(blocks)
@@ -286,10 +306,6 @@
     adj = []
     for h in range(parts):
         adj.append(list(adjoint(blocks, order, h, count, k)))
-    tops = spread("row", list(tops), row_order, top_count)
-    tops_partner = swap(tops, "col", 1)
-    t = split(tops) + split(tops_partner)
-
     tag_rows = -(-mode_local // top_count)
     owner_map, coupling, _ = lax.optimization_barrier((owner_map, coupling, adj[1][0]))
     tags = owner_map[:, 0].astype(F32)

time: 78.3 us -> 79.1 us (1.010)
  starting transfers between devices: 30.1 us -> 31.4 us
  local copies, waits for them, and re-layouts: 2.6 us -> 1.68 us
    ppermute x27, starting transfers between devices: 30.1 us -> 31.4 us  [swap(): return lax.ppermute(v, axis, [(i, i ^ mask) for i in range(n)])]
    reshape x1 -> x0, local copies, waits for them, and re-layouts: 0.91 us -> none  [on_device(): operator.reshape(fanout, block, width)[:, block - top_local:]]
  transfers between devices with their start and end apart: 27 -> 27, of which waited for: 14 -> 13; matrix products, arithmetic and copies ran while one was open for 2% -> 0% of each run, Pallas kernels for 14% -> 13%
where the time goes in v4:
time: 79.1 us; the launch traced here: 78.9 us
  starting transfers between devices  31.4 us (40%)
  waiting for transfers between devices  30.3 us (38%)
  Pallas kernels  14.2 us (18%)
  local copies, waits for them, and re-layouts  1.68 us (2%)
  between operations  1.01 us (1%)
    ppermute x27, starting transfers between devices, swap(): return lax.ppermute(v, axis, [(i, i ^ mask) for i in range(n)])  31.4 us
    ppermute x27, waiting for transfers between devices, swap(): return lax.ppermute(v, axis, [(i, i ^ mask) for i in range(n)])  30.3 us
    pallas_call x2, Pallas kernels, expand(): pl.pallas_call(body, out_shape=[shape((sep_local, nv * parts)), shape((in...  7.36 us
    pallas_call x12, Pallas kernels, call(): pl.pallas_call(body, out_shape=out, in_specs=specs, out_specs=[pl.BlockSp...  6.88 us
    unnamed x15, local copies, waits for them, and re-layouts  1.63 us
  transfers between devices with their start and end apart: 27, of which 13 were waited for; matrix products, arithmetic and copies ran while one was open for 0% of the time, Pallas kernels for 13%

profile of v4, /device:TPU:0, one launch (start us, length us, event | category | flops | bytes accessed | tf_op | source)
XLA Modules:
  0.0 78.9 jit_solution(6057248593894435233)
XLA Ops:
  0.6 0.6 collective-permute-start.3
  1.2 1.6 %copy-done.1 = f32[1024,512]{1,0:T(8,128)S(1)} copy-done((f32[1024,512]{1,0:T(8,128)S(1)}, f32[1024,512]{1,0:T(8,128)}, u32[]{:S(2)}) %copy-start.1) | copy-done | bytes 2097176
  2.8 0.4 shard_map.86
  3.2 4.7 %collective-permute-start.9 = (f32[64,512]{1,0:T(8,128)S(1)}, f32[64,512]{1,0:T(8,128)S(1)}, u32[]{:S(2)}, u32[]{:S(2)}) collective-permute-start(f32[64,512]{1,0:T(8,128)S(1)} %get-tuple-element.35.refs_0_), channel_id=1, source_target_pairs={{0,24},{8,16},{16,8},{24,0},{1,25},{9,17},{17,9},{25,1},{2,26},{10... | collective-permute-start | bytes 393224 | tf_op jit(solution)/shard_map/ppermute | solution.py:16
  7.8 0.6 collective-permute-start.7
  8.5 2.6 %collective-permute-start.2 = (f32[32,1024]{1,0:T(8,128)S(1)}, f32[32,1024]{1,0:T(8,128)S(1)}, u32[]{:S(2)}, u32[]{:S(2)}) collective-permute-start(f32[32,1024]{1,0:T(8,128)S(1)} %bitcast.37), channel_id=1, source_target_pairs={{0,6},{1,7},{2,4},{3,5},{4,2},{5,3},{6,0},{7,1},{8,14},{9,15},{10,... | collective-permute-start | bytes 393224 | tf_op jit(solution)/shard_map/ppermute | solution.py:16
  11.1 1.2 %collective-permute-done.9.refs_3_ = f32[64,512]{1,0:T(8,128)S(1)} collective-permute-done((f32[64,512]{1,0:T(8,128)S(1)}, f32[64,512]{1,0:T(8,128)S(1)}, u32[]{:S(2)}, u32[]{:S(2)}) %collective-permute-start.9) | collective-permute-done | bytes 131104 | tf_op jit(solution)/shard_map/ppermute | solution.py:16
  12.3 1.7 %collective-permute-start.1 = (f32[32,1024]{1,0:T(8,128)S(1)}, f32[32,1024]{1,0:T(8,128)S(1)}, u32[]{:S(2)}, u32[]{:S(2)}) collective-permute-start(f32[32,1024]{1,0:T(8,128)S(1)} %bitcast.38), channel_id=1, source_target_pairs={{0,4},{1,5},{2,6},{3,7},{4,0},{5,1},{6,2},{7,3},{8,12},{9,13},{10,... | collective-permute-start | bytes 393224 | tf_op jit(solution)/shard_map/ppermute | solution.py:16
  14.0 5.6 %collective-permute-done.8.refs_2_ = f32[64,512]{1,0:T(8,128)S(1)} collective-permute-done((f32[64,512]{1,0:T(8,128)S(1)}, f32[64,512]{1,0:T(8,128)S(1)}, u32[]{:S(2)}, u32[]{:S(2)}) %collective-permute-start.8) | collective-permute-done | bytes 131104 | tf_op jit(solution)/shard_map/ppermute | solution.py:16
  19.6 1.5 %collective-permute-start = (f32[32,1024]{1,0:T(8,128)S(1)}, f32[32,1024]{1,0:T(8,128)S(1)}, u32[]{:S(2)}, u32[]{:S(2)}) collective-permute-start(f32[32,1024]{1,0:T(8,128)S(1)} %bitcast.39), channel_id=1, source_target_pairs={{0,2},{1,3},{2,0},{3,1},{4,6},{5,7},{6,4},{7,5},{8,10},{9,11},{10,... | collective-permute-start | bytes 393224 | tf_op jit(solution)/shard_map/ppermute | solution.py:16
  21.1 0.1 collective-permute-start.10
  21.2 0.4 shard_map.87
  21.6 3.0 %collective-permute-done.refs_1_ = f32[32,1024]{1,0:T(8,128)S(1)} collective-permute-done((f32[32,1024]{1,0:T(8,128)S(1)}, f32[32,1024]{1,0:T(8,128)S(1)}, u32[]{:S(2)}, u32[]{:S(2)}) %collective-permute-start) | collective-permute-done | bytes 131104 | tf_op jit(solution)/shard_map/ppermute | solution.py:16
  24.6 0.8 shard_map.88
  25.4 0.8 shard_map.96
  26.3 2.0 %collective-permute-start.4 = (f32[64,512]{1,0:T(8,128)S(1)}, f32[64,512]{1,0:T(8,128)S(1)}, u32[]{:S(2)}, u32[]{:S(2)}) collective-permute-start(f32[64,512]{1,0:T(8,128)S(1)} %get-tuple-element.34), channel_id=1, source_target_pairs={{0,8},{8,0},{16,24},{24,16},{1,9},{9,1},{17,25},{25,17},{2,10},{10... | collective-permute-start | bytes 393224 | tf_op jit(solution)/shard_map/ppermute | solution.py:16
  28.3 3.6 %collective-permute-done.19 = f32[64,512]{1,0:T(8,128)S(1)} collective-permute-done((f32[64,512]{1,0:T(8,128)S(1)}, f32[64,512]{1,0:T(8,128)S(1)}, u32[]{:S(2)}, u32[]{:S(2)}) %collective-permute-start.19) | collective-permute-done | bytes 131104 | tf_op jit(solution)/shard_map/ppermute | solution.py:16
  31.9 1.8 %collective-permute-start.20 = (f32[64,512]{1,0:T(8,128)S(1)}, f32[64,512]{1,0:T(8,128)S(1)}, u32[]{:S(2)}, u32[]{:S(2)}) collective-permute-start(f32[64,512]{1,0:T(8,128)S(1)} %add.46), channel_id=1, source_target_pairs={{0,16},{8,24},{16,0},{24,8},{1,17},{9,25},{17,1},{25,9},{2,18},{10... | collective-permute-start | bytes 393224 | tf_op jit(solution)/shard_map/ppermute | solution.py:16
  33.8 0.3 collective-permute-done.4
  34.1 2.0 %collective-permute-start.5 = (f32[64,512]{1,0:T(8,128)S(1)}, f32[64,512]{1,0:T(8,128)S(1)}, u32[]{:S(2)}, u32[]{:S(2)}) collective-permute-start(f32[64,512]{1,0:T(8,128)S(1)} %add.40), channel_id=1, source_target_pairs={{0,16},{8,24},{16,0},{24,8},{1,17},{9,25},{17,1},{25,9},{2,18},{10... | collective-permute-start | bytes 393224 | tf_op jit(solution)/shard_map/ppermute | solution.py:16
  36.1 6.9 %collective-permute-done.20 = f32[64,512]{1,0:T(8,128)S(1)} collective-permute-done((f32[64,512]{1,0:T(8,128)S(1)}, f32[64,512]{1,0:T(8,128)S(1)}, u32[]{:S(2)}, u32[]{:S(2)}) %collective-permute-start.20) | collective-permute-done | bytes 131104 | tf_op jit(solution)/shard_map/ppermute | solution.py:16
  43.0 0.2 collective-permute-start.21
  43.2 1.6 %collective-permute-start.17 = (f32[2,40,256]{2,1,0:T(8,128)S(1)}, f32[2,40,256]{2,1,0:T(8,128)S(1)}, u32[]{:S(2)}, u32[]{:S(2)}) collective-permute-start(f32[2,40,256]{2,1,0:T(8,128)S(1)} %pad_maximum_fusion.3), channel_id=1, source_target_pairs={{0,2},{1,3},{2,0},{3,1},{4,6},{5,7},{6,4},{7,5},{8,10},{9,11},{10,... | collective-permute-start | bytes 245768 | tf_op jit(solution)/shard_map/ppermute | solution.py:16
  44.8 0.1 shard_map.90
  44.9 0.1 shard_map.91
  45.0 2.0 %collective-permute-start.6 = (f32[64,512]{1,0:T(8,128)S(1)}, f32[64,512]{1,0:T(8,128)S(1)}, u32[]{:S(2)}, u32[]{:S(2)}) collective-permute-start(f32[64,512]{1,0:T(8,128)S(1)} %add.41.refs_0_), channel_id=1, source_target_pairs={{0,8},{8,0},{16,24},{24,16},{1,9},{9,1},{17,25},{25,17},{2,10},{10... | collective-permute-start | bytes 393224 | tf_op jit(solution)/shard_map/ppermute | solution.py:16
  47.0 2.1 %collective-permute-done.21.refs_1_ = f32[64,512]{1,0:T(8,128)S(1)} collective-permute-done((f32[64,512]{1,0:T(8,128)S(1)}, f32[64,512]{1,0:T(8,128)S(1)}, u32[]{:S(2)}, u32[]{:S(2)}) %collective-permute-start.21) | collective-permute-done | bytes 131104 | tf_op jit(solution)/shard_map/ppermute | solution.py:16
  49.1 1.7 %shard_map.97 = (f32[64,640]{1,0:T(8,128)S(1)}, f32[64,640]{1,0:T(8,128)S(1)}) custom-call(f32[64,512]{1,0:T(8,128)S(1)} %add.47.refs_0_, f32[64,512]{1,0:T(8,128)S(1)} %collective-permute-done.21.refs_1_, bf16[1024,512]{1,0:T(8,128)(2,1)S(1)} %get-tuple-element.29.refs_4_.refs_2_, bf16[1024,512]{1,0:T(8,128)(2,1)S(1)} %get-tuple-element.30.refs_5_.refs_3_, ...), custom_call_target="tpu_custom_call" | custom-call | flops 503316480 | bytes 5832704 | tf_op jit(solution)/shard_map/pallas_call | solution.py:24
  50.8 1.6 %collective-permute-start.22 = (f32[64,640]{1,0:T(8,128)S(1)}, f32[64,640]{1,0:T(8,128)S(1)}, u32[]{:S(2)}, u32[]{:S(2)}) collective-permute-start(f32[64,640]{1,0:T(8,128)S(1)} %get-tuple-element.50), channel_id=1, source_target_pairs={{0,2},{1,3},{2,0},{3,1},{4,6},{5,7},{6,4},{7,5},{8,10},{9,11},{10,... | collective-permute-start | bytes 491528 | tf_op jit(solution)/shard_map/ppermute | solution.py:16
  52.4 1.5 %collective-permute-start.24 = (f32[64,640]{1,0:T(8,128)S(1)}, f32[64,640]{1,0:T(8,128)S(1)}, u32[]{:S(2)}, u32[]{:S(2)}) collective-permute-start(f32[64,640]{1,0:T(8,128)S(1)} %get-tuple-element.51), channel_id=1, source_target_pairs={{0,4},{1,5},{2,6},{3,7},{4,0},{5,1},{6,2},{7,3},{8,12},{9,13},{10,... | collective-permute-start | bytes 491528 | tf_op jit(solution)/shard_map/ppermute | solution.py:16
  53.9 0.6 collective-permute-start.18
  54.5 1.7 %shard_map.92 = (f32[64,640]{1,0:T(8,128)S(1)}, f32[64,640]{1,0:T(8,128)S(1)}) custom-call(f32[64,512]{1,0:T(8,128)S(1)} %add.41.refs_0_, f32[64,512]{1,0:T(8,128)S(1)} %collective-permute-done.6.refs_1_, bf16[1024,512]{1,0:T(8,128)(2,1)S(1)} %get-tuple-element.29.refs_4_.refs_2_, bf16[1024,512]{1,0:T(8,128)(2,1)S(1)} %get-tuple-element.30.refs_5_.refs_3_, ...), custom_call_target="tpu_custom_call" | custom-call | flops 503316480 | bytes 5832704 | tf_op jit(solution)/shard_map/pallas_call | solution.py:24
  56.2 0.6 collective-permute-start.11
  56.8 1.5 %collective-permute-start.13 = (f32[64,640]{1,0:T(8,128)S(1)}, f32[64,640]{1,0:T(8,128)S(1)}, u32[]{:S(2)}, u32[]{:S(2)}) collective-permute-start(f32[64,640]{1,0:T(8,128)S(1)} %get-tuple-element.41), channel_id=1, source_target_pairs={{0,4},{1,5},{2,6},{3,7},{4,0},{5,1},{6,2},{7,3},{8,12},{9,13},{10,... | collective-permute-start | bytes 491528 | tf_op jit(solution)/shard_map/ppermute | solution.py:16
  58.3 0.7 collective-permute-start.23
  59.0 0.4 collective-permute-done.24
  59.5 1.7 %collective-permute-start.25 = (f32[64,640]{1,0:T(8,128)S(1)}, f32[64,640]{1,0:T(8,128)S(1)}, u32[]{:S(2)}, u32[]{:S(2)}) collective-permute-start(f32[64,640]{1,0:T(8,128)S(1)} %add.50), channel_id=1, source_target_pairs={{0,2},{1,3},{2,0},{3,1},{4,6},{5,7},{6,4},{7,5},{8,10},{9,11},{10,... | collective-permute-start | bytes 491528 | tf_op jit(solution)/shard_map/ppermute | solution.py:16
  61.1 2.0 %collective-permute-done.11 = f32[64,640]{1,0:T(8,128)S(1)} collective-permute-done((f32[64,640]{1,0:T(8,128)S(1)}, f32[64,640]{1,0:T(8,128)S(1)}, u32[]{:S(2)}, u32[]{:S(2)}) %collective-permute-start.11) | collective-permute-done | bytes 163872 | tf_op jit(solution)/shard_map/ppermute | solution.py:16
  63.2 1.1 %collective-permute-start.12 = (f32[64,640]{1,0:T(8,128)S(1)}, f32[64,640]{1,0:T(8,128)S(1)}, u32[]{:S(2)}, u32[]{:S(2)}) collective-permute-start(f32[64,640]{1,0:T(8,128)S(1)} %add.42), channel_id=1, source_target_pairs={{0,4},{1,5},{2,6},{3,7},{4,0},{5,1},{6,2},{7,3},{8,12},{9,13},{10,... | collective-permute-start | bytes 491528 | tf_op jit(solution)/shard_map/ppermute | solution.py:16
  64.3 0.6 collective-permute-done.13
  65.0 0.6 collective-permute-start.14
  65.6 1.1 %collective-permute-done.23 = f32[64,640]{1,0:T(8,128)S(1)} collective-permute-done((f32[64,640]{1,0:T(8,128)S(1)}, f32[64,640]{1,0:T(8,128)S(1)}, u32[]{:S(2)}, u32[]{:S(2)}) %collective-permute-start.23) | collective-permute-done | bytes 163872 | tf_op jit(solution)/shard_map/ppermute | solution.py:16
  66.9 1.7 %collective-permute-done.12 = f32[64,640]{1,0:T(8,128)S(1)} collective-permute-done((f32[64,640]{1,0:T(8,128)S(1)}, f32[64,640]{1,0:T(8,128)S(1)}, u32[]{:S(2)}, u32[]{:S(2)}) %collective-permute-start.12) | collective-permute-done | bytes 163872 | tf_op jit(solution)/shard_map/ppermute | solution.py:16
  68.6 1.7 %collective-permute-done.14 = f32[64,640]{1,0:T(8,128)S(1)} collective-permute-done((f32[64,640]{1,0:T(8,128)S(1)}, f32[64,640]{1,0:T(8,128)S(1)}, u32[]{:S(2)}, u32[]{:S(2)}) %collective-permute-start.14) | collective-permute-done | bytes 163872 | tf_op jit(solution)/shard_map/ppermute | solution.py:16
  70.4 0.1 collective-permute-start.15
  70.7 0.8 %shard_map.95 = (bf16[512,1024]{1,0:T(8,128)(2,1)S(1)}, bf16[512,512]{1,0:T(8,128)(2,1)S(1)}) custom-call(f32[8,128]{1,0:T(8,128)S(1)} %slice.14.tag_ref, s32[1,512]{1,0:T(1,128)S(1)} %bitcast.43), custom_call_target="tpu_custom_call" | custom-call | bytes 1579008 | tf_op jit(solution)/shard_map/pallas_call | solution.py:24
  71.5 3.7 %shard_map.98 = (f32[32,256]{1,0:T(8,128)}, f32[2048,256]{1,0:T(8,128)}) custom-call(f32[64,1280]{1,0:T(8,128)S(1)} %pad_maximum_fusion.1.own_ref, f32[64,1280]{1,0:T(8,128)S(1)} %collective-permute-done.26.other_ref, bf16[256,256]{1,0:T(8,128)(2,1)S(1)} %get-tuple-element.44.ch, bf16[256,256]{1,0:T(8,128)(2,1)S(1)} %get-tuple-element.45.cl, ...), custom_call_target="tpu_custom_call" | custom-call | flops 2415919104 | bytes 7340032 | tf_op jit(solution)/shard_map/pallas_call | solution.py:244
  75.2 3.7 %shard_map.99 = (f32[32,256]{1,0:T(8,128)}, f32[2048,256]{1,0:T(8,128)}) custom-call(f32[64,1280]{1,0:T(8,128)S(1)} %pad_maximum_fusion.own_ref, f32[64,1280]{1,0:T(8,128)S(1)} %collective-permute-done.15.other_ref, bf16[256,256]{1,0:T(8,128)(2,1)S(1)} %get-tuple-element.44.ch, ...), custom_call_target="tpu_custom_call", output_to_operand_aliasing={{0}: (8, {}), {1}: (9, {})} | custom-call | flops 2415919104 | bytes 7340032 | tf_op jit(solution)/shard_map/pallas_call | solution.py:244
  (59 shorter events, 0.8 us)
Async XLA Ops:
  0.6 20.6 %collective-permute-start.3 = (f32[1024,512]{1,0:T(8,128)}, f32[1024,512]{1,0:T(8,128)S(1)}, u32[]{:S(2)}, u32[]{:S(2)}) collective-permute-start(f32[1024,512]{1,0:T(8,128)} %v_ref.1), channel_id=1, source_target_pairs={{0,1},{1,0},{2,3},{3,2},{4,5},{5,4},{6,7},{7,6},{8,9},{9,8},{10,11... | collective-permute-start | bytes 6291464 | tf_op jit(solution)/shard_map/ppermute | solution.py:16
  1.2 1.6 %copy-start.1 = (f32[1024,512]{1,0:T(8,128)S(1)}, f32[1024,512]{1,0:T(8,128)}, u32[]{:S(2)}) copy-start(f32[1024,512]{1,0:T(8,128)} %v_ref.1) | copy-start | bytes 6291460
  2.8 5.7 %copy-start.3 = (f32[1024,32]{0,1:T(8,128)S(1)}, f32[1024,32]{0,1:T(8,128)}, u32[]{:S(2)}) copy-start(f32[1024,32]{0,1:T(8,128)} %param.8) | copy-start | bytes 393220
  3.2 9.1 %collective-permute-start.9 = (f32[64,512]{1,0:T(8,128)S(1)}, f32[64,512]{1,0:T(8,128)S(1)}, u32[]{:S(2)}, u32[]{:S(2)}) collective-permute-start(f32[64,512]{1,0:T(8,128)S(1)} %get-tuple-element.35.refs_0_), channel_id=1, source_target_pairs={{0,24},{8,16},{16,8},{24,0},{1,25},{9,17},{17,9},{25,1},{2,26},{10... | collective-permute-start | bytes 393224 | tf_op jit(solution)/shard_map/ppermute | solution.py:16
  7.8 11.7 %collective-permute-start.8 = (f32[64,512]{1,0:T(8,128)S(1)}, f32[64,512]{1,0:T(8,128)S(1)}, u32[]{:S(2)}, u32[]{:S(2)}) collective-permute-start(f32[64,512]{1,0:T(8,128)S(1)} %get-tuple-element.35.refs_0_), channel_id=1, source_target_pairs={{0,16},{8,24},{16,0},{24,8},{1,17},{9,25},{17,1},{25,9},{2,18},{10... | collective-permute-start | bytes 393224 | tf_op jit(solution)/shard_map/ppermute | solution.py:16
  7.8 13.2 %collective-permute-start.7 = (f32[64,512]{1,0:T(8,128)S(1)}, f32[64,512]{1,0:T(8,128)S(1)}, u32[]{:S(2)}, u32[]{:S(2)}) collective-permute-start(f32[64,512]{1,0:T(8,128)S(1)} %get-tuple-element.35.refs_0_), channel_id=1, source_target_pairs={{0,8},{8,0},{16,24},{24,16},{1,9},{9,1},{17,25},{25,17},{2,10},{10... | collective-permute-start | bytes 393224 | tf_op jit(solution)/shard_map/ppermute | solution.py:16
  8.5 13.1 %collective-permute-start.2 = (f32[32,1024]{1,0:T(8,128)S(1)}, f32[32,1024]{1,0:T(8,128)S(1)}, u32[]{:S(2)}, u32[]{:S(2)}) collective-permute-start(f32[32,1024]{1,0:T(8,128)S(1)} %bitcast.37), channel_id=1, source_target_pairs={{0,6},{1,7},{2,4},{3,5},{4,2},{5,3},{6,0},{7,1},{8,14},{9,15},{10,... | collective-permute-start | bytes 393224 | tf_op jit(solution)/shard_map/ppermute | solution.py:16
  12.3 9.3 %collective-permute-start.1 = (f32[32,1024]{1,0:T(8,128)S(1)}, f32[32,1024]{1,0:T(8,128)S(1)}, u32[]{:S(2)}, u32[]{:S(2)}) collective-permute-start(f32[32,1024]{1,0:T(8,128)S(1)} %bitcast.38), channel_id=1, source_target_pairs={{0,4},{1,5},{2,6},{3,7},{4,0},{5,1},{6,2},{7,3},{8,12},{9,13},{10,... | collective-permute-start | bytes 393224 | tf_op jit(solution)/shard_map/ppermute | solution.py:16
  19.6 5.0 %collective-permute-start = (f32[32,1024]{1,0:T(8,128)S(1)}, f32[32,1024]{1,0:T(8,128)S(1)}, u32[]{:S(2)}, u32[]{:S(2)}) collective-permute-start(f32[32,1024]{1,0:T(8,128)S(1)} %bitcast.39), channel_id=1, source_target_pairs={{0,2},{1,3},{2,0},{3,1},{4,6},{5,7},{6,4},{7,5},{8,10},{9,11},{10,... | collective-permute-start | bytes 393224 | tf_op jit(solution)/shard_map/ppermute | solution.py:16
  21.1 23.7 %collective-permute-start.10 = (f32[256,512]{1,0:T(8,128)S(1)}, f32[256,512]{1,0:T(8,128)S(1)}, u32[]{:S(2)}, u32[]{:S(2)}) collective-permute-start(f32[256,512]{1,0:T(8,128)S(1)} %shard_map.89.v_ref), channel_id=1, source_target_pairs={{0,1},{1,0},{2,3},{3,2},{4,5},{5,4},{6,7},{7,6},{8,9},{9,8},{10,11... | collective-permute-start | bytes 1572872 | tf_op jit(solution)/shard_map/ppermute | solution.py:16
  25.4 2.9 %copy-start.6 = (s32[88,1]{0,1:T(1,128)S(1)}, s32[88,1]{0,1:T(1,128)}, u32[]{:S(2)}) copy-start(s32[88,1]{0,1:T(1,128)} %param.9) | copy-start | bytes 1060
  25.4 8.3 %copy-start.5 = (f32[1,32,256]{2,1,0:T(8,128)S(1)}, f32[1,32,256]{2,1,0:T(8,128)}, u32[]{:S(2)}) copy-start(f32[1,32,256]{2,1,0:T(8,128)} %param.10) | copy-start | bytes 98308
  26.2 5.7 %collective-permute-start.19 = (f32[64,512]{1,0:T(8,128)S(1)}, f32[64,512]{1,0:T(8,128)S(1)}, u32[]{:S(2)}, u32[]{:S(2)}) collective-permute-start(f32[64,512]{1,0:T(8,128)S(1)} %get-tuple-element.49), channel_id=1, source_target_pairs={{0,8},{8,0},{16,24},{24,16},{1,9},{9,1},{17,25},{25,17},{2,10},{10... | collective-permute-start | bytes 393224 | tf_op jit(solution)/shard_map/ppermute | solution.py:16
  26.3 7.8 %collective-permute-start.4 = (f32[64,512]{1,0:T(8,128)S(1)}, f32[64,512]{1,0:T(8,128)S(1)}, u32[]{:S(2)}, u32[]{:S(2)}) collective-permute-start(f32[64,512]{1,0:T(8,128)S(1)} %get-tuple-element.34), channel_id=1, source_target_pairs={{0,8},{8,0},{16,24},{24,16},{1,9},{9,1},{17,25},{25,17},{2,10},{10... | collective-permute-start | bytes 393224 | tf_op jit(solution)/shard_map/ppermute | solution.py:16
  31.9 11.1 %collective-permute-start.20 = (f32[64,512]{1,0:T(8,128)S(1)}, f32[64,512]{1,0:T(8,128)S(1)}, u32[]{:S(2)}, u32[]{:S(2)}) collective-permute-start(f32[64,512]{1,0:T(8,128)S(1)} %add.46), channel_id=1, source_target_pairs={{0,16},{8,24},{16,0},{24,8},{1,17},{9,25},{17,1},{25,9},{2,18},{10... | collective-permute-start | bytes 393224 | tf_op jit(solution)/shard_map/ppermute | solution.py:16
  33.7 9.5 %collective-permute-start.16 = (f32[1,40,256]{2,1,0:T(8,128)S(1)}, f32[1,40,256]{2,1,0:T(8,128)S(1)}, u32[]{:S(2)}, u32[]{:S(2)}) collective-permute-start(f32[1,40,256]{2,1,0:T(8,128)S(1)} %get-tuple-element.62), channel_id=1, source_target_pairs={{0,1},{1,0},{2,3},{3,2},{4,5},{5,4},{6,7},{7,6},{8,9},{9,8},{10,11... | collective-permute-start | bytes 122888 | tf_op jit(solution)/shard_map/ppermute | solution.py:16
  34.1 10.8 %collective-permute-start.5 = (f32[64,512]{1,0:T(8,128)S(1)}, f32[64,512]{1,0:T(8,128)S(1)}, u32[]{:S(2)}, u32[]{:S(2)}) collective-permute-start(f32[64,512]{1,0:T(8,128)S(1)} %add.40), channel_id=1, source_target_pairs={{0,16},{8,24},{16,0},{24,8},{1,17},{9,25},{17,1},{25,9},{2,18},{10... | collective-permute-start | bytes 393224 | tf_op jit(solution)/shard_map/ppermute | solution.py:16
  43.0 6.1 %collective-permute-start.21 = (f32[64,512]{1,0:T(8,128)S(1)}, f32[64,512]{1,0:T(8,128)S(1)}, u32[]{:S(2)}, u32[]{:S(2)}) collective-permute-start(f32[64,512]{1,0:T(8,128)S(1)} %add.47.refs_0_), channel_id=1, source_target_pairs={{0,8},{8,0},{16,24},{24,16},{1,9},{9,1},{17,25},{25,17},{2,10},{10... | collective-permute-start | bytes 393224 | tf_op jit(solution)/shard_map/ppermute | solution.py:16
  43.2 10.7 %collective-permute-start.17 = (f32[2,40,256]{2,1,0:T(8,128)S(1)}, f32[2,40,256]{2,1,0:T(8,128)S(1)}, u32[]{:S(2)}, u32[]{:S(2)}) collective-permute-start(f32[2,40,256]{2,1,0:T(8,128)S(1)} %pad_maximum_fusion.3), channel_id=1, source_target_pairs={{0,2},{1,3},{2,0},{3,1},{4,6},{5,7},{6,4},{7,5},{8,10},{9,11},{10,... | collective-permute-start | bytes 245768 | tf_op jit(solution)/shard_map/ppermute | solution.py:16
  45.0 9.5 %collective-permute-start.6 = (f32[64,512]{1,0:T(8,128)S(1)}, f32[64,512]{1,0:T(8,128)S(1)}, u32[]{:S(2)}, u32[]{:S(2)}) collective-permute-start(f32[64,512]{1,0:T(8,128)S(1)} %add.41.refs_0_), channel_id=1, source_target_pairs={{0,8},{8,0},{16,24},{24,16},{1,9},{9,1},{17,25},{25,17},{2,10},{10... | collective-permute-start | bytes 393224 | tf_op jit(solution)/shard_map/ppermute | solution.py:16
  50.8 7.5 %collective-permute-start.22 = (f32[64,640]{1,0:T(8,128)S(1)}, f32[64,640]{1,0:T(8,128)S(1)}, u32[]{:S(2)}, u32[]{:S(2)}) collective-permute-start(f32[64,640]{1,0:T(8,128)S(1)} %get-tuple-element.50), channel_id=1, source_target_pairs={{0,2},{1,3},{2,0},{3,1},{4,6},{5,7},{6,4},{7,5},{8,10},{9,11},{10,... | collective-permute-start | bytes 491528 | tf_op jit(solution)/shard_map/ppermute | solution.py:16
  52.4 7.1 %collective-permute-start.24 = (f32[64,640]{1,0:T(8,128)S(1)}, f32[64,640]{1,0:T(8,128)S(1)}, u32[]{:S(2)}, u32[]{:S(2)}) collective-permute-start(f32[64,640]{1,0:T(8,128)S(1)} %get-tuple-element.51), channel_id=1, source_target_pairs={{0,4},{1,5},{2,6},{3,7},{4,0},{5,1},{6,2},{7,3},{8,12},{9,13},{10,... | collective-permute-start | bytes 491528 | tf_op jit(solution)/shard_map/ppermute | solution.py:16
  53.9 16.6 %collective-permute-start.18 = (f32[4,40,256]{2,1,0:T(8,128)S(1)}, f32[4,40,256]{2,1,0:T(8,128)S(1)}, u32[]{:S(2)}, u32[]{:S(2)}) collective-permute-start(f32[4,40,256]{2,1,0:T(8,128)S(1)} %pad_maximum_fusion.2), channel_id=1, source_target_pairs={{0,4},{1,5},{2,6},{3,7},{4,0},{5,1},{6,2},{7,3},{8,12},{9,13},{10,... | collective-permute-start | bytes 491528 | tf_op jit(solution)/shard_map/ppermute | solution.py:16
  56.2 7.0 %collective-permute-start.11 = (f32[64,640]{1,0:T(8,128)S(1)}, f32[64,640]{1,0:T(8,128)S(1)}, u32[]{:S(2)}, u32[]{:S(2)}) collective-permute-start(f32[64,640]{1,0:T(8,128)S(1)} %get-tuple-element.40), channel_id=1, source_target_pairs={{0,2},{1,3},{2,0},{3,1},{4,6},{5,7},{6,4},{7,5},{8,10},{9,11},{10,... | collective-permute-start | bytes 491528 | tf_op jit(solution)/shard_map/ppermute | solution.py:16
  56.8 8.1 %collective-permute-start.13 = (f32[64,640]{1,0:T(8,128)S(1)}, f32[64,640]{1,0:T(8,128)S(1)}, u32[]{:S(2)}, u32[]{:S(2)}) collective-permute-start(f32[64,640]{1,0:T(8,128)S(1)} %get-tuple-element.41), channel_id=1, source_target_pairs={{0,4},{1,5},{2,6},{3,7},{4,0},{5,1},{6,2},{7,3},{8,12},{9,13},{10,... | collective-permute-start | bytes 491528 | tf_op jit(solution)/shard_map/ppermute | solution.py:16
  58.3 8.3 %collective-permute-start.23 = (f32[64,640]{1,0:T(8,128)S(1)}, f32[64,640]{1,0:T(8,128)S(1)}, u32[]{:S(2)}, u32[]{:S(2)}) collective-permute-start(f32[64,640]{1,0:T(8,128)S(1)} %add.48), channel_id=1, source_target_pairs={{0,4},{1,5},{2,6},{3,7},{4,0},{5,1},{6,2},{7,3},{8,12},{9,13},{10,... | collective-permute-start | bytes 491528 | tf_op jit(solution)/shard_map/ppermute | solution.py:16
  59.4 12.1 %copy-start.2 = (f32[1,1,2048,256]{3,2,1,0:T(8,128)S(1)}, f32[1,1,2048,256]{3,2,1,0:T(8,128)}, u32[]{:S(2)}) copy-start(f32[1,1,2048,256]{3,2,1,0:T(8,128)} %param.12) | copy-start | bytes 6291460
  59.5 7.3 %collective-permute-start.25 = (f32[64,640]{1,0:T(8,128)S(1)}, f32[64,640]{1,0:T(8,128)S(1)}, u32[]{:S(2)}, u32[]{:S(2)}) collective-permute-start(f32[64,640]{1,0:T(8,128)S(1)} %add.50), channel_id=1, source_target_pairs={{0,2},{1,3},{2,0},{3,1},{4,6},{5,7},{6,4},{7,5},{8,10},{9,11},{10,... | collective-permute-start | bytes 491528 | tf_op jit(solution)/shard_map/ppermute | solution.py:16
  63.2 5.4 %collective-permute-start.12 = (f32[64,640]{1,0:T(8,128)S(1)}, f32[64,640]{1,0:T(8,128)S(1)}, u32[]{:S(2)}, u32[]{:S(2)}) collective-permute-start(f32[64,640]{1,0:T(8,128)S(1)} %add.42), channel_id=1, source_target_pairs={{0,4},{1,5},{2,6},{3,7},{4,0},{5,1},{6,2},{7,3},{8,12},{9,13},{10,... | collective-permute-start | bytes 491528 | tf_op jit(solution)/shard_map/ppermute | solution.py:16
  65.0 5.4 %collective-permute-start.14 = (f32[64,640]{1,0:T(8,128)S(1)}, f32[64,640]{1,0:T(8,128)S(1)}, u32[]{:S(2)}, u32[]{:S(2)}) collective-permute-start(f32[64,640]{1,0:T(8,128)S(1)} %add.44), channel_id=1, source_target_pairs={{0,2},{1,3},{2,0},{3,1},{4,6},{5,7},{6,4},{7,5},{8,10},{9,11},{10,... | collective-permute-start | bytes 491528 | tf_op jit(solution)/shard_map/ppermute | solution.py:16
  66.7 4.8 %copy-start = (f32[1,1,2048,512]{3,2,1,0:T(8,128)S(1)}, f32[1,1,2048,512]{3,2,1,0:T(8,128)}, u32[]{:S(2)}) copy-start(f32[1,1,2048,512]{3,2,1,0:T(8,128)} %param.13) | copy-start | bytes 12582916
  66.8 3.9 %copy-start.4 = (s32[1,1,512]{2,1,0:T(1,128)S(1)}, s32[1,1,512]{2,1,0:T(1,128)}, u32[]{:S(2)}) copy-start(s32[1,1,512]{2,1,0:T(1,128)} %param.11) | copy-start | bytes 6148
  66.8 4.7 %collective-permute-start.26 = (f32[64,1280]{1,0:T(8,128)S(1)}, f32[64,1280]{1,0:T(8,128)S(1)}, u32[]{:S(2)}, u32[]{:S(2)}) collective-permute-start(f32[64,1280]{1,0:T(8,128)S(1)} %pad_maximum_fusion.1.own_ref), channel_id=1, source_target_pairs={{0,1},{1,0},{2,3},{3,2},{4,5},{5,4},{6,7},{7,6},{8,9},{9,8},{10,11... | collective-permute-start | bytes 983048 | tf_op jit(solution)/shard_map/ppermute | solution.py:16
  70.4 4.8 %collective-permute-start.15 = (f32[64,1280]{1,0:T(8,128)S(1)}, f32[64,1280]{1,0:T(8,128)S(1)}, u32[]{:S(2)}, u32[]{:S(2)}) collective-permute-start(f32[64,1280]{1,0:T(8,128)S(1)} %pad_maximum_fusion.own_ref), channel_id=1, source_target_pairs={{0,1},{1,0},{2,3},{3,2},{4,5},{5,4},{6,7},{7,6},{8,9},{9,8},{10,11... | collective-permute-start | bytes 983048 | tf_op jit(solution)/shard_map/ppermute | solution.py:16

commit v5 on v4

--- a/solution.py
+++ b/solution.py
@@ -143,11 +143,14 @@
             src, at = (kr, lo) if lo < rows else (tr, lo - rows)
             size = min(step, (rows if lo < rows else total) - lo)
             s = slice(at, at + size)
-            p = None
+            y = z = None
             for j in range(2):
                 h, l = parts[j]
-                q = three(h, l, src[2 * j][s], src[2 * j + 1][s], NT)
-                p = q if p is None else p + q
+                u = dot(src[2 * j][s], jnp.concatenate([h, l], axis=0), NT)
+                v = dot(src[2 * j + 1][s], h, NT)
+                y, z = (u, v) if y is None else (y + u, z + v)
+            y = y.T
+            p = y[:n] + y[n:] + z.T
             for o in range(2):
                 b, e = max(lo, o * half), min(lo + size, (o + 1) * half)
                 if b < e:
@@ -160,9 +163,7 @@
 
 def picks(tags, anc, block, mode_local, sep_local, slots, cands):
     fanout = tags.shape[0]
-    rows = fanout * block
-    seps = fanout * sep_local
-    modes = slots * fanout
+    group = slots + sep_local
     count = anc.shape[1]
 
     def body(tag_ref, anc_ref, p_ref, q_ref):
@@ -173,26 +174,25 @@
             jnp.int32, (block, block), 1
         )
         rank = dot(ones, jnp.where(before, 1.0, 0.0).astype(BF16), NN).astype(jnp.int32)
-        place = lax.broadcasted_iota(jnp.int32, (fanout, block), 0) * slots + rank
-        place = jnp.where(hit, place, -1)
         sep = (lane >= mode_local) & (lane < mode_local + sep_local)
-        home = modes + lax.broadcasted_iota(jnp.int32, (fanout, block), 0) * sep_local + lane - mode_local
-        place = jnp.where(sep, home, place)
-        row = lax.broadcasted_iota(jnp.int32, (modes + seps, block), 0)
+        place = jnp.where(sep, slots + lane - mode_local, jnp.where(hit, rank, -1))
+        row = lax.broadcasted_iota(jnp.int32, (group, block), 0)
         for f in range(fanout):
-            p_ref[:, f * block : (f + 1) * block] = jnp.where(row == place[f : f + 1], 1.0, 0.0).astype(BF16)
+            p_ref[f * group : (f + 1) * group] = jnp.where(row == place[f : f + 1], 1.0, 0.0).astype(BF16)
         which = lax.broadcasted_iota(jnp.int32, (count, cands), 1)
         wanted = jnp.broadcast_to(anc_ref[...], (8, count)).astype(F32).T[:, :1].astype(jnp.int32)
         q_ref[...] = jnp.where(which == wanted, 1.0, 0.0).astype(BF16)
 
-    return call(body, [shape((modes + seps, rows), BF16), shape((count, cands), BF16)], tags, anc)
+    return call(body, [shape((fanout * group, block), BF16), shape((count, cands), BF16)], tags, anc)
 
 
 def expand(nblocks, own, other, coup, p, q, leaf, cons, part, parts, sep_local, prior):
     n, wide = own.shape
-    rows = p.shape[1]
+    group, block = sep_local + leaf.shape[1] * p.shape[1] // (wide - coup[0].shape[1]), p.shape[1]
+    fanout = p.shape[0] // group
+    rows, slots = fanout * block, group - sep_local
     inter, modes = leaf.shape
-    seps = p.shape[0] - modes
+    seps = fanout * sep_local
     count = cons.shape[1]
     nv = 2 * n
     tile = 256
@@ -209,11 +209,13 @@
             f_ref[pl.ds(a, low)] = own_ref[s]
             f_ref[pl.ds(b, low)] = other_ref[s]
         both = jnp.concatenate(cut(f_ref[:, :rows]), axis=0)
-        got = dot(p_ref[...], both, NT)
-        d_ref[:modes] = got[:modes].astype(BF16)
-        raw = got[modes:, :nv] + got[modes:, nv:]
+        raw = []
+        for f in range(fanout):
+            got = dot(p_ref[f * group : (f + 1) * group], both[:, f * block : (f + 1) * block], NT)
+            d_ref[f * slots : (f + 1) * slots] = got[:slots].astype(BF16)
+            raw.append(got[slots:, :nv] + got[slots:, nv:])
         th, tl = cut(f_ref[:, rows:].T)
-        sep = raw + three(ch[...], cl[...], th, tl, NN)
+        sep = jnp.concatenate(raw, axis=0) + three(ch[...], cl[...], th, tl, NN)
         s_ref[...] = sep
         tops = jnp.concatenate([th, tl], axis=1)
         cand = jnp.concatenate([tops, jnp.concatenate(cut(sep), axis=1)], axis=0)

time: 79.1 us -> 77.9 us (0.985)
  Pallas kernels: 14.2 us -> 12.9 us
    pallas_call x12, Pallas kernels: 6.88 us -> 6.08 us  [call(): pl.pallas_call(body, out_shape=out, in_specs=specs, out_specs=[pl.BlockSp...]
  transfers between devices with their start and end apart: 27 -> 27, of which waited for: 13 -> 13; matrix products, arithmetic and copies ran while one was open for 0% -> 0% of each run, Pallas kernels for 13% -> 12%
where the time goes in v5:
time: 77.9 us; the launch traced here: 77.7 us
  starting transfers between devices  31.5 us (40%)
  waiting for transfers between devices  30.3 us (39%)
  Pallas kernels  12.9 us (17%)
  local copies, waits for them, and re-layouts  1.68 us (2%)
  between operations  1.01 us (1%)
    ppermute x27, starting transfers between devices, swap(): return lax.ppermute(v, axis, [(i, i ^ mask) for i in range(n)])  31.5 us
    ppermute x27, waiting for transfers between devices, swap(): return lax.ppermute(v, axis, [(i, i ^ mask) for i in range(n)])  30.3 us
    pallas_call x2, Pallas kernels, expand(): pl.pallas_call(body, out_shape=[shape((sep_local, nv * parts)), shape((in...  6.82 us
    pallas_call x12, Pallas kernels, call(): pl.pallas_call(body, out_shape=out, in_specs=specs, out_specs=[pl.BlockSp...  6.08 us
    unnamed x15, local copies, waits for them, and re-layouts  1.63 us
  transfers between devices with their start and end apart: 27, of which 13 were waited for; matrix products, arithmetic and copies ran while one was open for 0% of the time, Pallas kernels for 12%

profile of v5, /device:TPU:0, one launch (start us, length us, event | category | flops | bytes accessed | tf_op | source)
XLA Modules:
  0.0 77.7 jit_solution(16900806723818492429)
XLA Ops:
  0.6 0.6 collective-permute-start.3
  1.2 1.6 %copy-done.2 = f32[1024,512]{1,0:T(8,128)S(1)} copy-done((f32[1024,512]{1,0:T(8,128)S(1)}, f32[1024,512]{1,0:T(8,128)}, u32[]{:S(2)}) %copy-start.2) | copy-done | bytes 2097176
  2.8 0.4 shard_map.86
  3.2 4.7 %collective-permute-start.9 = (f32[64,512]{1,0:T(8,128)S(1)}, f32[64,512]{1,0:T(8,128)S(1)}, u32[]{:S(2)}, u32[]{:S(2)}) collective-permute-start(f32[64,512]{1,0:T(8,128)S(1)} %get-tuple-element.35.refs_0_), channel_id=1, source_target_pairs={{0,24},{8,16},{16,8},{24,0},{1,25},{9,17},{17,9},{25,1},{2,26},{10... | collective-permute-start | bytes 393224 | tf_op jit(solution)/shard_map/ppermute | solution.py:16
  7.8 0.6 collective-permute-start.7
  8.5 2.6 %collective-permute-start.2 = (f32[32,1024]{1,0:T(8,128)S(1)}, f32[32,1024]{1,0:T(8,128)S(1)}, u32[]{:S(2)}, u32[]{:S(2)}) collective-permute-start(f32[32,1024]{1,0:T(8,128)S(1)} %bitcast.37), channel_id=1, source_target_pairs={{0,6},{1,7},{2,4},{3,5},{4,2},{5,3},{6,0},{7,1},{8,14},{9,15},{10,... | collective-permute-start | bytes 393224 | tf_op jit(solution)/shard_map/ppermute | solution.py:16
  11.1 1.2 %collective-permute-done.9.refs_3_ = f32[64,512]{1,0:T(8,128)S(1)} collective-permute-done((f32[64,512]{1,0:T(8,128)S(1)}, f32[64,512]{1,0:T(8,128)S(1)}, u32[]{:S(2)}, u32[]{:S(2)}) %collective-permute-start.9) | collective-permute-done | bytes 131104 | tf_op jit(solution)/shard_map/ppermute | solution.py:16
  12.3 1.7 %collective-permute-start.1 = (f32[32,1024]{1,0:T(8,128)S(1)}, f32[32,1024]{1,0:T(8,128)S(1)}, u32[]{:S(2)}, u32[]{:S(2)}) collective-permute-start(f32[32,1024]{1,0:T(8,128)S(1)} %bitcast.38), channel_id=1, source_target_pairs={{0,4},{1,5},{2,6},{3,7},{4,0},{5,1},{6,2},{7,3},{8,12},{9,13},{10,... | collective-permute-start | bytes 393224 | tf_op jit(solution)/shard_map/ppermute | solution.py:16
  14.0 5.6 %collective-permute-done.8.refs_2_ = f32[64,512]{1,0:T(8,128)S(1)} collective-permute-done((f32[64,512]{1,0:T(8,128)S(1)}, f32[64,512]{1,0:T(8,128)S(1)}, u32[]{:S(2)}, u32[]{:S(2)}) %collective-permute-start.8) | collective-permute-done | bytes 131104 | tf_op jit(solution)/shard_map/ppermute | solution.py:16
  19.6 1.5 %collective-permute-start = (f32[32,1024]{1,0:T(8,128)S(1)}, f32[32,1024]{1,0:T(8,128)S(1)}, u32[]{:S(2)}, u32[]{:S(2)}) collective-permute-start(f32[32,1024]{1,0:T(8,128)S(1)} %bitcast.39), channel_id=1, source_target_pairs={{0,2},{1,3},{2,0},{3,1},{4,6},{5,7},{6,4},{7,5},{8,10},{9,11},{10,... | collective-permute-start | bytes 393224 | tf_op jit(solution)/shard_map/ppermute | solution.py:16
  21.2 0.4 shard_map.87
  21.6 3.0 %collective-permute-done.refs_1_ = f32[32,1024]{1,0:T(8,128)S(1)} collective-permute-done((f32[32,1024]{1,0:T(8,128)S(1)}, f32[32,1024]{1,0:T(8,128)S(1)}, u32[]{:S(2)}, u32[]{:S(2)}) %collective-permute-start) | collective-permute-done | bytes 131104 | tf_op jit(solution)/shard_map/ppermute | solution.py:16
  24.6 0.8 %shard_map.88 = (f32[64,512]{1,0:T(8,128)S(1)}, f32[64,512]{1,0:T(8,128)S(1)}) custom-call(f32[32,1024]{1,0:T(8,128)S(1)} %bitcast.40, f32[32,1024]{1,0:T(8,128)S(1)} %collective-permute-done.refs_1_, f32[32,1024]{1,0:T(8,128)S(1)} %collective-permute-done.1.refs_2_, f32[32,1024]{1,0:T(8,128)S(1)} %collective-permute-done.2.refs_3_, ...), custom_call_target="tpu_custom_call" | custom-call | flops 402653184 | bytes 4980736 | tf_op jit(solution)/shard_map/pallas_call | solution.py:24
  25.4 0.8 %shard_map.96 = (f32[64,512]{1,0:T(8,128)S(1)}, f32[64,512]{1,0:T(8,128)S(1)}) custom-call(f32[32,1024]{1,0:T(8,128)S(1)} %bitcast.41, f32[32,1024]{1,0:T(8,128)S(1)} %collective-permute-done.refs_1_, f32[32,1024]{1,0:T(8,128)S(1)} %collective-permute-done.1.refs_2_, f32[32,1024]{1,0:T(8,128)S(1)} %collective-permute-done.2.refs_3_, ...), custom_call_target="tpu_custom_call" | custom-call | flops 402653184 | bytes 4980736 | tf_op jit(solution)/shard_map/pallas_call | solution.py:24
  26.3 2.0 %collective-permute-start.4 = (f32[64,512]{1,0:T(8,128)S(1)}, f32[64,512]{1,0:T(8,128)S(1)}, u32[]{:S(2)}, u32[]{:S(2)}) collective-permute-start(f32[64,512]{1,0:T(8,128)S(1)} %get-tuple-element.34), channel_id=1, source_target_pairs={{0,8},{8,0},{16,24},{24,16},{1,9},{9,1},{17,25},{25,17},{2,10},{10... | collective-permute-start | bytes 393224 | tf_op jit(solution)/shard_map/ppermute | solution.py:16
  28.3 3.6 %collective-permute-done.19 = f32[64,512]{1,0:T(8,128)S(1)} collective-permute-done((f32[64,512]{1,0:T(8,128)S(1)}, f32[64,512]{1,0:T(8,128)S(1)}, u32[]{:S(2)}, u32[]{:S(2)}) %collective-permute-start.19) | collective-permute-done | bytes 131104 | tf_op jit(solution)/shard_map/ppermute | solution.py:16
  31.9 1.8 %collective-permute-start.20 = (f32[64,512]{1,0:T(8,128)S(1)}, f32[64,512]{1,0:T(8,128)S(1)}, u32[]{:S(2)}, u32[]{:S(2)}) collective-permute-start(f32[64,512]{1,0:T(8,128)S(1)} %add.46), channel_id=1, source_target_pairs={{0,16},{8,24},{16,0},{24,8},{1,17},{9,25},{17,1},{25,9},{2,18},{10... | collective-permute-start | bytes 393224 | tf_op jit(solution)/shard_map/ppermute | solution.py:16
  33.8 0.3 collective-permute-done.4
  34.1 2.0 %collective-permute-start.5 = (f32[64,512]{1,0:T(8,128)S(1)}, f32[64,512]{1,0:T(8,128)S(1)}, u32[]{:S(2)}, u32[]{:S(2)}) collective-permute-start(f32[64,512]{1,0:T(8,128)S(1)} %add.40), channel_id=1, source_target_pairs={{0,16},{8,24},{16,0},{24,8},{1,17},{9,25},{17,1},{25,9},{2,18},{10... | collective-permute-start | bytes 393224 | tf_op jit(solution)/shard_map/ppermute | solution.py:16
  36.1 6.9 %collective-permute-done.20 = f32[64,512]{1,0:T(8,128)S(1)} collective-permute-done((f32[64,512]{1,0:T(8,128)S(1)}, f32[64,512]{1,0:T(8,128)S(1)}, u32[]{:S(2)}, u32[]{:S(2)}) %collective-permute-start.20) | collective-permute-done | bytes 131104 | tf_op jit(solution)/shard_map/ppermute | solution.py:16
  43.0 0.2 collective-permute-start.21
  43.2 1.6 %collective-permute-start.17 = (f32[2,40,256]{2,1,0:T(8,128)S(1)}, f32[2,40,256]{2,1,0:T(8,128)S(1)}, u32[]{:S(2)}, u32[]{:S(2)}) collective-permute-start(f32[2,40,256]{2,1,0:T(8,128)S(1)} %pad_maximum_fusion.3), channel_id=1, source_target_pairs={{0,2},{1,3},{2,0},{3,1},{4,6},{5,7},{6,4},{7,5},{8,10},{9,11},{10,... | collective-permute-start | bytes 245768 | tf_op jit(solution)/shard_map/ppermute | solution.py:16
  44.8 0.1 shard_map.90
  44.9 0.1 shard_map.91
  45.0 2.0 %collective-permute-start.6 = (f32[64,512]{1,0:T(8,128)S(1)}, f32[64,512]{1,0:T(8,128)S(1)}, u32[]{:S(2)}, u32[]{:S(2)}) collective-permute-start(f32[64,512]{1,0:T(8,128)S(1)} %add.41.refs_0_), channel_id=1, source_target_pairs={{0,8},{8,0},{16,24},{24,16},{1,9},{9,1},{17,25},{25,17},{2,10},{10... | collective-permute-start | bytes 393224 | tf_op jit(solution)/shard_map/ppermute | solution.py:16
  47.0 2.1 %collective-permute-done.21.refs_1_ = f32[64,512]{1,0:T(8,128)S(1)} collective-permute-done((f32[64,512]{1,0:T(8,128)S(1)}, f32[64,512]{1,0:T(8,128)S(1)}, u32[]{:S(2)}, u32[]{:S(2)}) %collective-permute-start.21) | collective-permute-done | bytes 131104 | tf_op jit(solution)/shard_map/ppermute | solution.py:16
  49.1 1.6 %shard_map.97 = (f32[64,640]{1,0:T(8,128)S(1)}, f32[64,640]{1,0:T(8,128)S(1)}) custom-call(f32[64,512]{1,0:T(8,128)S(1)} %add.47.refs_0_, f32[64,512]{1,0:T(8,128)S(1)} %collective-permute-done.21.refs_1_, bf16[1024,512]{1,0:T(8,128)(2,1)S(1)} %get-tuple-element.29.refs_4_.refs_2_, bf16[1024,512]{1,0:T(8,128)(2,1)S(1)} %get-tuple-element.30.refs_5_.refs_3_, ...), custom_call_target="tpu_custom_call" | custom-call | flops 503316480 | bytes 5832704 | tf_op jit(solution)/shard_map/pallas_call | solution.py:24
  50.7 1.6 %collective-permute-start.22 = (f32[64,640]{1,0:T(8,128)S(1)}, f32[64,640]{1,0:T(8,128)S(1)}, u32[]{:S(2)}, u32[]{:S(2)}) collective-permute-start(f32[64,640]{1,0:T(8,128)S(1)} %get-tuple-element.50), channel_id=1, source_target_pairs={{0,2},{1,3},{2,0},{3,1},{4,6},{5,7},{6,4},{7,5},{8,10},{9,11},{10,... | collective-permute-start | bytes 491528 | tf_op jit(solution)/shard_map/ppermute | solution.py:16
  52.2 1.5 %collective-permute-start.24 = (f32[64,640]{1,0:T(8,128)S(1)}, f32[64,640]{1,0:T(8,128)S(1)}, u32[]{:S(2)}, u32[]{:S(2)}) collective-permute-start(f32[64,640]{1,0:T(8,128)S(1)} %get-tuple-element.51), channel_id=1, source_target_pairs={{0,4},{1,5},{2,6},{3,7},{4,0},{5,1},{6,2},{7,3},{8,12},{9,13},{10,... | collective-permute-start | bytes 491528 | tf_op jit(solution)/shard_map/ppermute | solution.py:16
  53.8 0.6 collective-permute-start.18
  54.3 1.6 %shard_map.92 = (f32[64,640]{1,0:T(8,128)S(1)}, f32[64,640]{1,0:T(8,128)S(1)}) custom-call(f32[64,512]{1,0:T(8,128)S(1)} %add.41.refs_0_, f32[64,512]{1,0:T(8,128)S(1)} %collective-permute-done.6.refs_1_, bf16[1024,512]{1,0:T(8,128)(2,1)S(1)} %get-tuple-element.29.refs_4_.refs_2_, bf16[1024,512]{1,0:T(8,128)(2,1)S(1)} %get-tuple-element.30.refs_5_.refs_3_, ...), custom_call_target="tpu_custom_call" | custom-call | flops 503316480 | bytes 5832704 | tf_op jit(solution)/shard_map/pallas_call | solution.py:24
  55.9 0.6 collective-permute-start.11
  56.5 1.5 %collective-permute-start.13 = (f32[64,640]{1,0:T(8,128)S(1)}, f32[64,640]{1,0:T(8,128)S(1)}, u32[]{:S(2)}, u32[]{:S(2)}) collective-permute-start(f32[64,640]{1,0:T(8,128)S(1)} %get-tuple-element.41), channel_id=1, source_target_pairs={{0,4},{1,5},{2,6},{3,7},{4,0},{5,1},{6,2},{7,3},{8,12},{9,13},{10,... | collective-permute-start | bytes 491528 | tf_op jit(solution)/shard_map/ppermute | solution.py:16
  58.1 0.8 %collective-permute-start.23 = (f32[64,640]{1,0:T(8,128)S(1)}, f32[64,640]{1,0:T(8,128)S(1)}, u32[]{:S(2)}, u32[]{:S(2)}) collective-permute-start(f32[64,640]{1,0:T(8,128)S(1)} %add.48), channel_id=1, source_target_pairs={{0,4},{1,5},{2,6},{3,7},{4,0},{5,1},{6,2},{7,3},{8,12},{9,13},{10,... | collective-permute-start | bytes 491528 | tf_op jit(solution)/shard_map/ppermute | solution.py:16
  58.9 0.4 collective-permute-done.24
  59.3 1.7 %collective-permute-start.25 = (f32[64,640]{1,0:T(8,128)S(1)}, f32[64,640]{1,0:T(8,128)S(1)}, u32[]{:S(2)}, u32[]{:S(2)}) collective-permute-start(f32[64,640]{1,0:T(8,128)S(1)} %add.50), channel_id=1, source_target_pairs={{0,2},{1,3},{2,0},{3,1},{4,6},{5,7},{6,4},{7,5},{8,10},{9,11},{10,... | collective-permute-start | bytes 491528 | tf_op jit(solution)/shard_map/ppermute | solution.py:16
  61.0 2.0 %collective-permute-done.11 = f32[64,640]{1,0:T(8,128)S(1)} collective-permute-done((f32[64,640]{1,0:T(8,128)S(1)}, f32[64,640]{1,0:T(8,128)S(1)}, u32[]{:S(2)}, u32[]{:S(2)}) %collective-permute-start.11) | collective-permute-done | bytes 163872 | tf_op jit(solution)/shard_map/ppermute | solution.py:16
  63.1 1.1 %collective-permute-start.12 = (f32[64,640]{1,0:T(8,128)S(1)}, f32[64,640]{1,0:T(8,128)S(1)}, u32[]{:S(2)}, u32[]{:S(2)}) collective-permute-start(f32[64,640]{1,0:T(8,128)S(1)} %add.42), channel_id=1, source_target_pairs={{0,4},{1,5},{2,6},{3,7},{4,0},{5,1},{6,2},{7,3},{8,12},{9,13},{10,... | collective-permute-start | bytes 491528 | tf_op jit(solution)/shard_map/ppermute | solution.py:16
  64.2 0.6 collective-permute-done.13
  64.8 0.6 collective-permute-start.14
  65.4 1.1 %collective-permute-done.23 = f32[64,640]{1,0:T(8,128)S(1)} collective-permute-done((f32[64,640]{1,0:T(8,128)S(1)}, f32[64,640]{1,0:T(8,128)S(1)}, u32[]{:S(2)}, u32[]{:S(2)}) %collective-permute-start.23) | collective-permute-done | bytes 163872 | tf_op jit(solution)/shard_map/ppermute | solution.py:16
  66.7 0.1 collective-permute-start.26
  66.8 1.7 %collective-permute-done.12 = f32[64,640]{1,0:T(8,128)S(1)} collective-permute-done((f32[64,640]{1,0:T(8,128)S(1)}, f32[64,640]{1,0:T(8,128)S(1)}, u32[]{:S(2)}, u32[]{:S(2)}) %collective-permute-start.12) | collective-permute-done | bytes 163872 | tf_op jit(solution)/shard_map/ppermute | solution.py:16
  68.5 1.8 %collective-permute-done.14 = f32[64,640]{1,0:T(8,128)S(1)} collective-permute-done((f32[64,640]{1,0:T(8,128)S(1)}, f32[64,640]{1,0:T(8,128)S(1)}, u32[]{:S(2)}, u32[]{:S(2)}) %collective-permute-start.14) | collective-permute-done | bytes 163872 | tf_op jit(solution)/shard_map/ppermute | solution.py:16
  70.3 0.1 collective-permute-start.15
  70.5 0.3 shard_map.95
  70.9 3.4 %shard_map.98 = (f32[32,256]{1,0:T(8,128)}, f32[2048,256]{1,0:T(8,128)}) custom-call(f32[64,1280]{1,0:T(8,128)S(1)} %pad_maximum_fusion.1.own_ref, f32[64,1280]{1,0:T(8,128)S(1)} %collective-permute-done.26.other_ref, bf16[256,256]{1,0:T(8,128)(2,1)S(1)} %get-tuple-element.44.ch, bf16[256,256]{1,0:T(8,128)(2,1)S(1)} %get-tuple-element.45.cl, ...), custom_call_target="tpu_custom_call" | custom-call | flops 2415919104 | bytes 7340032 | tf_op jit(solution)/shard_map/pallas_call | solution.py:246
  74.3 3.4 %shard_map.99 = (f32[32,256]{1,0:T(8,128)}, f32[2048,256]{1,0:T(8,128)}) custom-call(f32[64,1280]{1,0:T(8,128)S(1)} %pad_maximum_fusion.own_ref, f32[64,1280]{1,0:T(8,128)S(1)} %collective-permute-done.15.other_ref, bf16[256,256]{1,0:T(8,128)(2,1)S(1)} %get-tuple-element.44.ch, ...), custom_call_target="tpu_custom_call", output_to_operand_aliasing={{0}: (8, {}), {1}: (9, {})} | custom-call | flops 2415919104 | bytes 7340032 | tf_op jit(solution)/shard_map/pallas_call | solution.py:246
  (59 shorter events, 0.8 us)
Async XLA Ops:
  0.6 20.6 %collective-permute-start.3 = (f32[1024,512]{1,0:T(8,128)}, f32[1024,512]{1,0:T(8,128)S(1)}, u32[]{:S(2)}, u32[]{:S(2)}) collective-permute-start(f32[1024,512]{1,0:T(8,128)} %v_ref.1), channel_id=1, source_target_pairs={{0,1},{1,0},{2,3},{3,2},{4,5},{5,4},{6,7},{7,6},{8,9},{9,8},{10,11... | collective-permute-start | bytes 6291464 | tf_op jit(solution)/shard_map/ppermute | solution.py:16
  1.2 1.6 %copy-start.2 = (f32[1024,512]{1,0:T(8,128)S(1)}, f32[1024,512]{1,0:T(8,128)}, u32[]{:S(2)}) copy-start(f32[1024,512]{1,0:T(8,128)} %v_ref.1) | copy-start | bytes 6291460
  2.8 5.7 %copy-start.3 = (f32[1024,32]{0,1:T(8,128)S(1)}, f32[1024,32]{0,1:T(8,128)}, u32[]{:S(2)}) copy-start(f32[1024,32]{0,1:T(8,128)} %param.8) | copy-start | bytes 393220
  3.2 9.1 %collective-permute-start.9 = (f32[64,512]{1,0:T(8,128)S(1)}, f32[64,512]{1,0:T(8,128)S(1)}, u32[]{:S(2)}, u32[]{:S(2)}) collective-permute-start(f32[64,512]{1,0:T(8,128)S(1)} %get-tuple-element.35.refs_0_), channel_id=1, source_target_pairs={{0,24},{8,16},{16,8},{24,0},{1,25},{9,17},{17,9},{25,1},{2,26},{10... | collective-permute-start | bytes 393224 | tf_op jit(solution)/shard_map/ppermute | solution.py:16
  7.8 11.7 %collective-permute-start.8 = (f32[64,512]{1,0:T(8,128)S(1)}, f32[64,512]{1,0:T(8,128)S(1)}, u32[]{:S(2)}, u32[]{:S(2)}) collective-permute-start(f32[64,512]{1,0:T(8,128)S(1)} %get-tuple-element.35.refs_0_), channel_id=1, source_target_pairs={{0,16},{8,24},{16,0},{24,8},{1,17},{9,25},{17,1},{25,9},{2,18},{10... | collective-permute-start | bytes 393224 | tf_op jit(solution)/shard_map/ppermute | solution.py:16
  7.8 13.2 %collective-permute-start.7 = (f32[64,512]{1,0:T(8,128)S(1)}, f32[64,512]{1,0:T(8,128)S(1)}, u32[]{:S(2)}, u32[]{:S(2)}) collective-permute-start(f32[64,512]{1,0:T(8,128)S(1)} %get-tuple-element.35.refs_0_), channel_id=1, source_target_pairs={{0,8},{8,0},{16,24},{24,16},{1,9},{9,1},{17,25},{25,17},{2,10},{10... | collective-permute-start | bytes 393224 | tf_op jit(solution)/shard_map/ppermute | solution.py:16
  8.5 13.1 %collective-permute-start.2 = (f32[32,1024]{1,0:T(8,128)S(1)}, f32[32,1024]{1,0:T(8,128)S(1)}, u32[]{:S(2)}, u32[]{:S(2)}) collective-permute-start(f32[32,1024]{1,0:T(8,128)S(1)} %bitcast.37), channel_id=1, source_target_pairs={{0,6},{1,7},{2,4},{3,5},{4,2},{5,3},{6,0},{7,1},{8,14},{9,15},{10,... | collective-permute-start | bytes 393224 | tf_op jit(solution)/shard_map/ppermute | solution.py:16
  12.3 9.3 %collective-permute-start.1 = (f32[32,1024]{1,0:T(8,128)S(1)}, f32[32,1024]{1,0:T(8,128)S(1)}, u32[]{:S(2)}, u32[]{:S(2)}) collective-permute-start(f32[32,1024]{1,0:T(8,128)S(1)} %bitcast.38), channel_id=1, source_target_pairs={{0,4},{1,5},{2,6},{3,7},{4,0},{5,1},{6,2},{7,3},{8,12},{9,13},{10,... | collective-permute-start | bytes 393224 | tf_op jit(solution)/shard_map/ppermute | solution.py:16
  19.6 5.0 %collective-permute-start = (f32[32,1024]{1,0:T(8,128)S(1)}, f32[32,1024]{1,0:T(8,128)S(1)}, u32[]{:S(2)}, u32[]{:S(2)}) collective-permute-start(f32[32,1024]{1,0:T(8,128)S(1)} %bitcast.39), channel_id=1, source_target_pairs={{0,2},{1,3},{2,0},{3,1},{4,6},{5,7},{6,4},{7,5},{8,10},{9,11},{10,... | collective-permute-start | bytes 393224 | tf_op jit(solution)/shard_map/ppermute | solution.py:16
  21.1 23.7 %collective-permute-start.10 = (f32[256,512]{1,0:T(8,128)S(1)}, f32[256,512]{1,0:T(8,128)S(1)}, u32[]{:S(2)}, u32[]{:S(2)}) collective-permute-start(f32[256,512]{1,0:T(8,128)S(1)} %shard_map.89.v_ref), channel_id=1, source_target_pairs={{0,1},{1,0},{2,3},{3,2},{4,5},{5,4},{6,7},{7,6},{8,9},{9,8},{10,11... | collective-permute-start | bytes 1572872 | tf_op jit(solution)/shard_map/ppermute | solution.py:16
  25.4 2.9 %copy-start.6 = (s32[88,1]{0,1:T(1,128)S(1)}, s32[88,1]{0,1:T(1,128)}, u32[]{:S(2)}) copy-start(s32[88,1]{0,1:T(1,128)} %param.9) | copy-start | bytes 1060
  25.4 8.3 %copy-start.5 = (f32[1,32,256]{2,1,0:T(8,128)S(1)}, f32[1,32,256]{2,1,0:T(8,128)}, u32[]{:S(2)}) copy-start(f32[1,32,256]{2,1,0:T(8,128)} %param.10) | copy-start | bytes 98308
  26.2 5.7 %collective-permute-start.19 = (f32[64,512]{1,0:T(8,128)S(1)}, f32[64,512]{1,0:T(8,128)S(1)}, u32[]{:S(2)}, u32[]{:S(2)}) collective-permute-start(f32[64,512]{1,0:T(8,128)S(1)} %get-tuple-element.49), channel_id=1, source_target_pairs={{0,8},{8,0},{16,24},{24,16},{1,9},{9,1},{17,25},{25,17},{2,10},{10... | collective-permute-start | bytes 393224 | tf_op jit(solution)/shard_map/ppermute | solution.py:16
  26.3 7.8 %collective-permute-start.4 = (f32[64,512]{1,0:T(8,128)S(1)}, f32[64,512]{1,0:T(8,128)S(1)}, u32[]{:S(2)}, u32[]{:S(2)}) collective-permute-start(f32[64,512]{1,0:T(8,128)S(1)} %get-tuple-element.34), channel_id=1, source_target_pairs={{0,8},{8,0},{16,24},{24,16},{1,9},{9,1},{17,25},{25,17},{2,10},{10... | collective-permute-start | bytes 393224 | tf_op jit(solution)/shard_map/ppermute | solution.py:16
  31.9 11.1 %collective-permute-start.20 = (f32[64,512]{1,0:T(8,128)S(1)}, f32[64,512]{1,0:T(8,128)S(1)}, u32[]{:S(2)}, u32[]{:S(2)}) collective-permute-start(f32[64,512]{1,0:T(8,128)S(1)} %add.46), channel_id=1, source_target_pairs={{0,16},{8,24},{16,0},{24,8},{1,17},{9,25},{17,1},{25,9},{2,18},{10... | collective-permute-start | bytes 393224 | tf_op jit(solution)/shard_map/ppermute | solution.py:16
  33.7 9.5 %collective-permute-start.16 = (f32[1,40,256]{2,1,0:T(8,128)S(1)}, f32[1,40,256]{2,1,0:T(8,128)S(1)}, u32[]{:S(2)}, u32[]{:S(2)}) collective-permute-start(f32[1,40,256]{2,1,0:T(8,128)S(1)} %get-tuple-element.62), channel_id=1, source_target_pairs={{0,1},{1,0},{2,3},{3,2},{4,5},{5,4},{6,7},{7,6},{8,9},{9,8},{10,11... | collective-permute-start | bytes 122888 | tf_op jit(solution)/shard_map/ppermute | solution.py:16
  34.1 10.8 %collective-permute-start.5 = (f32[64,512]{1,0:T(8,128)S(1)}, f32[64,512]{1,0:T(8,128)S(1)}, u32[]{:S(2)}, u32[]{:S(2)}) collective-permute-start(f32[64,512]{1,0:T(8,128)S(1)} %add.40), channel_id=1, source_target_pairs={{0,16},{8,24},{16,0},{24,8},{1,17},{9,25},{17,1},{25,9},{2,18},{10... | collective-permute-start | bytes 393224 | tf_op jit(solution)/shard_map/ppermute | solution.py:16
  43.0 6.1 %collective-permute-start.21 = (f32[64,512]{1,0:T(8,128)S(1)}, f32[64,512]{1,0:T(8,128)S(1)}, u32[]{:S(2)}, u32[]{:S(2)}) collective-permute-start(f32[64,512]{1,0:T(8,128)S(1)} %add.47.refs_0_), channel_id=1, source_target_pairs={{0,8},{8,0},{16,24},{24,16},{1,9},{9,1},{17,25},{25,17},{2,10},{10... | collective-permute-start | bytes 393224 | tf_op jit(solution)/shard_map/ppermute | solution.py:16
  43.2 10.5 %collective-permute-start.17 = (f32[2,40,256]{2,1,0:T(8,128)S(1)}, f32[2,40,256]{2,1,0:T(8,128)S(1)}, u32[]{:S(2)}, u32[]{:S(2)}) collective-permute-start(f32[2,40,256]{2,1,0:T(8,128)S(1)} %pad_maximum_fusion.3), channel_id=1, source_target_pairs={{0,2},{1,3},{2,0},{3,1},{4,6},{5,7},{6,4},{7,5},{8,10},{9,11},{10,... | collective-permute-start | bytes 245768 | tf_op jit(solution)/shard_map/ppermute | solution.py:16
  45.0 9.3 %collective-permute-start.6 = (f32[64,512]{1,0:T(8,128)S(1)}, f32[64,512]{1,0:T(8,128)S(1)}, u32[]{:S(2)}, u32[]{:S(2)}) collective-permute-start(f32[64,512]{1,0:T(8,128)S(1)} %add.41.refs_0_), channel_id=1, source_target_pairs={{0,8},{8,0},{16,24},{24,16},{1,9},{9,1},{17,25},{25,17},{2,10},{10... | collective-permute-start | bytes 393224 | tf_op jit(solution)/shard_map/ppermute | solution.py:16
  50.7 7.4 %collective-permute-start.22 = (f32[64,640]{1,0:T(8,128)S(1)}, f32[64,640]{1,0:T(8,128)S(1)}, u32[]{:S(2)}, u32[]{:S(2)}) collective-permute-start(f32[64,640]{1,0:T(8,128)S(1)} %get-tuple-element.50), channel_id=1, source_target_pairs={{0,2},{1,3},{2,0},{3,1},{4,6},{5,7},{6,4},{7,5},{8,10},{9,11},{10,... | collective-permute-start | bytes 491528 | tf_op jit(solution)/shard_map/ppermute | solution.py:16
  52.2 7.1 %collective-permute-start.24 = (f32[64,640]{1,0:T(8,128)S(1)}, f32[64,640]{1,0:T(8,128)S(1)}, u32[]{:S(2)}, u32[]{:S(2)}) collective-permute-start(f32[64,640]{1,0:T(8,128)S(1)} %get-tuple-element.51), channel_id=1, source_target_pairs={{0,4},{1,5},{2,6},{3,7},{4,0},{5,1},{6,2},{7,3},{8,12},{9,13},{10,... | collective-permute-start | bytes 491528 | tf_op jit(solution)/shard_map/ppermute | solution.py:16
  53.8 16.6 %collective-permute-start.18 = (f32[4,40,256]{2,1,0:T(8,128)S(1)}, f32[4,40,256]{2,1,0:T(8,128)S(1)}, u32[]{:S(2)}, u32[]{:S(2)}) collective-permute-start(f32[4,40,256]{2,1,0:T(8,128)S(1)} %pad_maximum_fusion.2), channel_id=1, source_target_pairs={{0,4},{1,5},{2,6},{3,7},{4,0},{5,1},{6,2},{7,3},{8,12},{9,13},{10,... | collective-permute-start | bytes 491528 | tf_op jit(solution)/shard_map/ppermute | solution.py:16
  55.9 7.1 %collective-permute-start.11 = (f32[64,640]{1,0:T(8,128)S(1)}, f32[64,640]{1,0:T(8,128)S(1)}, u32[]{:S(2)}, u32[]{:S(2)}) collective-permute-start(f32[64,640]{1,0:T(8,128)S(1)} %get-tuple-element.40), channel_id=1, source_target_pairs={{0,2},{1,3},{2,0},{3,1},{4,6},{5,7},{6,4},{7,5},{8,10},{9,11},{10,... | collective-permute-start | bytes 491528 | tf_op jit(solution)/shard_map/ppermute | solution.py:16
  56.5 8.3 %collective-permute-start.13 = (f32[64,640]{1,0:T(8,128)S(1)}, f32[64,640]{1,0:T(8,128)S(1)}, u32[]{:S(2)}, u32[]{:S(2)}) collective-permute-start(f32[64,640]{1,0:T(8,128)S(1)} %get-tuple-element.41), channel_id=1, source_target_pairs={{0,4},{1,5},{2,6},{3,7},{4,0},{5,1},{6,2},{7,3},{8,12},{9,13},{10,... | collective-permute-start | bytes 491528 | tf_op jit(solution)/shard_map/ppermute | solution.py:16
  58.1 8.5 %collective-permute-start.23 = (f32[64,640]{1,0:T(8,128)S(1)}, f32[64,640]{1,0:T(8,128)S(1)}, u32[]{:S(2)}, u32[]{:S(2)}) collective-permute-start(f32[64,640]{1,0:T(8,128)S(1)} %add.48), channel_id=1, source_target_pairs={{0,4},{1,5},{2,6},{3,7},{4,0},{5,1},{6,2},{7,3},{8,12},{9,13},{10,... | collective-permute-start | bytes 491528 | tf_op jit(solution)/shard_map/ppermute | solution.py:16
  59.3 11.6 %copy-start.1 = (f32[1,1,2048,256]{3,2,1,0:T(8,128)S(1)}, f32[1,1,2048,256]{3,2,1,0:T(8,128)}, u32[]{:S(2)}) copy-start(f32[1,1,2048,256]{3,2,1,0:T(8,128)} %param.12) | copy-start | bytes 6291460
  59.3 7.3 %collective-permute-start.25 = (f32[64,640]{1,0:T(8,128)S(1)}, f32[64,640]{1,0:T(8,128)S(1)}, u32[]{:S(2)}, u32[]{:S(2)}) collective-permute-start(f32[64,640]{1,0:T(8,128)S(1)} %add.50), channel_id=1, source_target_pairs={{0,2},{1,3},{2,0},{3,1},{4,6},{5,7},{6,4},{7,5},{8,10},{9,11},{10,... | collective-permute-start | bytes 491528 | tf_op jit(solution)/shard_map/ppermute | solution.py:16
  63.1 5.4 %collective-permute-start.12 = (f32[64,640]{1,0:T(8,128)S(1)}, f32[64,640]{1,0:T(8,128)S(1)}, u32[]{:S(2)}, u32[]{:S(2)}) collective-permute-start(f32[64,640]{1,0:T(8,128)S(1)} %add.42), channel_id=1, source_target_pairs={{0,4},{1,5},{2,6},{3,7},{4,0},{5,1},{6,2},{7,3},{8,12},{9,13},{10,... | collective-permute-start | bytes 491528 | tf_op jit(solution)/shard_map/ppermute | solution.py:16
  64.8 5.4 %collective-permute-start.14 = (f32[64,640]{1,0:T(8,128)S(1)}, f32[64,640]{1,0:T(8,128)S(1)}, u32[]{:S(2)}, u32[]{:S(2)}) collective-permute-start(f32[64,640]{1,0:T(8,128)S(1)} %add.44), channel_id=1, source_target_pairs={{0,2},{1,3},{2,0},{3,1},{4,6},{5,7},{6,4},{7,5},{8,10},{9,11},{10,... | collective-permute-start | bytes 491528 | tf_op jit(solution)/shard_map/ppermute | solution.py:16
  66.6 4.3 %copy-start = (f32[1,1,2048,512]{3,2,1,0:T(8,128)S(1)}, f32[1,1,2048,512]{3,2,1,0:T(8,128)}, u32[]{:S(2)}) copy-start(f32[1,1,2048,512]{3,2,1,0:T(8,128)} %param.13) | copy-start | bytes 12582916
  66.6 3.9 %copy-start.4 = (s32[1,1,512]{2,1,0:T(1,128)S(1)}, s32[1,1,512]{2,1,0:T(1,128)}, u32[]{:S(2)}) copy-start(s32[1,1,512]{2,1,0:T(1,128)} %param.11) | copy-start | bytes 6148
  66.7 4.2 %collective-permute-start.26 = (f32[64,1280]{1,0:T(8,128)S(1)}, f32[64,1280]{1,0:T(8,128)S(1)}, u32[]{:S(2)}, u32[]{:S(2)}) collective-permute-start(f32[64,1280]{1,0:T(8,128)S(1)} %pad_maximum_fusion.1.own_ref), channel_id=1, source_target_pairs={{0,1},{1,0},{2,3},{3,2},{4,5},{5,4},{6,7},{7,6},{8,9},{9,8},{10,11... | collective-permute-start | bytes 983048 | tf_op jit(solution)/shard_map/ppermute | solution.py:16
  70.3 4.0 %collective-permute-start.15 = (f32[64,1280]{1,0:T(8,128)S(1)}, f32[64,1280]{1,0:T(8,128)S(1)}, u32[]{:S(2)}, u32[]{:S(2)}) collective-permute-start(f32[64,1280]{1,0:T(8,128)S(1)} %pad_maximum_fusion.own_ref), channel_id=1, source_target_pairs={{0,1},{1,0},{2,3},{3,2},{4,5},{5,4},{6,7},{7,6},{8,9},{9,8},{10,11... | collective-permute-start | bytes 983048 | tf_op jit(solution)/shard_map/ppermute | solution.py:16

commit v6 on v5

--- a/solution.py
+++ b/solution.py
@@ -195,7 +195,7 @@
     seps = fanout * sep_local
     count = cons.shape[1]
     nv = 2 * n
-    tile = 256
+    tile = 128
     low = n * parts // nblocks
 
     def body(own_ref, other_ref, ch, cl, p_ref, q_ref, l_ref, c_ref, *rest):
@@ -258,9 +258,7 @@
             pltpu.SemaphoreType.DMA((tiles + 1,)),
         ],
         input_output_aliases={8 + i: i for i in range(len(prior))},
-        compiler_params=pltpu.CompilerParams(
-            vmem_limit_bytes=sum(a.size * a.dtype.itemsize for a in args) + (8 << 20)
-        ),
+        compiler_params=pltpu.CompilerParams(vmem_limit_bytes=sum(a.size * a.dtype.itemsize for a in args) + (8 << 20)),
         cost_estimate=pl.CostEstimate(
             flops=12 * inter * (modes + count) * nv,
             bytes_accessed=4 * inter * (modes + count + nv),

time: 77.9 us -> 78 us (level)
  no operation moved by 1% of the time
where the time goes in v6:
time: 78 us; the launch traced here: 77.9 us
  starting transfers between devices  31.5 us (40%)
  waiting for transfers between devices  30.3 us (39%)
  Pallas kernels  13 us (17%)
  local copies, waits for them, and re-layouts  1.68 us (2%)
  between operations  1.01 us (1%)
    ppermute x27, starting transfers between devices, swap(): return lax.ppermute(v, axis, [(i, i ^ mask) for i in range(n)])  31.5 us
    ppermute x27, waiting for transfers between devices, swap(): return lax.ppermute(v, axis, [(i, i ^ mask) for i in range(n)])  30.3 us
    pallas_call x2, Pallas kernels, expand(): pl.pallas_call(body, out_shape=[shape((sep_local, nv * parts)), shape((in...  6.97 us
    pallas_call x12, Pallas kernels, call(): pl.pallas_call(body, out_shape=out, in_specs=specs, out_specs=[pl.BlockSp...  6.08 us
    unnamed x15, local copies, waits for them, and re-layouts  1.63 us
  transfers between devices with their start and end apart: 27, of which 13 were waited for; matrix products, arithmetic and copies ran while one was open for 0% of the time, Pallas kernels for 12%

profile of v6, /device:TPU:0, one launch (start us, length us, event | category | flops | bytes accessed | tf_op | source)
XLA Modules:
  0.0 77.9 jit_solution(13862201321646202202)
XLA Ops:
  0.6 0.6 collective-permute-start.3
  1.2 1.6 %copy-done.2 = f32[1024,512]{1,0:T(8,128)S(1)} copy-done((f32[1024,512]{1,0:T(8,128)S(1)}, f32[1024,512]{1,0:T(8,128)}, u32[]{:S(2)}) %copy-start.2) | copy-done | bytes 2097176
  2.8 0.4 shard_map.86
  3.2 4.7 %collective-permute-start.9 = (f32[64,512]{1,0:T(8,128)S(1)}, f32[64,512]{1,0:T(8,128)S(1)}, u32[]{:S(2)}, u32[]{:S(2)}) collective-permute-start(f32[64,512]{1,0:T(8,128)S(1)} %get-tuple-element.35.refs_0_), channel_id=1, source_target_pairs={{0,24},{8,16},{16,8},{24,0},{1,25},{9,17},{17,9},{25,1},{2,26},{10... | collective-permute-start | bytes 393224 | tf_op jit(solution)/shard_map/ppermute | solution.py:16
  7.8 0.6 collective-permute-start.7
  8.5 2.6 %collective-permute-start.2 = (f32[32,1024]{1,0:T(8,128)S(1)}, f32[32,1024]{1,0:T(8,128)S(1)}, u32[]{:S(2)}, u32[]{:S(2)}) collective-permute-start(f32[32,1024]{1,0:T(8,128)S(1)} %bitcast.37), channel_id=1, source_target_pairs={{0,6},{1,7},{2,4},{3,5},{4,2},{5,3},{6,0},{7,1},{8,14},{9,15},{10,... | collective-permute-start | bytes 393224 | tf_op jit(solution)/shard_map/ppermute | solution.py:16
  11.1 1.2 %collective-permute-done.9.refs_3_ = f32[64,512]{1,0:T(8,128)S(1)} collective-permute-done((f32[64,512]{1,0:T(8,128)S(1)}, f32[64,512]{1,0:T(8,128)S(1)}, u32[]{:S(2)}, u32[]{:S(2)}) %collective-permute-start.9) | collective-permute-done | bytes 131104 | tf_op jit(solution)/shard_map/ppermute | solution.py:16
  12.3 1.7 %collective-permute-start.1 = (f32[32,1024]{1,0:T(8,128)S(1)}, f32[32,1024]{1,0:T(8,128)S(1)}, u32[]{:S(2)}, u32[]{:S(2)}) collective-permute-start(f32[32,1024]{1,0:T(8,128)S(1)} %bitcast.38), channel_id=1, source_target_pairs={{0,4},{1,5},{2,6},{3,7},{4,0},{5,1},{6,2},{7,3},{8,12},{9,13},{10,... | collective-permute-start | bytes 393224 | tf_op jit(solution)/shard_map/ppermute | solution.py:16
  14.0 5.6 %collective-permute-done.8.refs_2_ = f32[64,512]{1,0:T(8,128)S(1)} collective-permute-done((f32[64,512]{1,0:T(8,128)S(1)}, f32[64,512]{1,0:T(8,128)S(1)}, u32[]{:S(2)}, u32[]{:S(2)}) %collective-permute-start.8) | collective-permute-done | bytes 131104 | tf_op jit(solution)/shard_map/ppermute | solution.py:16
  19.6 1.5 %collective-permute-start = (f32[32,1024]{1,0:T(8,128)S(1)}, f32[32,1024]{1,0:T(8,128)S(1)}, u32[]{:S(2)}, u32[]{:S(2)}) collective-permute-start(f32[32,1024]{1,0:T(8,128)S(1)} %bitcast.39), channel_id=1, source_target_pairs={{0,2},{1,3},{2,0},{3,1},{4,6},{5,7},{6,4},{7,5},{8,10},{9,11},{10,... | collective-permute-start | bytes 393224 | tf_op jit(solution)/shard_map/ppermute | solution.py:16
  21.2 0.4 shard_map.87
  21.6 3.0 %collective-permute-done.refs_1_ = f32[32,1024]{1,0:T(8,128)S(1)} collective-permute-done((f32[32,1024]{1,0:T(8,128)S(1)}, f32[32,1024]{1,0:T(8,128)S(1)}, u32[]{:S(2)}, u32[]{:S(2)}) %collective-permute-start) | collective-permute-done | bytes 131104 | tf_op jit(solution)/shard_map/ppermute | solution.py:16
  24.6 0.8 %shard_map.88 = (f32[64,512]{1,0:T(8,128)S(1)}, f32[64,512]{1,0:T(8,128)S(1)}) custom-call(f32[32,1024]{1,0:T(8,128)S(1)} %bitcast.40, f32[32,1024]{1,0:T(8,128)S(1)} %collective-permute-done.refs_1_, f32[32,1024]{1,0:T(8,128)S(1)} %collective-permute-done.1.refs_2_, f32[32,1024]{1,0:T(8,128)S(1)} %collective-permute-done.2.refs_3_, ...), custom_call_target="tpu_custom_call" | custom-call | flops 402653184 | bytes 4980736 | tf_op jit(solution)/shard_map/pallas_call | solution.py:24
  25.4 0.8 %shard_map.96 = (f32[64,512]{1,0:T(8,128)S(1)}, f32[64,512]{1,0:T(8,128)S(1)}) custom-call(f32[32,1024]{1,0:T(8,128)S(1)} %bitcast.41, f32[32,1024]{1,0:T(8,128)S(1)} %collective-permute-done.refs_1_, f32[32,1024]{1,0:T(8,128)S(1)} %collective-permute-done.1.refs_2_, f32[32,1024]{1,0:T(8,128)S(1)} %collective-permute-done.2.refs_3_, ...), custom_call_target="tpu_custom_call" | custom-call | flops 402653184 | bytes 4980736 | tf_op jit(solution)/shard_map/pallas_call | solution.py:24
  26.3 2.0 %collective-permute-start.4 = (f32[64,512]{1,0:T(8,128)S(1)}, f32[64,512]{1,0:T(8,128)S(1)}, u32[]{:S(2)}, u32[]{:S(2)}) collective-permute-start(f32[64,512]{1,0:T(8,128)S(1)} %get-tuple-element.34), channel_id=1, source_target_pairs={{0,8},{8,0},{16,24},{24,16},{1,9},{9,1},{17,25},{25,17},{2,10},{10... | collective-permute-start | bytes 393224 | tf_op jit(solution)/shard_map/ppermute | solution.py:16
  28.3 3.6 %collective-permute-done.19 = f32[64,512]{1,0:T(8,128)S(1)} collective-permute-done((f32[64,512]{1,0:T(8,128)S(1)}, f32[64,512]{1,0:T(8,128)S(1)}, u32[]{:S(2)}, u32[]{:S(2)}) %collective-permute-start.19) | collective-permute-done | bytes 131104 | tf_op jit(solution)/shard_map/ppermute | solution.py:16
  31.9 1.8 %collective-permute-start.20 = (f32[64,512]{1,0:T(8,128)S(1)}, f32[64,512]{1,0:T(8,128)S(1)}, u32[]{:S(2)}, u32[]{:S(2)}) collective-permute-start(f32[64,512]{1,0:T(8,128)S(1)} %add.46), channel_id=1, source_target_pairs={{0,16},{8,24},{16,0},{24,8},{1,17},{9,25},{17,1},{25,9},{2,18},{10... | collective-permute-start | bytes 393224 | tf_op jit(solution)/shard_map/ppermute | solution.py:16
  33.8 0.3 collective-permute-done.4
  34.1 2.0 %collective-permute-start.5 = (f32[64,512]{1,0:T(8,128)S(1)}, f32[64,512]{1,0:T(8,128)S(1)}, u32[]{:S(2)}, u32[]{:S(2)}) collective-permute-start(f32[64,512]{1,0:T(8,128)S(1)} %add.40), channel_id=1, source_target_pairs={{0,16},{8,24},{16,0},{24,8},{1,17},{9,25},{17,1},{25,9},{2,18},{10... | collective-permute-start | bytes 393224 | tf_op jit(solution)/shard_map/ppermute | solution.py:16
  36.1 6.9 %collective-permute-done.20 = f32[64,512]{1,0:T(8,128)S(1)} collective-permute-done((f32[64,512]{1,0:T(8,128)S(1)}, f32[64,512]{1,0:T(8,128)S(1)}, u32[]{:S(2)}, u32[]{:S(2)}) %collective-permute-start.20) | collective-permute-done | bytes 131104 | tf_op jit(solution)/shard_map/ppermute | solution.py:16
  43.0 0.2 collective-permute-start.21
  43.2 1.6 %collective-permute-start.17 = (f32[2,40,256]{2,1,0:T(8,128)S(1)}, f32[2,40,256]{2,1,0:T(8,128)S(1)}, u32[]{:S(2)}, u32[]{:S(2)}) collective-permute-start(f32[2,40,256]{2,1,0:T(8,128)S(1)} %pad_maximum_fusion.3), channel_id=1, source_target_pairs={{0,2},{1,3},{2,0},{3,1},{4,6},{5,7},{6,4},{7,5},{8,10},{9,11},{10,... | collective-permute-start | bytes 245768 | tf_op jit(solution)/shard_map/ppermute | solution.py:16
  44.8 0.1 shard_map.90
  44.9 0.1 shard_map.91
  45.0 2.0 %collective-permute-start.6 = (f32[64,512]{1,0:T(8,128)S(1)}, f32[64,512]{1,0:T(8,128)S(1)}, u32[]{:S(2)}, u32[]{:S(2)}) collective-permute-start(f32[64,512]{1,0:T(8,128)S(1)} %add.41.refs_0_), channel_id=1, source_target_pairs={{0,8},{8,0},{16,24},{24,16},{1,9},{9,1},{17,25},{25,17},{2,10},{10... | collective-permute-start | bytes 393224 | tf_op jit(solution)/shard_map/ppermute | solution.py:16
  47.0 2.1 %collective-permute-done.21.refs_1_ = f32[64,512]{1,0:T(8,128)S(1)} collective-permute-done((f32[64,512]{1,0:T(8,128)S(1)}, f32[64,512]{1,0:T(8,128)S(1)}, u32[]{:S(2)}, u32[]{:S(2)}) %collective-permute-start.21) | collective-permute-done | bytes 131104 | tf_op jit(solution)/shard_map/ppermute | solution.py:16
  49.1 1.6 %shard_map.97 = (f32[64,640]{1,0:T(8,128)S(1)}, f32[64,640]{1,0:T(8,128)S(1)}) custom-call(f32[64,512]{1,0:T(8,128)S(1)} %add.47.refs_0_, f32[64,512]{1,0:T(8,128)S(1)} %collective-permute-done.21.refs_1_, bf16[1024,512]{1,0:T(8,128)(2,1)S(1)} %get-tuple-element.29.refs_4_.refs_2_, bf16[1024,512]{1,0:T(8,128)(2,1)S(1)} %get-tuple-element.30.refs_5_.refs_3_, ...), custom_call_target="tpu_custom_call" | custom-call | flops 503316480 | bytes 5832704 | tf_op jit(solution)/shard_map/pallas_call | solution.py:24
  50.7 1.6 %collective-permute-start.22 = (f32[64,640]{1,0:T(8,128)S(1)}, f32[64,640]{1,0:T(8,128)S(1)}, u32[]{:S(2)}, u32[]{:S(2)}) collective-permute-start(f32[64,640]{1,0:T(8,128)S(1)} %get-tuple-element.50), channel_id=1, source_target_pairs={{0,2},{1,3},{2,0},{3,1},{4,6},{5,7},{6,4},{7,5},{8,10},{9,11},{10,... | collective-permute-start | bytes 491528 | tf_op jit(solution)/shard_map/ppermute | solution.py:16
  52.2 1.5 %collective-permute-start.24 = (f32[64,640]{1,0:T(8,128)S(1)}, f32[64,640]{1,0:T(8,128)S(1)}, u32[]{:S(2)}, u32[]{:S(2)}) collective-permute-start(f32[64,640]{1,0:T(8,128)S(1)} %get-tuple-element.51), channel_id=1, source_target_pairs={{0,4},{1,5},{2,6},{3,7},{4,0},{5,1},{6,2},{7,3},{8,12},{9,13},{10,... | collective-permute-start | bytes 491528 | tf_op jit(solution)/shard_map/ppermute | solution.py:16
  53.8 0.6 collective-permute-start.18
  54.3 1.6 %shard_map.92 = (f32[64,640]{1,0:T(8,128)S(1)}, f32[64,640]{1,0:T(8,128)S(1)}) custom-call(f32[64,512]{1,0:T(8,128)S(1)} %add.41.refs_0_, f32[64,512]{1,0:T(8,128)S(1)} %collective-permute-done.6.refs_1_, bf16[1024,512]{1,0:T(8,128)(2,1)S(1)} %get-tuple-element.29.refs_4_.refs_2_, bf16[1024,512]{1,0:T(8,128)(2,1)S(1)} %get-tuple-element.30.refs_5_.refs_3_, ...), custom_call_target="tpu_custom_call" | custom-call | flops 503316480 | bytes 5832704 | tf_op jit(solution)/shard_map/pallas_call | solution.py:24
  55.9 0.6 collective-permute-start.11
  56.5 1.5 %collective-permute-start.13 = (f32[64,640]{1,0:T(8,128)S(1)}, f32[64,640]{1,0:T(8,128)S(1)}, u32[]{:S(2)}, u32[]{:S(2)}) collective-permute-start(f32[64,640]{1,0:T(8,128)S(1)} %get-tuple-element.41), channel_id=1, source_target_pairs={{0,4},{1,5},{2,6},{3,7},{4,0},{5,1},{6,2},{7,3},{8,12},{9,13},{10,... | collective-permute-start | bytes 491528 | tf_op jit(solution)/shard_map/ppermute | solution.py:16
  58.1 0.8 %collective-permute-start.23 = (f32[64,640]{1,0:T(8,128)S(1)}, f32[64,640]{1,0:T(8,128)S(1)}, u32[]{:S(2)}, u32[]{:S(2)}) collective-permute-start(f32[64,640]{1,0:T(8,128)S(1)} %add.48), channel_id=1, source_target_pairs={{0,4},{1,5},{2,6},{3,7},{4,0},{5,1},{6,2},{7,3},{8,12},{9,13},{10,... | collective-permute-start | bytes 491528 | tf_op jit(solution)/shard_map/ppermute | solution.py:16
  58.9 0.4 collective-permute-done.24
  59.3 1.7 %collective-permute-start.25 = (f32[64,640]{1,0:T(8,128)S(1)}, f32[64,640]{1,0:T(8,128)S(1)}, u32[]{:S(2)}, u32[]{:S(2)}) collective-permute-start(f32[64,640]{1,0:T(8,128)S(1)} %add.50), channel_id=1, source_target_pairs={{0,2},{1,3},{2,0},{3,1},{4,6},{5,7},{6,4},{7,5},{8,10},{9,11},{10,... | collective-permute-start | bytes 491528 | tf_op jit(solution)/shard_map/ppermute | solution.py:16
  61.0 2.0 %collective-permute-done.11 = f32[64,640]{1,0:T(8,128)S(1)} collective-permute-done((f32[64,640]{1,0:T(8,128)S(1)}, f32[64,640]{1,0:T(8,128)S(1)}, u32[]{:S(2)}, u32[]{:S(2)}) %collective-permute-start.11) | collective-permute-done | bytes 163872 | tf_op jit(solution)/shard_map/ppermute | solution.py:16
  63.1 1.1 %collective-permute-start.12 = (f32[64,640]{1,0:T(8,128)S(1)}, f32[64,640]{1,0:T(8,128)S(1)}, u32[]{:S(2)}, u32[]{:S(2)}) collective-permute-start(f32[64,640]{1,0:T(8,128)S(1)} %add.42), channel_id=1, source_target_pairs={{0,4},{1,5},{2,6},{3,7},{4,0},{5,1},{6,2},{7,3},{8,12},{9,13},{10,... | collective-permute-start | bytes 491528 | tf_op jit(solution)/shard_map/ppermute | solution.py:16
  64.2 0.6 collective-permute-done.13
  64.8 0.6 collective-permute-start.14
  65.4 1.1 %collective-permute-done.23 = f32[64,640]{1,0:T(8,128)S(1)} collective-permute-done((f32[64,640]{1,0:T(8,128)S(1)}, f32[64,640]{1,0:T(8,128)S(1)}, u32[]{:S(2)}, u32[]{:S(2)}) %collective-permute-start.23) | collective-permute-done | bytes 163872 | tf_op jit(solution)/shard_map/ppermute | solution.py:16
  66.7 0.1 collective-permute-start.26
  66.8 1.7 %collective-permute-done.12 = f32[64,640]{1,0:T(8,128)S(1)} collective-permute-done((f32[64,640]{1,0:T(8,128)S(1)}, f32[64,640]{1,0:T(8,128)S(1)}, u32[]{:S(2)}, u32[]{:S(2)}) %collective-permute-start.12) | collective-permute-done | bytes 163872 | tf_op jit(solution)/shard_map/ppermute | solution.py:16
  68.5 1.8 %collective-permute-done.14 = f32[64,640]{1,0:T(8,128)S(1)} collective-permute-done((f32[64,640]{1,0:T(8,128)S(1)}, f32[64,640]{1,0:T(8,128)S(1)}, u32[]{:S(2)}, u32[]{:S(2)}) %collective-permute-start.14) | collective-permute-done | bytes 163872 | tf_op jit(solution)/shard_map/ppermute | solution.py:16
  70.3 0.1 collective-permute-start.15
  70.5 0.3 shard_map.95
  70.9 3.5 %shard_map.98 = (f32[32,256]{1,0:T(8,128)}, f32[2048,256]{1,0:T(8,128)}) custom-call(f32[64,1280]{1,0:T(8,128)S(1)} %pad_maximum_fusion.1.own_ref, f32[64,1280]{1,0:T(8,128)S(1)} %collective-permute-done.26.other_ref, bf16[256,256]{1,0:T(8,128)(2,1)S(1)} %get-tuple-element.44.ch, bf16[256,256]{1,0:T(8,128)(2,1)S(1)} %get-tuple-element.45.cl, ...), custom_call_target="tpu_custom_call" | custom-call | flops 2415919104 | bytes 7340032 | tf_op jit(solution)/shard_map/pallas_call | solution.py:246
  74.4 3.5 %shard_map.99 = (f32[32,256]{1,0:T(8,128)}, f32[2048,256]{1,0:T(8,128)}) custom-call(f32[64,1280]{1,0:T(8,128)S(1)} %pad_maximum_fusion.own_ref, f32[64,1280]{1,0:T(8,128)S(1)} %collective-permute-done.15.other_ref, bf16[256,256]{1,0:T(8,128)(2,1)S(1)} %get-tuple-element.44.ch, ...), custom_call_target="tpu_custom_call", output_to_operand_aliasing={{0}: (8, {}), {1}: (9, {})} | custom-call | flops 2415919104 | bytes 7340032 | tf_op jit(solution)/shard_map/pallas_call | solution.py:246
  (59 shorter events, 0.8 us)
Async XLA Ops:
  0.6 20.6 %collective-permute-start.3 = (f32[1024,512]{1,0:T(8,128)}, f32[1024,512]{1,0:T(8,128)S(1)}, u32[]{:S(2)}, u32[]{:S(2)}) collective-permute-start(f32[1024,512]{1,0:T(8,128)} %v_ref.1), channel_id=1, source_target_pairs={{0,1},{1,0},{2,3},{3,2},{4,5},{5,4},{6,7},{7,6},{8,9},{9,8},{10,11... | collective-permute-start | bytes 6291464 | tf_op jit(solution)/shard_map/ppermute | solution.py:16
  1.2 1.6 %copy-start.2 = (f32[1024,512]{1,0:T(8,128)S(1)}, f32[1024,512]{1,0:T(8,128)}, u32[]{:S(2)}) copy-start(f32[1024,512]{1,0:T(8,128)} %v_ref.1) | copy-start | bytes 6291460
  2.8 5.7 %copy-start.3 = (f32[1024,32]{0,1:T(8,128)S(1)}, f32[1024,32]{0,1:T(8,128)}, u32[]{:S(2)}) copy-start(f32[1024,32]{0,1:T(8,128)} %param.8) | copy-start | bytes 393220
  3.2 9.1 %collective-permute-start.9 = (f32[64,512]{1,0:T(8,128)S(1)}, f32[64,512]{1,0:T(8,128)S(1)}, u32[]{:S(2)}, u32[]{:S(2)}) collective-permute-start(f32[64,512]{1,0:T(8,128)S(1)} %get-tuple-element.35.refs_0_), channel_id=1, source_target_pairs={{0,24},{8,16},{16,8},{24,0},{1,25},{9,17},{17,9},{25,1},{2,26},{10... | collective-permute-start | bytes 393224 | tf_op jit(solution)/shard_map/ppermute | solution.py:16
  7.8 11.7 %collective-permute-start.8 = (f32[64,512]{1,0:T(8,128)S(1)}, f32[64,512]{1,0:T(8,128)S(1)}, u32[]{:S(2)}, u32[]{:S(2)}) collective-permute-start(f32[64,512]{1,0:T(8,128)S(1)} %get-tuple-element.35.refs_0_), channel_id=1, source_target_pairs={{0,16},{8,24},{16,0},{24,8},{1,17},{9,25},{17,1},{25,9},{2,18},{10... | collective-permute-start | bytes 393224 | tf_op jit(solution)/shard_map/ppermute | solution.py:16
  7.8 13.2 %collective-permute-start.7 = (f32[64,512]{1,0:T(8,128)S(1)}, f32[64,512]{1,0:T(8,128)S(1)}, u32[]{:S(2)}, u32[]{:S(2)}) collective-permute-start(f32[64,512]{1,0:T(8,128)S(1)} %get-tuple-element.35.refs_0_), channel_id=1, source_target_pairs={{0,8},{8,0},{16,24},{24,16},{1,9},{9,1},{17,25},{25,17},{2,10},{10... | collective-permute-start | bytes 393224 | tf_op jit(solution)/shard_map/ppermute | solution.py:16
  8.5 13.1 %collective-permute-start.2 = (f32[32,1024]{1,0:T(8,128)S(1)}, f32[32,1024]{1,0:T(8,128)S(1)}, u32[]{:S(2)}, u32[]{:S(2)}) collective-permute-start(f32[32,1024]{1,0:T(8,128)S(1)} %bitcast.37), channel_id=1, source_target_pairs={{0,6},{1,7},{2,4},{3,5},{4,2},{5,3},{6,0},{7,1},{8,14},{9,15},{10,... | collective-permute-start | bytes 393224 | tf_op jit(solution)/shard_map/ppermute | solution.py:16
  12.3 9.3 %collective-permute-start.1 = (f32[32,1024]{1,0:T(8,128)S(1)}, f32[32,1024]{1,0:T(8,128)S(1)}, u32[]{:S(2)}, u32[]{:S(2)}) collective-permute-start(f32[32,1024]{1,0:T(8,128)S(1)} %bitcast.38), channel_id=1, source_target_pairs={{0,4},{1,5},{2,6},{3,7},{4,0},{5,1},{6,2},{7,3},{8,12},{9,13},{10,... | collective-permute-start | bytes 393224 | tf_op jit(solution)/shard_map/ppermute | solution.py:16
  19.6 5.0 %collective-permute-start = (f32[32,1024]{1,0:T(8,128)S(1)}, f32[32,1024]{1,0:T(8,128)S(1)}, u32[]{:S(2)}, u32[]{:S(2)}) collective-permute-start(f32[32,1024]{1,0:T(8,128)S(1)} %bitcast.39), channel_id=1, source_target_pairs={{0,2},{1,3},{2,0},{3,1},{4,6},{5,7},{6,4},{7,5},{8,10},{9,11},{10,... | collective-permute-start | bytes 393224 | tf_op jit(solution)/shard_map/ppermute | solution.py:16
  21.1 23.7 %collective-permute-start.10 = (f32[256,512]{1,0:T(8,128)S(1)}, f32[256,512]{1,0:T(8,128)S(1)}, u32[]{:S(2)}, u32[]{:S(2)}) collective-permute-start(f32[256,512]{1,0:T(8,128)S(1)} %shard_map.89.v_ref), channel_id=1, source_target_pairs={{0,1},{1,0},{2,3},{3,2},{4,5},{5,4},{6,7},{7,6},{8,9},{9,8},{10,11... | collective-permute-start | bytes 1572872 | tf_op jit(solution)/shard_map/ppermute | solution.py:16
  25.4 2.9 %copy-start.6 = (s32[88,1]{0,1:T(1,128)S(1)}, s32[88,1]{0,1:T(1,128)}, u32[]{:S(2)}) copy-start(s32[88,1]{0,1:T(1,128)} %param.9) | copy-start | bytes 1060
  25.4 8.3 %copy-start.5 = (f32[1,32,256]{2,1,0:T(8,128)S(1)}, f32[1,32,256]{2,1,0:T(8,128)}, u32[]{:S(2)}) copy-start(f32[1,32,256]{2,1,0:T(8,128)} %param.10) | copy-start | bytes 98308
  26.2 5.7 %collective-permute-start.19 = (f32[64,512]{1,0:T(8,128)S(1)}, f32[64,512]{1,0:T(8,128)S(1)}, u32[]{:S(2)}, u32[]{:S(2)}) collective-permute-start(f32[64,512]{1,0:T(8,128)S(1)} %get-tuple-element.49), channel_id=1, source_target_pairs={{0,8},{8,0},{16,24},{24,16},{1,9},{9,1},{17,25},{25,17},{2,10},{10... | collective-permute-start | bytes 393224 | tf_op jit(solution)/shard_map/ppermute | solution.py:16
  26.3 7.8 %collective-permute-start.4 = (f32[64,512]{1,0:T(8,128)S(1)}, f32[64,512]{1,0:T(8,128)S(1)}, u32[]{:S(2)}, u32[]{:S(2)}) collective-permute-start(f32[64,512]{1,0:T(8,128)S(1)} %get-tuple-element.34), channel_id=1, source_target_pairs={{0,8},{8,0},{16,24},{24,16},{1,9},{9,1},{17,25},{25,17},{2,10},{10... | collective-permute-start | bytes 393224 | tf_op jit(solution)/shard_map/ppermute | solution.py:16
  31.9 11.1 %collective-permute-start.20 = (f32[64,512]{1,0:T(8,128)S(1)}, f32[64,512]{1,0:T(8,128)S(1)}, u32[]{:S(2)}, u32[]{:S(2)}) collective-permute-start(f32[64,512]{1,0:T(8,128)S(1)} %add.46), channel_id=1, source_target_pairs={{0,16},{8,24},{16,0},{24,8},{1,17},{9,25},{17,1},{25,9},{2,18},{10... | collective-permute-start | bytes 393224 | tf_op jit(solution)/shard_map/ppermute | solution.py:16
  33.7 9.5 %collective-permute-start.16 = (f32[1,40,256]{2,1,0:T(8,128)S(1)}, f32[1,40,256]{2,1,0:T(8,128)S(1)}, u32[]{:S(2)}, u32[]{:S(2)}) collective-permute-start(f32[1,40,256]{2,1,0:T(8,128)S(1)} %get-tuple-element.62), channel_id=1, source_target_pairs={{0,1},{1,0},{2,3},{3,2},{4,5},{5,4},{6,7},{7,6},{8,9},{9,8},{10,11... | collective-permute-start | bytes 122888 | tf_op jit(solution)/shard_map/ppermute | solution.py:16
  34.1 10.8 %collective-permute-start.5 = (f32[64,512]{1,0:T(8,128)S(1)}, f32[64,512]{1,0:T(8,128)S(1)}, u32[]{:S(2)}, u32[]{:S(2)}) collective-permute-start(f32[64,512]{1,0:T(8,128)S(1)} %add.40), channel_id=1, source_target_pairs={{0,16},{8,24},{16,0},{24,8},{1,17},{9,25},{17,1},{25,9},{2,18},{10... | collective-permute-start | bytes 393224 | tf_op jit(solution)/shard_map/ppermute | solution.py:16
  43.0 6.1 %collective-permute-start.21 = (f32[64,512]{1,0:T(8,128)S(1)}, f32[64,512]{1,0:T(8,128)S(1)}, u32[]{:S(2)}, u32[]{:S(2)}) collective-permute-start(f32[64,512]{1,0:T(8,128)S(1)} %add.47.refs_0_), channel_id=1, source_target_pairs={{0,8},{8,0},{16,24},{24,16},{1,9},{9,1},{17,25},{25,17},{2,10},{10... | collective-permute-start | bytes 393224 | tf_op jit(solution)/shard_map/ppermute | solution.py:16
  43.2 10.5 %collective-permute-start.17 = (f32[2,40,256]{2,1,0:T(8,128)S(1)}, f32[2,40,256]{2,1,0:T(8,128)S(1)}, u32[]{:S(2)}, u32[]{:S(2)}) collective-permute-start(f32[2,40,256]{2,1,0:T(8,128)S(1)} %pad_maximum_fusion.3), channel_id=1, source_target_pairs={{0,2},{1,3},{2,0},{3,1},{4,6},{5,7},{6,4},{7,5},{8,10},{9,11},{10,... | collective-permute-start | bytes 245768 | tf_op jit(solution)/shard_map/ppermute | solution.py:16
  45.0 9.3 %collective-permute-start.6 = (f32[64,512]{1,0:T(8,128)S(1)}, f32[64,512]{1,0:T(8,128)S(1)}, u32[]{:S(2)}, u32[]{:S(2)}) collective-permute-start(f32[64,512]{1,0:T(8,128)S(1)} %add.41.refs_0_), channel_id=1, source_target_pairs={{0,8},{8,0},{16,24},{24,16},{1,9},{9,1},{17,25},{25,17},{2,10},{10... | collective-permute-start | bytes 393224 | tf_op jit(solution)/shard_map/ppermute | solution.py:16
  50.7 7.4 %collective-permute-start.22 = (f32[64,640]{1,0:T(8,128)S(1)}, f32[64,640]{1,0:T(8,128)S(1)}, u32[]{:S(2)}, u32[]{:S(2)}) collective-permute-start(f32[64,640]{1,0:T(8,128)S(1)} %get-tuple-element.50), channel_id=1, source_target_pairs={{0,2},{1,3},{2,0},{3,1},{4,6},{5,7},{6,4},{7,5},{8,10},{9,11},{10,... | collective-permute-start | bytes 491528 | tf_op jit(solution)/shard_map/ppermute | solution.py:16
  52.2 7.1 %collective-permute-start.24 = (f32[64,640]{1,0:T(8,128)S(1)}, f32[64,640]{1,0:T(8,128)S(1)}, u32[]{:S(2)}, u32[]{:S(2)}) collective-permute-start(f32[64,640]{1,0:T(8,128)S(1)} %get-tuple-element.51), channel_id=1, source_target_pairs={{0,4},{1,5},{2,6},{3,7},{4,0},{5,1},{6,2},{7,3},{8,12},{9,13},{10,... | collective-permute-start | bytes 491528 | tf_op jit(solution)/shard_map/ppermute | solution.py:16
  53.8 16.6 %collective-permute-start.18 = (f32[4,40,256]{2,1,0:T(8,128)S(1)}, f32[4,40,256]{2,1,0:T(8,128)S(1)}, u32[]{:S(2)}, u32[]{:S(2)}) collective-permute-start(f32[4,40,256]{2,1,0:T(8,128)S(1)} %pad_maximum_fusion.2), channel_id=1, source_target_pairs={{0,4},{1,5},{2,6},{3,7},{4,0},{5,1},{6,2},{7,3},{8,12},{9,13},{10,... | collective-permute-start | bytes 491528 | tf_op jit(solution)/shard_map/ppermute | solution.py:16
  55.9 7.1 %collective-permute-start.11 = (f32[64,640]{1,0:T(8,128)S(1)}, f32[64,640]{1,0:T(8,128)S(1)}, u32[]{:S(2)}, u32[]{:S(2)}) collective-permute-start(f32[64,640]{1,0:T(8,128)S(1)} %get-tuple-element.40), channel_id=1, source_target_pairs={{0,2},{1,3},{2,0},{3,1},{4,6},{5,7},{6,4},{7,5},{8,10},{9,11},{10,... | collective-permute-start | bytes 491528 | tf_op jit(solution)/shard_map/ppermute | solution.py:16
  56.5 8.3 %collective-permute-start.13 = (f32[64,640]{1,0:T(8,128)S(1)}, f32[64,640]{1,0:T(8,128)S(1)}, u32[]{:S(2)}, u32[]{:S(2)}) collective-permute-start(f32[64,640]{1,0:T(8,128)S(1)} %get-tuple-element.41), channel_id=1, source_target_pairs={{0,4},{1,5},{2,6},{3,7},{4,0},{5,1},{6,2},{7,3},{8,12},{9,13},{10,... | collective-permute-start | bytes 491528 | tf_op jit(solution)/shard_map/ppermute | solution.py:16
  58.1 8.5 %collective-permute-start.23 = (f32[64,640]{1,0:T(8,128)S(1)}, f32[64,640]{1,0:T(8,128)S(1)}, u32[]{:S(2)}, u32[]{:S(2)}) collective-permute-start(f32[64,640]{1,0:T(8,128)S(1)} %add.48), channel_id=1, source_target_pairs={{0,4},{1,5},{2,6},{3,7},{4,0},{5,1},{6,2},{7,3},{8,12},{9,13},{10,... | collective-permute-start | bytes 491528 | tf_op jit(solution)/shard_map/ppermute | solution.py:16
  59.3 11.6 %copy-start.1 = (f32[1,1,2048,256]{3,2,1,0:T(8,128)S(1)}, f32[1,1,2048,256]{3,2,1,0:T(8,128)}, u32[]{:S(2)}) copy-start(f32[1,1,2048,256]{3,2,1,0:T(8,128)} %param.12) | copy-start | bytes 6291460
  59.3 7.3 %collective-permute-start.25 = (f32[64,640]{1,0:T(8,128)S(1)}, f32[64,640]{1,0:T(8,128)S(1)}, u32[]{:S(2)}, u32[]{:S(2)}) collective-permute-start(f32[64,640]{1,0:T(8,128)S(1)} %add.50), channel_id=1, source_target_pairs={{0,2},{1,3},{2,0},{3,1},{4,6},{5,7},{6,4},{7,5},{8,10},{9,11},{10,... | collective-permute-start | bytes 491528 | tf_op jit(solution)/shard_map/ppermute | solution.py:16
  63.1 5.4 %collective-permute-start.12 = (f32[64,640]{1,0:T(8,128)S(1)}, f32[64,640]{1,0:T(8,128)S(1)}, u32[]{:S(2)}, u32[]{:S(2)}) collective-permute-start(f32[64,640]{1,0:T(8,128)S(1)} %add.42), channel_id=1, source_target_pairs={{0,4},{1,5},{2,6},{3,7},{4,0},{5,1},{6,2},{7,3},{8,12},{9,13},{10,... | collective-permute-start | bytes 491528 | tf_op jit(solution)/shard_map/ppermute | solution.py:16
  64.8 5.4 %collective-permute-start.14 = (f32[64,640]{1,0:T(8,128)S(1)}, f32[64,640]{1,0:T(8,128)S(1)}, u32[]{:S(2)}, u32[]{:S(2)}) collective-permute-start(f32[64,640]{1,0:T(8,128)S(1)} %add.44), channel_id=1, source_target_pairs={{0,2},{1,3},{2,0},{3,1},{4,6},{5,7},{6,4},{7,5},{8,10},{9,11},{10,... | collective-permute-start | bytes 491528 | tf_op jit(solution)/shard_map/ppermute | solution.py:16
  66.6 4.3 %copy-start = (f32[1,1,2048,512]{3,2,1,0:T(8,128)S(1)}, f32[1,1,2048,512]{3,2,1,0:T(8,128)}, u32[]{:S(2)}) copy-start(f32[1,1,2048,512]{3,2,1,0:T(8,128)} %param.13) | copy-start | bytes 12582916
  66.6 3.9 %copy-start.4 = (s32[1,1,512]{2,1,0:T(1,128)S(1)}, s32[1,1,512]{2,1,0:T(1,128)}, u32[]{:S(2)}) copy-start(s32[1,1,512]{2,1,0:T(1,128)} %param.11) | copy-start | bytes 6148
  66.7 4.2 %collective-permute-start.26 = (f32[64,1280]{1,0:T(8,128)S(1)}, f32[64,1280]{1,0:T(8,128)S(1)}, u32[]{:S(2)}, u32[]{:S(2)}) collective-permute-start(f32[64,1280]{1,0:T(8,128)S(1)} %pad_maximum_fusion.1.own_ref), channel_id=1, source_target_pairs={{0,1},{1,0},{2,3},{3,2},{4,5},{5,4},{6,7},{7,6},{8,9},{9,8},{10,11... | collective-permute-start | bytes 983048 | tf_op jit(solution)/shard_map/ppermute | solution.py:16
  70.3 4.1 %collective-permute-start.15 = (f32[64,1280]{1,0:T(8,128)S(1)}, f32[64,1280]{1,0:T(8,128)S(1)}, u32[]{:S(2)}, u32[]{:S(2)}) collective-permute-start(f32[64,1280]{1,0:T(8,128)S(1)} %pad_maximum_fusion.own_ref), channel_id=1, source_target_pairs={{0,1},{1,0},{2,3},{3,2},{4,5},{5,4},{6,7},{7,6},{8,9},{9,8},{10,11... | collective-permute-start | bytes 983048 | tf_op jit(solution)/shard_map/ppermute | solution.py:16
